TPU v7x, 128 devices: a whole 4x4x4 slice. The times are simulated.
128 devices in a mesh: row: 8 (over x, core), col: 16 (over y, z).
Axes of the slice: x: 4, y: 4, z: 4, core: 2. Of those that a mesh axis runs over, the one named last changes fastest.
Arguments:
- imu: bfloat16 [32768, 128], P(('row', 'col')), may hold values from -30 to 30
- camera: bfloat16 [16, 2048, 128], P('col', 'row'), may hold values from -30 to 30
- imu_mass: float32 [32768], P('row'), may hold values from 0.3 to 3
- cam_mass: float32 [32768], P('col'), may hold values from 0.3 to 3
Outputs:
- grad_imu: float32 [32768, 128], P(('row', 'col'))
- grad_camera: float32 [16, 2048, 128], P('col', 'row')
All inputs are finite; a program needn't handle non-finite values.
Results may differ from a plain program's by a relative error of at most 0.0028.
Values may be sent and summed in bfloat16 or wider, within the bound.
A program may use at most 128 MiB of HBM per device.

v0:
```python
import math

import jax
import jax.numpy as jnp
from jax import lax
from jax.sharding import PartitionSpec as P

D = 128
ITERS = 3


def cost_block(rows, rows_sq, cols, cols_sq):
    cross = jnp.dot(rows, cols.T, preferred_element_type=jnp.float32)
    return rows_sq[:, None] + cols_sq[None, :] - 2.0 * cross


def squares(values):
    return jnp.sum(jnp.square(values.astype(jnp.float32)), axis=1)


def local(imu, camera, imu_mass, cam_mass):
    epsilon = D / 20.0
    imu_rows = lax.all_gather(imu, "col", axis=0, tiled=True)
    cam_rows = lax.all_gather(camera, "row", axis=1, tiled=True)[0]
    rows = imu_rows.shape[0]
    cols = cam_rows.shape[0]
    block = math.gcd(rows, 512)
    count = rows // block
    rows_sq = squares(imu_rows)
    cols_sq = squares(cam_rows)
    log_a = jnp.log(imu_mass)
    log_b = jnp.log(cam_mass)
    stored = cost_block(imu_rows, rows_sq, cam_rows, cols_sq)

    def tile(k):
        return lax.dynamic_slice_in_dim(stored, k * block, block, 0)

    blocks = jnp.arange(count, dtype=jnp.int32)

    def row_lse(g):

        def single(k):
            scores = (g[None, :] - tile(k)) / epsilon
            peak = jnp.max(scores, axis=1)
            return (peak, jnp.sum(jnp.exp(scores - peak[:, None]), axis=1))

        peak, total = lax.map(single, blocks)
        peak = peak.reshape(rows)
        total = total.reshape(rows)
        top = lax.pmax(peak, "col")
        total = lax.psum(total * jnp.exp(peak - top), "col")
        peak = top
        return peak + jnp.log(total)

    def col_lse(f):

        def advance(k, carry):
            peak, total = carry
            f_blk = lax.dynamic_slice_in_dim(f, k * block, block, 0)
            scores = (f_blk[:, None] - tile(k)) / epsilon
            new_peak = jnp.maximum(peak, jnp.max(scores, axis=0))
            total = total * jnp.exp(peak - new_peak) + jnp.sum(
                jnp.exp(scores - new_peak[None, :]), axis=0
            )
            return (new_peak, total)

        start = (jnp.full((cols,), -1e30, jnp.float32), jnp.zeros((cols,), jnp.float32))
        peak, total = lax.fori_loop(0, count, advance, start)
        top = lax.pmax(peak, "row")
        total = lax.psum(total * jnp.exp(peak - top), "row")
        peak = top
        return peak + jnp.log(total)

    g = jnp.zeros((cols,), jnp.float32)
    f = jnp.zeros((rows,), jnp.float32)
    for step in range(ITERS):
        f = epsilon * log_a - epsilon * row_lse(g)
        g = epsilon * log_b - epsilon * col_lse(f)

    def plan_rows(k):
        f_blk = lax.dynamic_slice_in_dim(f, k * block, block, 0)
        return jnp.exp((f_blk[:, None] + g[None, :] - tile(k)) / epsilon).astype(jnp.bfloat16)

    plan = lax.map(plan_rows, blocks).reshape(rows, cols)
    row_total = jnp.sum(plan, axis=1, dtype=jnp.float32)
    col_total = jnp.sum(plan, axis=0, dtype=jnp.float32)
    imu_share = rows // lax.axis_size("col")
    cam_share = cols // lax.axis_size("row")
    plan_part = plan
    own = imu_rows.astype(jnp.float32)
    weight = row_total
    pulled = jnp.dot(plan_part, cam_rows, preferred_element_type=jnp.float32)
    whole_imu = lax.psum(2.0 * (weight[:, None] * own - pulled), "col")
    grad_imu = lax.dynamic_slice_in_dim(whole_imu, lax.axis_index("col") * imu_share, imu_share, 0)
    plan_part = plan
    own = cam_rows.astype(jnp.float32)
    weight = col_total
    pulled = lax.dot_general(
        plan_part, imu_rows, (((0,), (0,)), ((), ())), preferred_element_type=jnp.float32
    )
    whole_cam = lax.psum(2.0 * (weight[:, None] * own - pulled), "row")
    grad_cam = lax.dynamic_slice_in_dim(whole_cam, lax.axis_index("row") * cam_share, cam_share, 0)
    return (grad_imu, grad_cam[None])


def solution(mesh):
    in_specs = (P(("row", "col"), None), P("col", "row", None), P("row"), P("col"))
    out_specs = (P(("row", "col"), None), P("col", "row", None))
    return jax.shard_map(local, mesh=mesh, in_specs=in_specs, out_specs=out_specs, check_vma=False)
```

profile of v0, /device:TPU:116, one launch (start us, length us, event | category | flops | bytes accessed | tf_op | source)
XLA Modules:
  0.0 1096.9 jit_solution(795377166092080157)
XLA Ops:
  8.0 12.1 %all_gather.7 = bf16[1,2048,128]{2,1,0:T(8,128)(2,1)S(1)} all-gather(bf16[1,256,128]{2,1,0:T(8,128)(2,1)} %param.19), channel_id=1, replica_groups=mesh['row'=8,'col'=16] {'row'}, dimensions={1}, use_global_device_ids=true | all-gather | bytes 589824 | tf_op jit(solution)/shard_map/all_gather | solution.py:24
  20.5 31.6 %all-gather.2.cloned.1.call-done = bf16[4096,128]{1,0:T(8,128)(2,1)} async-done(((bf16[256,128]{1,0:T(8,128)(2,1)}), bf16[4096,128]{1,0:T(8,128)(2,1)}) %all-gather.2.cloned.1.call-update) | async-done | bytes 1048592 | tf_op jit(solution)/shard_map/all_gather | solution.py:23
  53.9 14.3 %multiply_subtract_fusion = f32[4096,2048]{1,0:T(8,128)} fusion(f32[2048]{0:T(1024)S(1)} %fusion.14, f32[4096]{0:T(1024)S(1)} %fusion.13, bf16[4096,128]{1,0:T(8,128)(2,1)} %all-gather.2.cloned.1.call-done, bf16[1,2048,128]{2,1,0:T(8,128)(2,1)S(1)} %all_gather.7), kind=kOutput, calls=%fused_computation.32 | convolution fusion | flops 2172649472 | bytes 35151872 | tf_op jit(solution)/shard_map/dot_general | solution.py:13
  68.2 56.4 %while.94 = (s32[]{:T(128)}, f32[8,512]{1,0:T(8,128)S(1)}, f32[8,512]{1,0:T(8,128)S(1)}, s32[8]{0:T(128)S(1)}, f32[4096,2048]{1,0:T(8,128)}, /*index=5*/s32[]{:T(128)}, s32[1]{0:T(128)}, s32[]{:T(128)}, s32[]{:T(128)}) while((s32[]{:T(128)}, f32[8,512]{1,0:T(8,128)S(1)}, f32[8,512]{1,0:T(8,128)S(1)}, s32[8]{0:T(128)S(1)}, ...), condition=%wide.region_5.6_spmd, body=%wide.region_2.5_spmd.sunk | while | flops 7339014 | bytes 8403111 | solution.py:47
  124.7 63.4 %pmax.42 = f32[4096]{0:T(1024)S(1)} all-reduce(f32[4096]{0:T(1024)S(1)} %bitcast.72), channel_id=1, replica_groups=mesh['row'=8,'col'=16] {'col'}, use_global_device_ids=true, to_apply=%region_6.7 | all-reduce | flops 4096 | bytes 32768 | tf_op jit(solution)/shard_map/pmax | solution.py:50
  188.1 69.5 %psum.56 = f32[4096]{0:T(1024)S(1)} all-reduce(f32[4096]{0:T(1024)S(1)} %exponential_multiply_fusion.2), channel_id=1, replica_groups=mesh['row'=8,'col'=16] {'col'}, use_global_device_ids=true, to_apply=%region_7.8 | all-reduce | flops 4096 | bytes 32768 | tf_op jit(solution)/shard_map/psum | solution.py:51
  257.6 47.5 %while.98 = (s32[]{:T(128)}, f32[2048]{0:T(1024)S(1)}, f32[2048]{0:T(1024)S(1)}, f32[4096]{0:T(1024)S(1)}, f32[4096,2048]{1,0:T(8,128)}, /*index=5*/s32[]{:T(128)}, s32[]{:T(128)}, s32[]{:T(128)}, s32[]{:T(128)}) while((s32[]{:T(128)}, f32[2048]{0:T(1024)S(1)}, f32[2048]{0:T(1024)S(1)}, f32[4096]{0:T(1024)S(1)}, ...), condition=%wide.region_11.12_spmd.clone, body=%wide.region_8.11_spmd.clone.sunk | while | flops 7350279 | bytes 8503458 | solution.py:68
  315.7 10.6 psum.57
  326.4 57.8 %while.95 = (s32[]{:T(128)}, f32[8,512]{1,0:T(8,128)S(1)}, f32[8,512]{1,0:T(8,128)S(1)}, f32[2048]{0:T(1024)S(1)}, s32[8]{0:T(128)S(1)}, /*index=5*/f32[4096,204...) while((s32[]{:T(128)}, f32[8,512]{1,0:T(8,128)S(1)}, f32[8,512]{1,0:T(8,128)S(1)}, ...), condition=%wide.region_17.18_spmd, body=%wide.region_14.17_spmd.sunk | while | flops 7339014 | bytes 8419503 | solution.py:47
  384.1 69.5 %pmax.44 = f32[4096]{0:T(1024)S(1)} all-reduce(f32[4096]{0:T(1024)S(1)} %bitcast.74), channel_id=1, replica_groups=mesh['row'=8,'col'=16] {'col'}, use_global_device_ids=true, to_apply=%region_18.19 | all-reduce | flops 4096 | bytes 32768 | tf_op jit(solution)/shard_map/pmax | solution.py:50
  453.7 69.5 %psum.58 = f32[4096]{0:T(1024)S(1)} all-reduce(f32[4096]{0:T(1024)S(1)} %exponential_multiply_fusion.1), channel_id=1, replica_groups=mesh['row'=8,'col'=16] {'col'}, use_global_device_ids=true, to_apply=%region_19.20 | all-reduce | flops 4096 | bytes 32768 | tf_op jit(solution)/shard_map/psum | solution.py:51
  523.2 47.5 %while.99 = (s32[]{:T(128)}, f32[2048]{0:T(1024)S(1)}, f32[2048]{0:T(1024)S(1)}, f32[4096]{0:T(1024)S(1)}, f32[4096,2048]{1,0:T(8,128)}, /*index=5*/s32[]{:T(128)}, s32[]{:T(128)}, s32[]{:T(128)}, s32[]{:T(128)}) while((s32[]{:T(128)}, f32[2048]{0:T(1024)S(1)}, f32[2048]{0:T(1024)S(1)}, f32[4096]{0:T(1024)S(1)}, ...), condition=%wide.region_23.24_spmd.clone, body=%wide.region_20.23_spmd.clone.sunk | while | flops 7350279 | bytes 8503458 | solution.py:68
  570.7 11.1 %pmax.45 = f32[2048]{0:T(1024)S(1)} all-reduce(f32[2048]{0:T(1024)S(1)} %get-tuple-element.419), channel_id=1, replica_groups=mesh['row'=8,'col'=16] {'row'}, use_global_device_ids=true, to_apply=%region_24.25 | all-reduce | flops 2048 | bytes 16384 | tf_op jit(solution)/shard_map/pmax | solution.py:69
  581.8 14.4 %psum.59 = f32[2048]{0:T(1024)S(1)} all-reduce(f32[2048]{0:T(1024)S(1)} %exponential_multiply_fusion.4), channel_id=1, replica_groups=mesh['row'=8,'col'=16] {'row'}, use_global_device_ids=true, to_apply=%region_25.26 | all-reduce | flops 2048 | bytes 16384 | tf_op jit(solution)/shard_map/psum | solution.py:70
  596.3 56.9 %while.96 = (s32[]{:T(128)}, f32[8,512]{1,0:T(8,128)S(1)}, f32[8,512]{1,0:T(8,128)S(1)}, f32[2048]{0:T(1024)S(1)}, s32[8]{0:T(128)S(1)}, /*index=5*/f32[4096,204...) while((s32[]{:T(128)}, f32[8,512]{1,0:T(8,128)S(1)}, f32[8,512]{1,0:T(8,128)S(1)}, ...), condition=%wide.region_29.30_spmd, body=%wide.region_26.29_spmd.sunk | while | flops 7339014 | bytes 8419503 | solution.py:47
  653.2 69.5 %pmax.46 = f32[4096]{0:T(1024)S(1)} all-reduce(f32[4096]{0:T(1024)S(1)} %bitcast.76), channel_id=1, replica_groups=mesh['row'=8,'col'=16] {'col'}, use_global_device_ids=true, to_apply=%region_30.31 | all-reduce | flops 4096 | bytes 32768 | tf_op jit(solution)/shard_map/pmax | solution.py:50
  722.8 69.6 %psum.60 = f32[4096]{0:T(1024)S(1)} all-reduce(f32[4096]{0:T(1024)S(1)} %exponential_multiply_fusion), channel_id=1, replica_groups=mesh['row'=8,'col'=16] {'col'}, use_global_device_ids=true, to_apply=%region_31.32 | all-reduce | flops 4096 | bytes 32768 | tf_op jit(solution)/shard_map/psum | solution.py:51
  792.3 47.5 %while.100 = (s32[]{:T(128)}, f32[2048]{0:T(1024)S(1)}, f32[2048]{0:T(1024)S(1)}, f32[4096]{0:T(1024)S(1)}, f32[4096,2048]{1,0:T(8,128)}, /*index=5*/s32[]{:T(128)}, s32[]{:T(128)}, s32[]{:T(128)}, s32[]{:T(128)}) while((s32[]{:T(128)}, f32[2048]{0:T(1024)S(1)}, f32[2048]{0:T(1024)S(1)}, f32[4096]{0:T(1024)S(1)}, ...), condition=%wide.region_35.36_spmd.clone, body=%wide.region_32.35_spmd.clone.sunk | while | flops 7350279 | bytes 8503458 | solution.py:68
  839.8 11.0 %pmax.47 = f32[2048]{0:T(1024)S(1)} all-reduce(f32[2048]{0:T(1024)S(1)} %get-tuple-element.423), channel_id=1, replica_groups=mesh['row'=8,'col'=16] {'row'}, use_global_device_ids=true, to_apply=%region_36.37 | all-reduce | flops 2048 | bytes 16384 | tf_op jit(solution)/shard_map/pmax | solution.py:69
  850.9 14.3 %psum.61 = f32[2048]{0:T(1024)S(1)} all-reduce(f32[2048]{0:T(1024)S(1)} %exponential_multiply_fusion.3), channel_id=1, replica_groups=mesh['row'=8,'col'=16] {'row'}, use_global_device_ids=true, to_apply=%region_37.38 | all-reduce | flops 2048 | bytes 16384 | tf_op jit(solution)/shard_map/psum | solution.py:70
  865.2 45.2 %while.97 = (s32[]{:T(128)}, bf16[8,512,2048]{2,1,0:T(8,128)(2,1)}, s32[8]{0:T(128)S(1)}, f32[4096]{0:T(1024)S(1)}, f32[2048]{0:T(1024)S(1)}, /*index=5*/f32[409...) while((s32[]{:T(128)}, bf16[8,512,2048]{2,1,0:T(8,128)(2,1)}, s32[8]{0:T(128)S(1)}, ...), condition=%wide.region_39.40_spmd, body=%wide.region_38.39_spmd.sunk | while | flops 4194310 | bytes 6306471 | solution.py:84
  927.1 11.7 %fusion.11 = f32[4096,128]{1,0:T(8,128)} fusion(bf16[4096,2048]{1,0:T(8,128)(2,1)} %bitcast.64, bf16[4096,128]{1,0:T(8,128)(2,1)S(1)} %copy-done.1, f32[4096]{0:T(1024)S(1)} %bitcast.88, bf16[1,2048,128]{2,1,0:T(8,128)(2,1)S(1)} %all_gather.7), kind=kOutput, calls=%fused_computation.34 | convolution fusion | flops 2149580800 | bytes 20463616 | tf_op jit(solution)/shard_map/dot_general | solution.py:92
  938.9 54.8 %all-reduce.5.cloned.1.call-done = f32[2048,128]{1,0:T(8,128)} async-done(((f32[2048,128]{1,0:T(8,128)}), f32[2048,128]{1,0:T(8,128)}) %all-reduce.5.cloned.1.call-update) | async-done | bytes 1048592 | tf_op jit(solution)/shard_map/psum | solution.py:101
  995.2 93.5 %all-reduce.3.cloned.1.call-done = f32[4096,128]{1,0:T(8,128)} async-done(((f32[4096,128]{1,0:T(8,128)}), f32[4096,128]{1,0:T(8,128)}) %all-reduce.3.cloned.1.call-update) | async-done | bytes 2097168 | tf_op jit(solution)/shard_map/psum | solution.py:93
  (345 shorter events, 370.4 us)
Async XLA Ops:
  7.2 44.9 %all-gather.2.cloned.1.call-start = ((), (), s32[]{:S(2)}) async-start(), calls=%async_computation | async-start | bytes 1114112 | tf_op jit(solution)/shard_map/all_gather | solution.py:23
  7.9 985.8 %all-reduce.5.cloned.1.call-start = ((), (), s32[]{:S(2)}) async-start(), calls=%async_computation.2 | async-start | bytes 2097152 | tf_op jit(solution)/shard_map/psum | solution.py:101
  68.2 189.4 %copy-start.2 = (f32[4096]{0:T(1024)S(1)}, f32[4096]{0:T(1024)}, u32[]{:S(2)}) copy-start(f32[4096]{0:T(1024)} %param.20) | copy-start | bytes 49156
  257.6 68.7 %copy-start.3 = (f32[2048]{0:T(1024)S(1)}, f32[2048]{0:T(1024)}, u32[]{:S(2)}) copy-start(f32[2048]{0:T(1024)} %param.21) | copy-start | bytes 24580
  865.1 53.7 %copy-start.1 = (bf16[4096,128]{1,0:T(8,128)(2,1)S(1)}, bf16[4096,128]{1,0:T(8,128)(2,1)}, u32[]{:S(2)}) copy-start(bf16[4096,128]{1,0:T(8,128)(2,1)} %all-gather.2.cloned.1.call-done) | copy-start | bytes 3145732
  910.3 10.7 copy-start
  926.9 161.9 %all-reduce.3.cloned.1.call-start = ((), (), s32[]{:S(2)}) async-start(), calls=%async_computation.1 | async-start | bytes 4194304 | tf_op jit(solution)/shard_map/psum | solution.py:93
Sparse Core Ops, SparseCore 0:
  10.1 41.8 all-gather.1
  927.0 66.6 all-reduce.4
  997.0 91.7 all-reduce.2
where the time goes:
time: 1100 us
  blocking collectives  495 us (45%)
  other arithmetic  324 us (29%)
  waiting for transfers between devices  181 us (16%)
  matrix products  31.8 us (3%)
  local copies, waits for them, and re-layouts  29.3 us (3%)
  loops' own time  21.8 us (2%)
  between operations  14.1 us (1%)
    psum x3, blocking collectives, row_lse(): total = lax.psum(total * jnp.exp(peak - top), 'col')  209 us
    pmax x3, blocking collectives, row_lse(): top = lax.pmax(peak, 'col')  202 us
    psum x1, waiting for transfers between devices, local(): whole_imu = lax.psum(2.0 * (weight[:, None] * own - pulled), 'col')  93.5 us
    reduce_sum x24, other arithmetic, single(): return (peak, jnp.sum(jnp.exp(scores - peak[:, None]), axis=1))  75 us
    reduce_sum x24, other arithmetic, advance(): jnp.sum(jnp.exp(scores - new_peak[None, :]), axis=0)  74.4 us
    reduce_max x24, other arithmetic, single(): peak = jnp.max(scores, axis=1)  64.4 us
    reduce_max x24, other arithmetic, advance(): new_peak = jnp.maximum(peak, jnp.max(scores, axis=0))  64.1 us
    psum x1, waiting for transfers between devices, local(): whole_cam = lax.psum(2.0 * (weight[:, None] * own - pulled), 'row')  54.8 us
  transfers between devices with their start and end apart: 3, of which 3 were waited for; matrix products, arithmetic and copies ran while one was open for 1% of the time, Pallas kernels for 0%

commit v1 on v0

--- a/solution.py
+++ b/solution.py
@@ -16,6 +16,12 @@
 
 def squares(values):
     return jnp.sum(jnp.square(values.astype(jnp.float32)), axis=1)
+
+
+def combine(part, axis):
+    parts = lax.all_gather(part, axis, axis=0)
+    top = jnp.max(parts, axis=0)
+    return top + jnp.log(jnp.sum(jnp.exp(parts - top[None, :]), axis=0))
 
 
 def local(imu, camera, imu_mass, cam_mass):
@@ -47,10 +53,7 @@
         peak, total = lax.map(single, blocks)
         peak = peak.reshape(rows)
         total = total.reshape(rows)
-        top = lax.pmax(peak, "col")
-        total = lax.psum(total * jnp.exp(peak - top), "col")
-        peak = top
-        return peak + jnp.log(total)
+        return combine(peak + jnp.log(total), "col")
 
     def col_lse(f):
 
@@ -66,10 +69,7 @@
 
         start = (jnp.full((cols,), -1e30, jnp.float32), jnp.zeros((cols,), jnp.float32))
         peak, total = lax.fori_loop(0, count, advance, start)
-        top = lax.pmax(peak, "row")
-        total = lax.psum(total * jnp.exp(peak - top), "row")
-        peak = top
-        return peak + jnp.log(total)
+        return combine(peak + jnp.log(total), "row")
 
     g = jnp.zeros((cols,), jnp.float32)
     f = jnp.zeros((rows,), jnp.float32)
@@ -90,16 +90,14 @@
     own = imu_rows.astype(jnp.float32)
     weight = row_total
     pulled = jnp.dot(plan_part, cam_rows, preferred_element_type=jnp.float32)
-    whole_imu = lax.psum(2.0 * (weight[:, None] * own - pulled), "col")
-    grad_imu = lax.dynamic_slice_in_dim(whole_imu, lax.axis_index("col") * imu_share, imu_share, 0)
+    grad_imu = lax.psum_scatter(2.0 * (weight[:, None] * own - pulled), "col", scatter_dimension=0, tiled=True)
     plan_part = plan
     own = cam_rows.astype(jnp.float32)
     weight = col_total
     pulled = lax.dot_general(
         plan_part, imu_rows, (((0,), (0,)), ((), ())), preferred_element_type=jnp.float32
     )
-    whole_cam = lax.psum(2.0 * (weight[:, None] * own - pulled), "row")
-    grad_cam = lax.dynamic_slice_in_dim(whole_cam, lax.axis_index("row") * cam_share, cam_share, 0)
+    grad_cam = lax.psum_scatter(2.0 * (weight[:, None] * own - pulled), "row", scatter_dimension=0, tiled=True)
     return (grad_imu, grad_cam[None])
 
 

time: 1100 us -> 673 us (0.61)
  blocking collectives: 495 us -> 117 us
  waiting for transfers between devices: 181 us -> 130 us
    psum x6 -> x0, blocking collectives: 248 us -> none  [the longest x3 209 us: row_lse(): total = lax.psum(total * jnp.exp(peak - top), 'col')]
    pmax x6 -> x0, blocking collectives: 235 us -> none  [the longest x3 202 us: row_lse(): top = lax.pmax(peak, 'col')]
    psum x2 -> x0, waiting for transfers between devices: 148 us -> none  [the longest x1 93.5 us: local(): whole_imu = lax.psum(2.0 * (weight[:, None] * own - pulled), 'col')]
    all_gather x0 -> x6, blocking collectives: none -> 104 us  [combine(): parts = lax.all_gather(part, axis, axis=0)]
    reduce_scatter x0 -> x2, waiting for transfers between devices: none -> 97.4 us  [the longest x1 80.2 us: local(): lax.psum_scatter(2.0 * (weight[:, None] * own - pulled), 'col', scatter_d...]
  transfers between devices with their start and end apart: 3 -> 3, of which waited for: 3 -> 3; matrix products, arithmetic and copies ran while one was open for 1% -> 2% of each run, Pallas kernels for 0% -> 0%
where the time goes in v1:
time: 673 us; the launch traced here: 665 us
  other arithmetic  325 us (48%)
  waiting for transfers between devices  130 us (19%)
  blocking collectives  117 us (17%)
  matrix products  32 us (5%)
  local copies, waits for them, and re-layouts  26.3 us (4%)
  loops' own time  21.8 us (3%)
  between operations  14.2 us (2%)
    all_gather x6, blocking collectives, combine(): parts = lax.all_gather(part, axis, axis=0)  104 us
    reduce_scatter x1, waiting for transfers between devices, local(): lax.psum_scatter(2.0 * (weight[:, None] * own - pulled), 'col', scatter_d...  80.2 us
    reduce_sum x24, other arithmetic, single(): return (peak, jnp.sum(jnp.exp(scores - peak[:, None]), axis=1))  74.8 us
    reduce_sum x24, other arithmetic, advance(): jnp.sum(jnp.exp(scores - new_peak[None, :]), axis=0)  74.4 us
    reduce_max x24, other arithmetic, single(): peak = jnp.max(scores, axis=1)  64.3 us
    reduce_max x24, other arithmetic, advance(): new_peak = jnp.maximum(peak, jnp.max(scores, axis=0))  64.1 us
    dynamic_update_slice x8, other arithmetic, local(): plan = lax.map(plan_rows, blocks).reshape(rows, cols)  34.6 us
    all_gather x1, waiting for transfers between devices, local(): imu_rows = lax.all_gather(imu, 'col', axis=0, tiled=True)  31.6 us
  transfers between devices with their start and end apart: 3, of which 3 were waited for; matrix products, arithmetic and copies ran while one was open for 2% of the time, Pallas kernels for 0%

profile of v1, /device:TPU:116, one launch (start us, length us, event | category | flops | bytes accessed | tf_op | source)
XLA Modules:
  0.0 665.3 jit_solution(3283846206429722116)
XLA Ops:
  8.0 12.1 %all_gather.37 = bf16[1,2048,128]{2,1,0:T(8,128)(2,1)S(1)} all-gather(bf16[1,256,128]{2,1,0:T(8,128)(2,1)} %param.19), channel_id=1, replica_groups=mesh['row'=8,'col'=16] {'row'}, dimensions={1}, use_global_device_ids=true | all-gather | bytes 589824 | tf_op jit(solution)/shard_map/all_gather | solution.py:30
  20.5 31.6 %all-gather.8.cloned.1.call-done = bf16[4096,128]{1,0:T(8,128)(2,1)} async-done(((bf16[256,128]{1,0:T(8,128)(2,1)}), bf16[4096,128]{1,0:T(8,128)(2,1)}) %all-gather.8.cloned.1.call-update) | async-done | bytes 1048592 | tf_op jit(solution)/shard_map/all_gather | solution.py:29
  53.9 14.3 %multiply_subtract_fusion = f32[4096,2048]{1,0:T(8,128)} fusion(f32[2048]{0:T(1024)S(1)} %fusion.14, f32[4096]{0:T(1024)S(1)} %fusion.13, bf16[4096,128]{1,0:T(8,128)(2,1)} %all-gather.8.cloned.1.call-done, bf16[1,2048,128]{2,1,0:T(8,128)(2,1)S(1)} %all_gather.37), kind=kOutput, calls=%fused_computation.32 | convolution fusion | flops 2172649472 | bytes 35151872 | tf_op jit(solution)/shard_map/dot_general | solution.py:13
  68.2 56.4 %while.94 = (s32[]{:T(128)}, f32[8,512]{1,0:T(8,128)S(1)}, f32[8,512]{1,0:T(8,128)S(1)}, s32[8]{0:T(128)S(1)}, f32[4096,2048]{1,0:T(8,128)}, /*index=5*/s32[]{:T(128)}, s32[1]{0:T(128)}, s32[]{:T(128)}, s32[]{:T(128)}) while((s32[]{:T(128)}, f32[8,512]{1,0:T(8,128)S(1)}, f32[8,512]{1,0:T(8,128)S(1)}, s32[8]{0:T(128)S(1)}, ...), condition=%wide.region_5.6_spmd, body=%wide.region_2.5_spmd.sunk | while | flops 7339014 | bytes 8403111 | solution.py:53
  124.7 22.4 %all-gather.3 = f32[16,1,4096]{2,1,0:T(1,128)S(1)} all-gather(f32[1,1,4096]{2,1,0:T(1,128)S(1)} %reshape.116), channel_id=1, replica_groups=mesh['row'=8,'col'=16] {'col'}, dimensions={0}, use_global_device_ids=true | all-gather | bytes 278528 | tf_op jit(solution)/shard_map/all_gather | solution.py:22
  147.5 47.5 %while.98 = (s32[]{:T(128)}, f32[2048]{0:T(1024)S(1)}, f32[2048]{0:T(1024)S(1)}, f32[4096]{0:T(1024)S(1)}, f32[4096,2048]{1,0:T(8,128)}, /*index=5*/s32[]{:T(128)}, s32[]{:T(128)}, s32[]{:T(128)}, s32[]{:T(128)}) while((s32[]{:T(128)}, f32[2048]{0:T(1024)S(1)}, f32[2048]{0:T(1024)S(1)}, f32[4096]{0:T(1024)S(1)}, ...), condition=%wide.region_11.12_spmd.clone, body=%wide.region_8.11_spmd.clone.sunk | while | flops 7350279 | bytes 8503458 | solution.py:71
  195.0 11.5 %all-gather = f32[16384]{0:T(1024)S(1)} all-gather(f32[2048]{0:T(1024)S(1)} %log_add_fusion.5), channel_id=2, replica_groups=mesh['row'=8,'col'=16] {'row'}, dimensions={0}, use_global_device_ids=true | all-gather | bytes 73728 | tf_op jit(solution)/shard_map/all_gather | solution.py:22
  206.7 57.6 %while.95 = (s32[]{:T(128)}, f32[8,512]{1,0:T(8,128)S(1)}, f32[8,512]{1,0:T(8,128)S(1)}, f32[2048]{0:T(1024)S(1)}, s32[8]{0:T(128)S(1)}, /*index=5*/f32[4096,204...) while((s32[]{:T(128)}, f32[8,512]{1,0:T(8,128)S(1)}, f32[8,512]{1,0:T(8,128)S(1)}, ...), condition=%wide.region_17.18_spmd, body=%wide.region_14.17_spmd.sunk | while | flops 7339014 | bytes 8419503 | solution.py:53
  264.4 22.4 %all-gather.4 = f32[16,1,4096]{2,1,0:T(1,128)S(1)} all-gather(f32[1,1,4096]{2,1,0:T(1,128)S(1)} %reshape.118), channel_id=1, replica_groups=mesh['row'=8,'col'=16] {'col'}, dimensions={0}, use_global_device_ids=true | all-gather | bytes 278528 | tf_op jit(solution)/shard_map/all_gather | solution.py:22
  287.1 47.5 %while.99 = (s32[]{:T(128)}, f32[2048]{0:T(1024)S(1)}, f32[2048]{0:T(1024)S(1)}, f32[4096]{0:T(1024)S(1)}, f32[4096,2048]{1,0:T(8,128)}, /*index=5*/s32[]{:T(128)}, s32[]{:T(128)}, s32[]{:T(128)}, s32[]{:T(128)}) while((s32[]{:T(128)}, f32[2048]{0:T(1024)S(1)}, f32[2048]{0:T(1024)S(1)}, f32[4096]{0:T(1024)S(1)}, ...), condition=%wide.region_23.24_spmd.clone, body=%wide.region_20.23_spmd.clone.sunk | while | flops 7350279 | bytes 8503458 | solution.py:71
  334.6 12.8 %all-gather.1 = f32[16384]{0:T(1024)S(1)} all-gather(f32[2048]{0:T(1024)S(1)} %log_add_fusion.4), channel_id=3, replica_groups=mesh['row'=8,'col'=16] {'row'}, dimensions={0}, use_global_device_ids=true | all-gather | bytes 73728 | tf_op jit(solution)/shard_map/all_gather | solution.py:22
  347.5 56.7 %while.96 = (s32[]{:T(128)}, f32[8,512]{1,0:T(8,128)S(1)}, f32[8,512]{1,0:T(8,128)S(1)}, f32[2048]{0:T(1024)S(1)}, s32[8]{0:T(128)S(1)}, /*index=5*/f32[4096,204...) while((s32[]{:T(128)}, f32[8,512]{1,0:T(8,128)S(1)}, f32[8,512]{1,0:T(8,128)S(1)}, ...), condition=%wide.region_29.30_spmd, body=%wide.region_26.29_spmd.sunk | while | flops 7339014 | bytes 8419503 | solution.py:53
  404.2 22.4 %all-gather.5 = f32[16,1,4096]{2,1,0:T(1,128)S(1)} all-gather(f32[1,1,4096]{2,1,0:T(1,128)S(1)} %reshape.120), channel_id=1, replica_groups=mesh['row'=8,'col'=16] {'col'}, dimensions={0}, use_global_device_ids=true | all-gather | bytes 278528 | tf_op jit(solution)/shard_map/all_gather | solution.py:22
  427.1 47.5 %while.100 = (s32[]{:T(128)}, f32[2048]{0:T(1024)S(1)}, f32[2048]{0:T(1024)S(1)}, f32[4096]{0:T(1024)S(1)}, f32[4096,2048]{1,0:T(8,128)}, /*index=5*/s32[]{:T(128)}, s32[]{:T(128)}, s32[]{:T(128)}, s32[]{:T(128)}) while((s32[]{:T(128)}, f32[2048]{0:T(1024)S(1)}, f32[2048]{0:T(1024)S(1)}, f32[4096]{0:T(1024)S(1)}, ...), condition=%wide.region_35.36_spmd.clone, body=%wide.region_32.35_spmd.clone.sunk | while | flops 7350279 | bytes 8503458 | solution.py:71
  474.6 13.0 %all-gather.2 = f32[16384]{0:T(1024)S(1)} all-gather(f32[2048]{0:T(1024)S(1)} %log_add_fusion.3), channel_id=4, replica_groups=mesh['row'=8,'col'=16] {'row'}, dimensions={0}, use_global_device_ids=true | all-gather | bytes 73728 | tf_op jit(solution)/shard_map/all_gather | solution.py:22
  487.7 45.2 %while.97 = (s32[]{:T(128)}, bf16[8,512,2048]{2,1,0:T(8,128)(2,1)}, s32[8]{0:T(128)S(1)}, f32[4096]{0:T(1024)S(1)}, f32[2048]{0:T(1024)S(1)}, /*index=5*/f32[409...) while((s32[]{:T(128)}, bf16[8,512,2048]{2,1,0:T(8,128)(2,1)}, s32[8]{0:T(128)S(1)}, ...), condition=%wide.region_39.40_spmd, body=%wide.region_38.39_spmd.sunk | while | flops 4194310 | bytes 6306471 | solution.py:84
  494.7 4.4 fusion.40
  511.6 4.4 fusion.40
  522.9 4.4 fusion.40
  532.9 8.5 %convert_reduce_fusion = (f32[2048]{0:T(1024)S(1)}, f32[8,512]{1,0:T(8,128)S(1)}) fusion(bf16[8,512,2048]{2,1,0:T(8,128)(2,1)} %get-tuple-element.425), kind=kLoop, calls=%fused_computation.30 | loop fusion | flops 25159680 | bytes 16801792 | tf_op jit(solution)/shard_map/reduce_sum | solution.py:86
  543.6 6.0 fusion.12
  549.7 11.7 %fusion.11 = f32[4096,128]{1,0:T(8,128)} fusion(bf16[4096,2048]{1,0:T(8,128)(2,1)} %bitcast.69, bf16[4096,128]{1,0:T(8,128)(2,1)S(1)} %copy-done.1, f32[4096]{0:T(1024)S(1)} %bitcast.78, bf16[1,2048,128]{2,1,0:T(8,128)(2,1)S(1)} %all_gather.37), kind=kOutput, calls=%fused_computation.34 | convolution fusion | flops 2149580800 | bytes 20463616 | tf_op jit(solution)/shard_map/dot_general | solution.py:92
  561.4 17.3 %reduce-scatter.5.cloned.1.call-done = f32[256,128]{1,0:T(8,128)} async-done(((f32[2048,128]{1,0:T(8,128)}), f32[256,128]{1,0:T(8,128)}) %reduce-scatter.5.cloned.1.call-update) | async-done | bytes 131088 | tf_op jit(solution)/shard_map/reduce_scatter | solution.py:100
  578.6 80.2 %reduce-scatter.3.cloned.1.call-done = f32[256,128]{1,0:T(8,128)} async-done(((f32[4096,128]{1,0:T(8,128)}), f32[256,128]{1,0:T(8,128)}) %reduce-scatter.3.cloned.1.call-update) | async-done | bytes 131088 | tf_op jit(solution)/shard_map/reduce_scatter | solution.py:93
  (349 shorter events, 330.3 us)
Async XLA Ops:
  7.2 44.9 %all-gather.8.cloned.1.call-start = ((), (), s32[]{:S(2)}) async-start(), calls=%async_computation.2 | async-start | bytes 1114112 | tf_op jit(solution)/shard_map/all_gather | solution.py:29
  7.9 570.7 %reduce-scatter.5.cloned.1.call-start = ((), (), s32[]{:S(2)}) async-start(), calls=%async_computation.4 | async-start | bytes 1179648 | tf_op jit(solution)/shard_map/reduce_scatter | solution.py:100
  68.2 79.3 %copy-start.2 = (f32[4096]{0:T(1024)S(1)}, f32[4096]{0:T(1024)}, u32[]{:S(2)}) copy-start(f32[4096]{0:T(1024)} %param.20) | copy-start | bytes 49156
  147.5 59.1 %copy-start.3 = (f32[2048]{0:T(1024)S(1)}, f32[2048]{0:T(1024)}, u32[]{:S(2)}) copy-start(f32[2048]{0:T(1024)} %param.21) | copy-start | bytes 24580
  487.7 53.7 %copy-start.1 = (bf16[4096,128]{1,0:T(8,128)(2,1)S(1)}, bf16[4096,128]{1,0:T(8,128)(2,1)}, u32[]{:S(2)}) copy-start(bf16[4096,128]{1,0:T(8,128)(2,1)} %all-gather.8.cloned.1.call-done) | copy-start | bytes 3145732
  532.9 10.7 %copy-start = (bf16[8,512,2048]{2,1,0:T(8,128)(2,1)S(1)}, bf16[8,512,2048]{2,1,0:T(8,128)(2,1)}, u32[]{:S(2)}) copy-start(bf16[8,512,2048]{2,1,0:T(8,128)(2,1)} %get-tuple-element.425) | copy-start | bytes 50331652
  549.6 109.2 %reduce-scatter.3.cloned.1.call-start = ((), (), s32[]{:S(2)}) async-start(), calls=%async_computation.3 | async-start | bytes 2228224 | tf_op jit(solution)/shard_map/reduce_scatter | solution.py:93
Sparse Core Ops, SparseCore 0:
  10.1 41.8 all-gather.7
  549.7 28.8 reduce-scatter.4
  582.5 76.2 reduce-scatter.2

commit v2 on v1

v2 whole, which is shorter than its diff:
```python
import jax
import jax.numpy as jnp
from jax import lax
from jax.experimental import pallas as pl
from jax.experimental.pallas import tpu as pltpu
from jax.sharding import PartitionSpec as P

D = 128
ITERS = 3
EPS = D / 20.0
INV = 1.0 / EPS
TWO_INV = 2.0 / EPS
ROW_TILE = 512
COL_TILE = 256
VMEM_LIMIT = 60 * 1024 * 1024
NT = (((1,), (1,)), ((), ()))
TN = (((0,), (0,)), ((), ()))


def _params(semantics):
    return pltpu.CompilerParams(dimension_semantics=semantics, vmem_limit_bytes=VMEM_LIMIT)


def _row_kernel(x_ref, y_ref, b_ref, a_ref, o_ref):
    cross = lax.dot_general(x_ref[...], y_ref[...], NT, preferred_element_type=jnp.float32)
    t = a_ref[...] + TWO_INV * cross
    top = jnp.max(t, axis=1, keepdims=True)
    total = jnp.sum(jnp.exp(t - top), axis=1, keepdims=True)
    o_ref[...] = top + jnp.log(total) - b_ref[...]


def row_lse(x, y, b, a):
    rows, cols = x.shape[0], y.shape[0]
    return pl.pallas_call(
        _row_kernel,
        out_shape=jax.ShapeDtypeStruct((rows, 1), jnp.float32),
        grid=(rows // ROW_TILE,),
        in_specs=[
            pl.BlockSpec((ROW_TILE, D), lambda i: (i, 0)),
            pl.BlockSpec((cols, D), lambda i: (0, 0)),
            pl.BlockSpec((ROW_TILE, 1), lambda i: (i, 0)),
            pl.BlockSpec((1, cols), lambda i: (0, 0)),
        ],
        out_specs=pl.BlockSpec((ROW_TILE, 1), lambda i: (i, 0)),
        compiler_params=_params(("arbitrary",)),
    )(x, y, b, a)


def _col_kernel(x_ref, y_ref, u_ref, b_ref, o_ref):
    cross = lax.dot_general(x_ref[...], y_ref[...], NT, preferred_element_type=jnp.float32)
    t = u_ref[...] + TWO_INV * cross
    top = jnp.max(t, axis=0, keepdims=True)
    total = jnp.sum(jnp.exp(t - top), axis=0, keepdims=True)
    o_ref[...] = top + jnp.log(total) - b_ref[...]


def col_lse(x, y, u, b):
    rows, cols = x.shape[0], y.shape[0]
    return pl.pallas_call(
        _col_kernel,
        out_shape=jax.ShapeDtypeStruct((1, cols), jnp.float32),
        grid=(cols // COL_TILE,),
        in_specs=[
            pl.BlockSpec((rows, D), lambda j: (0, 0)),
            pl.BlockSpec((COL_TILE, D), lambda j: (j, 0)),
            pl.BlockSpec((rows, 1), lambda j: (0, 0)),
            pl.BlockSpec((1, COL_TILE), lambda j: (0, j)),
        ],
        out_specs=pl.BlockSpec((1, COL_TILE), lambda j: (0, j)),
        compiler_params=_params(("arbitrary",)),
    )(x, y, u, b)


def _plan_kernel(x_ref, y_ref, u_ref, a_ref, gi_ref, pc_ref, c_ref):
    @pl.when(pl.program_id(0) == 0)
    def _():
        pc_ref[...] = jnp.zeros_like(pc_ref)
        c_ref[...] = jnp.zeros_like(c_ref)

    x = x_ref[...]
    cross = lax.dot_general(x, y_ref[...], NT, preferred_element_type=jnp.float32)
    plan = jnp.exp(u_ref[...] + a_ref[...] + TWO_INV * cross).astype(jnp.bfloat16)
    wide = plan.astype(jnp.float32)
    r = jnp.sum(wide, axis=1, keepdims=True)
    c_ref[...] += jnp.sum(wide, axis=0, keepdims=True)
    pulled = jnp.dot(plan, y_ref[...], preferred_element_type=jnp.float32)
    gi_ref[...] = 2.0 * (r * x.astype(jnp.float32) - pulled)
    pc_ref[...] += lax.dot_general(plan, x, TN, preferred_element_type=jnp.float32)


def plan_grads(x, y, u, a):
    rows, cols = x.shape[0], y.shape[0]
    return pl.pallas_call(
        _plan_kernel,
        out_shape=(
            jax.ShapeDtypeStruct((rows, D), jnp.float32),
            jax.ShapeDtypeStruct((cols, D), jnp.float32),
            jax.ShapeDtypeStruct((1, cols), jnp.float32),
        ),
        grid=(rows // ROW_TILE,),
        in_specs=[
            pl.BlockSpec((ROW_TILE, D), lambda i: (i, 0)),
            pl.BlockSpec((cols, D), lambda i: (0, 0)),
            pl.BlockSpec((ROW_TILE, 1), lambda i: (i, 0)),
            pl.BlockSpec((1, cols), lambda i: (0, 0)),
        ],
        out_specs=(
            pl.BlockSpec((ROW_TILE, D), lambda i: (i, 0)),
            pl.BlockSpec((cols, D), lambda i: (0, 0)),
            pl.BlockSpec((1, cols), lambda i: (0, 0)),
        ),
        compiler_params=_params(("arbitrary",)),
    )(x, y, u, a)


def squares(values):
    return jnp.sum(jnp.square(values.astype(jnp.float32)), axis=1)


def combine(part, axis):
    parts = lax.all_gather(part, axis, axis=0)
    top = jnp.max(parts, axis=0)
    return top + jnp.log(jnp.sum(jnp.exp(parts - top[None, :]), axis=0))


def local(imu, camera, imu_mass, cam_mass):
    imu_rows = lax.all_gather(imu, "col", axis=0, tiled=True)
    cam_rows = lax.all_gather(camera, "row", axis=1, tiled=True)[0]
    rows_sq = squares(imu_rows)
    cols_sq = squares(cam_rows)
    log_a = jnp.log(imu_mass)
    log_b = jnp.log(cam_mass)
    row_b = (rows_sq * INV)[:, None]
    col_b = (cols_sq * INV)[None, :]

    g = jnp.zeros_like(cols_sq)
    f = jnp.zeros_like(rows_sq)
    for step in range(ITERS):
        a = (g[None, :] - cols_sq[None, :]) * INV
        lse = combine(row_lse(imu_rows, cam_rows, row_b, a)[:, 0], "col")
        f = EPS * log_a - EPS * lse
        u = ((f - rows_sq) * INV)[:, None]
        lse = combine(col_lse(imu_rows, cam_rows, u, col_b)[0], "row")
        g = EPS * log_b - EPS * lse

    a = (g[None, :] - cols_sq[None, :]) * INV
    u = ((f - rows_sq) * INV)[:, None]
    grad_rows, pulled_cam, col_total = plan_grads(imu_rows, cam_rows, u, a)
    grad_cols = 2.0 * (col_total[0][:, None] * cam_rows.astype(jnp.float32) - pulled_cam)
    grad_imu = lax.psum_scatter(grad_rows, "col", scatter_dimension=0, tiled=True)
    grad_cam = lax.psum_scatter(grad_cols, "row", scatter_dimension=0, tiled=True)
    return (grad_imu, grad_cam[None])


def solution(mesh):
    in_specs = (P(("row", "col"), None), P("col", "row", None), P("row"), P("col"))
    out_specs = (P(("row", "col"), None), P("col", "row", None))
    return jax.shard_map(local, mesh=mesh, in_specs=in_specs, out_specs=out_specs, check_vma=False)
```

time: 673 us -> 922 us (1.37)
  blocking collectives: 117 us -> 590 us
  other arithmetic: 325 us -> 53.7 us
  Pallas kernels: 0 us -> 110 us
  matrix products: 32 us -> 0 us
  loops' own time: 21.8 us -> 0 us
  local copies, waits for them, and re-layouts: 26.3 us -> 8.09 us
  waiting for transfers between devices: 130 us -> 141 us
    all_gather x6, blocking collectives: 104 us -> 578 us  [combine(): parts = lax.all_gather(part, axis, axis=0)]
    reduce_sum x49 -> x0, other arithmetic: 158 us -> none  [the longest x24 74.8 us: single(): return (peak, jnp.sum(jnp.exp(scores - peak[:, None]), axis=1))]
    reduce_max x48 -> x0, other arithmetic: 128 us -> none  [the longest x24 64.3 us: single(): peak = jnp.max(scores, axis=1)]
    pallas_call x0 -> x7, Pallas kernels: none -> 110 us  [the longest x3 49.8 us: col_lse(): pl.pallas_call(_col_kernel, out_shape=jax.ShapeDtypeStruct((1, cols), jnp...]
    all_gather x0 -> x3, other arithmetic: none -> 45.8 us  [combine(): parts = lax.all_gather(part, axis, axis=0)]
    dynamic_update_slice x8 -> x0, other arithmetic: 34.6 us -> none  [local(): plan = lax.map(plan_rows, blocks).reshape(rows, cols)]
    dot_general x3 -> x0, matrix products: 32 us -> none  [the longest x1 14.3 us: cost_block(): cross = jnp.dot(rows, cols.T, preferred_element_type=jnp.float32)]
    another operation x7 -> x0, loops' own time: 21.8 us -> none  [the longest x3 15 us: row_lse(): peak, total = lax.map(single, blocks)]
  transfers between devices with their start and end apart: 3 -> 3, of which waited for: 3 -> 3; matrix products, arithmetic and copies ran while one was open for 2% -> 0% of each run, Pallas kernels for 0% -> 0%
where the time goes in v2:
time: 922 us; the launch traced here: 917 us
  blocking collectives  590 us (64%)
  waiting for transfers between devices  141 us (15%)
  Pallas kernels  110 us (12%)
  other arithmetic  53.7 us (6%)
  between operations  13.9 us (2%)
    all_gather x6, blocking collectives, combine(): parts = lax.all_gather(part, axis, axis=0)  578 us
    reduce_scatter x1, waiting for transfers between devices, local(): lax.psum_scatter(grad_rows, 'col', scatter_dimension=0, tiled=True)  80.2 us
    pallas_call x3, Pallas kernels, col_lse(): pl.pallas_call(_col_kernel, out_shape=jax.ShapeDtypeStruct((1, cols), jnp...  49.8 us
    all_gather x3, other arithmetic, combine(): parts = lax.all_gather(part, axis, axis=0)  45.8 us
    pallas_call x3, Pallas kernels, row_lse(): pl.pallas_call(_row_kernel, out_shape=jax.ShapeDtypeStruct((rows, 1), jnp...  40 us
    all_gather x1, waiting for transfers between devices, local(): imu_rows = lax.all_gather(imu, 'col', axis=0, tiled=True)  31 us
    reduce_scatter x1, waiting for transfers between devices, local(): lax.psum_scatter(grad_cols, 'row', scatter_dimension=0, tiled=True)  28.3 us
    pallas_call x1, Pallas kernels, plan_grads(): pl.pallas_call(_plan_kernel, out_shape=(jax.ShapeDtypeStruct((rows, D), j...  20.6 us
  transfers between devices with their start and end apart: 3, of which 3 were waited for; matrix products, arithmetic and copies ran while one was open for 0% of the time, Pallas kernels for 0%

profile of v2, /device:TPU:116, one launch (start us, length us, event | category | flops | bytes accessed | tf_op | source)
XLA Modules:
  0.0 917.4 jit_solution(5682778065068161983)
XLA Ops:
  7.9 12.1 %all_gather.25 = bf16[1,2048,128]{2,1,0:T(8,128)(2,1)S(1)} all-gather(bf16[1,256,128]{2,1,0:T(8,128)(2,1)} %param.5), channel_id=1, replica_groups=mesh['row'=8,'col'=16] {'row'}, dimensions={1}, use_global_device_ids=true | all-gather | bytes 589824 | tf_op jit(solution)/shard_map/all_gather | solution.py:128
  21.0 31.0 %all-gather.8.cloned.1.call-done.x_ref = bf16[4096,128]{1,0:T(8,128)(2,1)} async-done(((bf16[256,128]{1,0:T(8,128)(2,1)}), bf16[4096,128]{1,0:T(8,128)(2,1)}) %all-gather.8.cloned.1.call-update) | async-done | bytes 1048592 | tf_op jit(solution)/shard_map/all_gather | solution.py:127
  53.9 2.0 copy.17.b_ref
  55.9 13.4 %shard_map.59 = f32[4096,1]{1,0:T(8,128)} custom-call(bf16[4096,128]{1,0:T(8,128)(2,1)} %all-gather.8.cloned.1.call-done.x_ref, bf16[2048,128]{1,0:T(8,128)(2,1)} %bitcast.35, f32[4096,1]{1,0:T(8,128)} %copy.17.b_ref, f32[1,2048]{1,0:T(1,128)} %bitcast.49), custom_call_target="tpu_custom_call" | custom-call | tf_op jit(solution)/shard_map/pallas_call | solution.py:34
  69.2 177.8 %all-gather = f32[65536,1]{1,0:T(8,128)} all-gather(f32[4096,1]{1,0:T(8,128)} %shard_map.59), channel_id=2, replica_groups=mesh['row'=8,'col'=16] {'col'}, dimensions={0}, use_global_device_ids=true | all-gather | bytes 278528 | tf_op jit(solution)/shard_map/all_gather | solution.py:121
  247.0 15.3 %reduce.3 = f32[65536]{0:T(1024)S(1)} reduce(f32[65536,1]{1,0:T(8,128)} %all-gather, f32[]{:T(128)} %constant.2), dimensions={1}, to_apply=%all-gather.reduce_sub_computation | reduce | bytes 524292 | tf_op jit(solution)/shard_map/all_gather | solution.py:121
  262.5 2.0 copy.14.u_ref
  264.5 16.6 %shard_map.60 = f32[1,2048]{1,0:T(1,128)} custom-call(bf16[4096,128]{1,0:T(8,128)(2,1)} %all-gather.8.cloned.1.call-done.x_ref, bf16[2048,128]{1,0:T(8,128)(2,1)} %bitcast.36, f32[4096,1]{1,0:T(8,128)} %copy.14.u_ref, f32[1,2048]{1,0:T(1,128)} %bitcast.42), custom_call_target="tpu_custom_call" | custom-call | tf_op jit(solution)/shard_map/pallas_call | solution.py:59
  281.1 11.7 %all-gather.3 = f32[8,1,2048]{2,1,0:T(1,128)S(1)} all-gather(f32[1,1,2048]{2,1,0:T(1,128)} %bitcast.53), channel_id=1, replica_groups=mesh['row'=8,'col'=16] {'row'}, dimensions={0}, use_global_device_ids=true | all-gather | bytes 73728 | tf_op jit(solution)/shard_map/all_gather | solution.py:121
  293.6 13.3 %shard_map.61 = f32[4096,1]{1,0:T(8,128)} custom-call(bf16[4096,128]{1,0:T(8,128)(2,1)} %all-gather.8.cloned.1.call-done.x_ref, bf16[2048,128]{1,0:T(8,128)(2,1)} %bitcast.37, f32[4096,1]{1,0:T(8,128)} %copy.17.b_ref, f32[1,2048]{1,0:T(1,128)} %bitcast.52), custom_call_target="tpu_custom_call" | custom-call | tf_op jit(solution)/shard_map/pallas_call | solution.py:34
  306.9 181.3 %all-gather.1 = f32[65536,1]{1,0:T(8,128)} all-gather(f32[4096,1]{1,0:T(8,128)} %shard_map.61), channel_id=3, replica_groups=mesh['row'=8,'col'=16] {'col'}, dimensions={0}, use_global_device_ids=true | all-gather | bytes 278528 | tf_op jit(solution)/shard_map/all_gather | solution.py:121
  488.3 15.3 %reduce.4 = f32[65536]{0:T(1024)S(1)} reduce(f32[65536,1]{1,0:T(8,128)} %all-gather.1, f32[]{:T(128)} %constant.2), dimensions={1}, to_apply=%all-gather.1.reduce_sub_computation | reduce | bytes 524292 | tf_op jit(solution)/shard_map/all_gather | solution.py:121
  503.7 2.0 copy.16.u_ref
  505.8 16.6 %shard_map.62 = f32[1,2048]{1,0:T(1,128)} custom-call(bf16[4096,128]{1,0:T(8,128)(2,1)} %all-gather.8.cloned.1.call-done.x_ref, bf16[2048,128]{1,0:T(8,128)(2,1)} %bitcast.38, f32[4096,1]{1,0:T(8,128)} %copy.16.u_ref, f32[1,2048]{1,0:T(1,128)} %bitcast.43), custom_call_target="tpu_custom_call" | custom-call | tf_op jit(solution)/shard_map/pallas_call | solution.py:59
  522.4 12.9 %all-gather.4 = f32[8,1,2048]{2,1,0:T(1,128)S(1)} all-gather(f32[1,1,2048]{2,1,0:T(1,128)} %bitcast.54), channel_id=1, replica_groups=mesh['row'=8,'col'=16] {'row'}, dimensions={0}, use_global_device_ids=true | all-gather | bytes 73728 | tf_op jit(solution)/shard_map/all_gather | solution.py:121
  536.0 13.3 %shard_map.63 = f32[4096,1]{1,0:T(8,128)} custom-call(bf16[4096,128]{1,0:T(8,128)(2,1)} %all-gather.8.cloned.1.call-done.x_ref, bf16[2048,128]{1,0:T(8,128)(2,1)} %bitcast.39, f32[4096,1]{1,0:T(8,128)} %copy.17.b_ref, f32[1,2048]{1,0:T(1,128)} %bitcast.51), custom_call_target="tpu_custom_call" | custom-call | tf_op jit(solution)/shard_map/pallas_call | solution.py:34
  549.4 181.2 %all-gather.2 = f32[65536,1]{1,0:T(8,128)} all-gather(f32[4096,1]{1,0:T(8,128)} %shard_map.63), channel_id=4, replica_groups=mesh['row'=8,'col'=16] {'col'}, dimensions={0}, use_global_device_ids=true | all-gather | bytes 278528 | tf_op jit(solution)/shard_map/all_gather | solution.py:121
  730.5 15.3 %reduce.5 = f32[65536]{0:T(1024)S(1)} reduce(f32[65536,1]{1,0:T(8,128)} %all-gather.2, f32[]{:T(128)} %constant.2), dimensions={1}, to_apply=%all-gather.2.reduce_sub_computation | reduce | bytes 524292 | tf_op jit(solution)/shard_map/all_gather | solution.py:121
  748.0 16.6 %shard_map.64 = f32[1,2048]{1,0:T(1,128)} custom-call(bf16[4096,128]{1,0:T(8,128)(2,1)} %all-gather.8.cloned.1.call-done.x_ref, bf16[2048,128]{1,0:T(8,128)(2,1)} %bitcast.40, f32[4096,1]{1,0:T(8,128)} %copy.19.u_ref, f32[1,2048]{1,0:T(1,128)} %bitcast.44), custom_call_target="tpu_custom_call" | custom-call | tf_op jit(solution)/shard_map/pallas_call | solution.py:59
  764.6 13.3 %all-gather.5 = f32[8,1,2048]{2,1,0:T(1,128)S(1)} all-gather(f32[1,1,2048]{2,1,0:T(1,128)} %bitcast.55), channel_id=1, replica_groups=mesh['row'=8,'col'=16] {'row'}, dimensions={0}, use_global_device_ids=true | all-gather | bytes 73728 | tf_op jit(solution)/shard_map/all_gather | solution.py:121
  778.6 20.6 %shard_map.65 = (f32[4096,128]{1,0:T(8,128)}, f32[2048,128]{1,0:T(8,128)}, f32[1,2048]{1,0:T(1,128)}) custom-call(bf16[4096,128]{1,0:T(8,128)(2,1)} %all-gather.8.cloned.1.call-done.x_ref, bf16[2048,128]{1,0:T(8,128)(2,1)} %bitcast.41, f32[4096,1]{1,0:T(8,128)} %copy.19.u_ref, f32[1,2048]{1,0:T(1,128)} %bitcast.50), custom_call_target="tpu_custom_call" | custom-call | tf_op jit(solution)/shard_map/pallas_call | solution.py:93
  799.2 2.5 fusion.2
  802.5 28.3 %reduce-scatter.5.cloned.1.call-done = f32[256,128]{1,0:T(8,128)} async-done(((f32[2048,128]{1,0:T(8,128)}), f32[256,128]{1,0:T(8,128)}) %reduce-scatter.5.cloned.1.call-update) | async-done | bytes 131088 | tf_op jit(solution)/shard_map/reduce_scatter | solution.py:151
  830.7 80.2 %reduce-scatter.3.cloned.1.call-done = f32[256,128]{1,0:T(8,128)} async-done(((f32[4096,128]{1,0:T(8,128)}), f32[256,128]{1,0:T(8,128)}) %reduce-scatter.3.cloned.1.call-update) | async-done | bytes 131088 | tf_op jit(solution)/shard_map/reduce_scatter | solution.py:150
  (40 shorter events, 8.9 us)
Async XLA Ops:
  7.2 44.9 %all-gather.8.cloned.1.call-start = ((), (), s32[]{:S(2)}) async-start(), calls=%async_computation.2 | async-start | bytes 1114112 | tf_op jit(solution)/shard_map/all_gather | solution.py:127
  7.9 822.8 %reduce-scatter.5.cloned.1.call-start = ((), (), s32[]{:S(2)}) async-start(), calls=%async_computation.4 | async-start | bytes 1179648 | tf_op jit(solution)/shard_map/reduce_scatter | solution.py:151
  20.1 35.8 %copy-start = (bf16[1,2048,128]{2,1,0:T(8,128)(2,1)}, bf16[1,2048,128]{2,1,0:T(8,128)(2,1)S(1)}, u32[]{:S(2)}) copy-start(bf16[1,2048,128]{2,1,0:T(8,128)(2,1)S(1)} %all_gather.25) | copy-start | bytes 1572868
  247.0 15.5 %copy-start.2 = (f32[4096]{0:T(1024)S(1)}, f32[4096]{0:T(1024)}, u32[]{:S(2)}) copy-start(f32[4096]{0:T(1024)} %param.6) | copy-start | bytes 49156
  264.5 28.5 %copy-start.3 = (f32[2048]{0:T(1024)S(1)}, f32[2048]{0:T(1024)}, u32[]{:S(2)}) copy-start(f32[2048]{0:T(1024)} %param.7) | copy-start | bytes 24580
  764.6 34.6 %copy-start.1 = (bf16[1,2048,128]{2,1,0:T(8,128)(2,1)S(1)}, bf16[1,2048,128]{2,1,0:T(8,128)(2,1)}, u32[]{:S(2)}) copy-start(bf16[1,2048,128]{2,1,0:T(8,128)(2,1)} %copy-done) | copy-start | bytes 1572868
  801.8 109.2 %reduce-scatter.3.cloned.1.call-start = ((), (), s32[]{:S(2)}) async-start(), calls=%async_computation.3 | async-start | bytes 2228224 | tf_op jit(solution)/shard_map/reduce_scatter | solution.py:150
Sparse Core Ops, SparseCore 0:
  10.1 41.8 all-gather.7
  801.9 28.8 reduce-scatter.4
  834.6 76.2 reduce-scatter.2

commit v3 on v2

--- a/solution.py
+++ b/solution.py
@@ -21,54 +21,37 @@
     return pltpu.CompilerParams(dimension_semantics=semantics, vmem_limit_bytes=VMEM_LIMIT)
 
 
-def _row_kernel(x_ref, y_ref, b_ref, a_ref, o_ref):
-    cross = lax.dot_general(x_ref[...], y_ref[...], NT, preferred_element_type=jnp.float32)
+def _to_row(col):
+    return jnp.transpose(jnp.broadcast_to(col, (col.shape[0], D)))[0:1, :]
+
+
+def _to_col(row):
+    return jnp.transpose(jnp.broadcast_to(row, (D, row.shape[1])))[:, 0:1]
+
+
+def _lse_kernel(p_ref, q_ref, a_ref, b_ref, o_ref):
+    cross = lax.dot_general(p_ref[...], q_ref[...], NT, preferred_element_type=jnp.float32)
     t = a_ref[...] + TWO_INV * cross
     top = jnp.max(t, axis=1, keepdims=True)
     total = jnp.sum(jnp.exp(t - top), axis=1, keepdims=True)
-    o_ref[...] = top + jnp.log(total) - b_ref[...]
+    o_ref[...] = _to_row(top + jnp.log(total)) - b_ref[...]
 
 
-def row_lse(x, y, b, a):
-    rows, cols = x.shape[0], y.shape[0]
+def lse(p, q, a, b, tile):
+    rows, cols = p.shape[0], q.shape[0]
     return pl.pallas_call(
-        _row_kernel,
-        out_shape=jax.ShapeDtypeStruct((rows, 1), jnp.float32),
-        grid=(rows // ROW_TILE,),
+        _lse_kernel,
+        out_shape=jax.ShapeDtypeStruct((1, rows), jnp.float32),
+        grid=(rows // tile,),
         in_specs=[
-            pl.BlockSpec((ROW_TILE, D), lambda i: (i, 0)),
+            pl.BlockSpec((tile, D), lambda i: (i, 0)),
             pl.BlockSpec((cols, D), lambda i: (0, 0)),
-            pl.BlockSpec((ROW_TILE, 1), lambda i: (i, 0)),
             pl.BlockSpec((1, cols), lambda i: (0, 0)),
+            pl.BlockSpec((1, tile), lambda i: (0, i)),
         ],
-        out_specs=pl.BlockSpec((ROW_TILE, 1), lambda i: (i, 0)),
+        out_specs=pl.BlockSpec((1, tile), lambda i: (0, i)),
         compiler_params=_params(("arbitrary",)),
-    )(x, y, b, a)
-
-
-def _col_kernel(x_ref, y_ref, u_ref, b_ref, o_ref):
-    cross = lax.dot_general(x_ref[...], y_ref[...], NT, preferred_element_type=jnp.float32)
-    t = u_ref[...] + TWO_INV * cross
-    top = jnp.max(t, axis=0, keepdims=True)
-    total = jnp.sum(jnp.exp(t - top), axis=0, keepdims=True)
-    o_ref[...] = top + jnp.log(total) - b_ref[...]
-
-
-def col_lse(x, y, u, b):
-    rows, cols = x.shape[0], y.shape[0]
-    return pl.pallas_call(
-        _col_kernel,
-        out_shape=jax.ShapeDtypeStruct((1, cols), jnp.float32),
-        grid=(cols // COL_TILE,),
-        in_specs=[
-            pl.BlockSpec((rows, D), lambda j: (0, 0)),
-            pl.BlockSpec((COL_TILE, D), lambda j: (j, 0)),
-            pl.BlockSpec((rows, 1), lambda j: (0, 0)),
-            pl.BlockSpec((1, COL_TILE), lambda j: (0, j)),
-        ],
-        out_specs=pl.BlockSpec((1, COL_TILE), lambda j: (0, j)),
-        compiler_params=_params(("arbitrary",)),
-    )(x, y, u, b)
+    )(p, q, a, b)
 
 
 def _plan_kernel(x_ref, y_ref, u_ref, a_ref, gi_ref, pc_ref, c_ref):
@@ -79,7 +62,7 @@
 
     x = x_ref[...]
     cross = lax.dot_general(x, y_ref[...], NT, preferred_element_type=jnp.float32)
-    plan = jnp.exp(u_ref[...] + a_ref[...] + TWO_INV * cross).astype(jnp.bfloat16)
+    plan = jnp.exp(_to_col(u_ref[...]) + a_ref[...] + TWO_INV * cross).astype(jnp.bfloat16)
     wide = plan.astype(jnp.float32)
     r = jnp.sum(wide, axis=1, keepdims=True)
     c_ref[...] += jnp.sum(wide, axis=0, keepdims=True)
@@ -101,7 +84,7 @@
         in_specs=[
             pl.BlockSpec((ROW_TILE, D), lambda i: (i, 0)),
             pl.BlockSpec((cols, D), lambda i: (0, 0)),
-            pl.BlockSpec((ROW_TILE, 1), lambda i: (i, 0)),
+            pl.BlockSpec((1, ROW_TILE), lambda i: (0, i)),
             pl.BlockSpec((1, cols), lambda i: (0, 0)),
         ],
         out_specs=(
@@ -130,21 +113,21 @@
     cols_sq = squares(cam_rows)
     log_a = jnp.log(imu_mass)
     log_b = jnp.log(cam_mass)
-    row_b = (rows_sq * INV)[:, None]
+    row_b = (rows_sq * INV)[None, :]
     col_b = (cols_sq * INV)[None, :]
 
     g = jnp.zeros_like(cols_sq)
     f = jnp.zeros_like(rows_sq)
     for step in range(ITERS):
         a = (g[None, :] - cols_sq[None, :]) * INV
-        lse = combine(row_lse(imu_rows, cam_rows, row_b, a)[:, 0], "col")
-        f = EPS * log_a - EPS * lse
-        u = ((f - rows_sq) * INV)[:, None]
-        lse = combine(col_lse(imu_rows, cam_rows, u, col_b)[0], "row")
-        g = EPS * log_b - EPS * lse
+        lse_f = combine(lse(imu_rows, cam_rows, a, row_b, ROW_TILE)[0], "col")
+        f = EPS * log_a - EPS * lse_f
+        u = ((f - rows_sq) * INV)[None, :]
+        lse_g = combine(lse(cam_rows, imu_rows, u, col_b, COL_TILE)[0], "row")
+        g = EPS * log_b - EPS * lse_g
 
     a = (g[None, :] - cols_sq[None, :]) * INV
-    u = ((f - rows_sq) * INV)[:, None]
+    u = ((f - rows_sq) * INV)[None, :]
     grad_rows, pulled_cam, col_total = plan_grads(imu_rows, cam_rows, u, a)
     grad_cols = 2.0 * (col_total[0][:, None] * cam_rows.astype(jnp.float32) - pulled_cam)
     grad_imu = lax.psum_scatter(grad_rows, "col", scatter_dimension=0, tiled=True)

time: 922 us -> 389 us (0.42)
  blocking collectives: 590 us -> 117 us
  other arithmetic: 53.7 us -> 11 us
    all_gather x6, blocking collectives: 578 us -> 105 us  [combine(): parts = lax.all_gather(part, axis, axis=0)]
    all_gather x3 -> x0, other arithmetic: 45.8 us -> none  [combine(): parts = lax.all_gather(part, axis, axis=0)]
where the time goes in v3:
time: 389 us; the launch traced here: 385 us
  waiting for transfers between devices  141 us (36%)
  blocking collectives  117 us (30%)
  Pallas kernels  102 us (26%)
  between operations  13.8 us (4%)
  other arithmetic  11 us (3%)
    all_gather x6, blocking collectives, combine(): parts = lax.all_gather(part, axis, axis=0)  105 us
    pallas_call x6, Pallas kernels, lse(): pl.pallas_call(_lse_kernel, out_shape=jax.ShapeDtypeStruct((1, rows), jnp...  82 us
    reduce_scatter x1, waiting for transfers between devices, local(): lax.psum_scatter(grad_rows, 'col', scatter_dimension=0, tiled=True)  80.1 us
    all_gather x1, waiting for transfers between devices, local(): imu_rows = lax.all_gather(imu, 'col', axis=0, tiled=True)  31 us
    reduce_scatter x1, waiting for transfers between devices, local(): lax.psum_scatter(grad_cols, 'row', scatter_dimension=0, tiled=True)  28.3 us
    pallas_call x1, Pallas kernels, plan_grads(): pl.pallas_call(_plan_kernel, out_shape=(jax.ShapeDtypeStruct((rows, D), j...  20.4 us
    all_gather x1, blocking collectives, local(): cam_rows = lax.all_gather(camera, 'row', axis=1, tiled=True)[0]  12.1 us
  transfers between devices with their start and end apart: 3, of which 3 were waited for; matrix products, arithmetic and copies ran while one was open for 0% of the time, Pallas kernels for 0%

profile of v3, /device:TPU:116, one launch (start us, length us, event | category | flops | bytes accessed | tf_op | source)
XLA Modules:
  0.0 385.1 jit_solution(11768431825267629349)
XLA Ops:
  7.2 0.7 all-gather.8.cloned.1.call-update
  7.9 12.1 %all_gather.25 = bf16[1,2048,128]{2,1,0:T(8,128)(2,1)S(1)} all-gather(bf16[1,256,128]{2,1,0:T(8,128)(2,1)} %param.5), channel_id=1, replica_groups=mesh['row'=8,'col'=16] {'row'}, dimensions={1}, use_global_device_ids=true | all-gather | bytes 589824 | tf_op jit(solution)/shard_map/all_gather | solution.py:111
  21.0 31.0 %all-gather.8.cloned.1.call-done.p_ref.q_ref.x_ref = bf16[4096,128]{1,0:T(8,128)(2,1)} async-done(((bf16[256,128]{1,0:T(8,128)(2,1)}), bf16[4096,128]{1,0:T(8,128)(2,1)}) %all-gather.8.cloned.1.call-update) | async-done | bytes 1048592 | tf_op jit(solution)/shard_map/all_gather | solution.py:110
  52.0 1.8 multiply_reduce_fusion
  54.5 13.6 %shard_map.59 = f32[1,4096]{1,0:T(1,128)} custom-call(bf16[4096,128]{1,0:T(8,128)(2,1)} %all-gather.8.cloned.1.call-done.p_ref.q_ref.x_ref, bf16[2048,128]{1,0:T(8,128)(2,1)} %bitcast.56, f32[1,2048]{1,0:T(1,128)} %bitcast.77, f32[1,4096]{1,0:T(1,128)} %bitcast.63), custom_call_target="tpu_custom_call" | custom-call | tf_op jit(solution)/shard_map/pallas_call | solution.py:42
  68.1 22.4 %all-gather = f32[16,1,4096]{2,1,0:T(1,128)S(1)} all-gather(f32[1,1,4096]{2,1,0:T(1,128)} %bitcast.74), channel_id=1, replica_groups=mesh['row'=8,'col'=16] {'col'}, dimensions={0}, use_global_device_ids=true | all-gather | bytes 278528 | tf_op jit(solution)/shard_map/all_gather | solution.py:104
  90.9 0.6 subtract_multiply_fusion.2
  91.5 13.8 %shard_map.60 = f32[1,2048]{1,0:T(1,128)} custom-call(bf16[2048,128]{1,0:T(8,128)(2,1)} %bitcast.57, bf16[4096,128]{1,0:T(8,128)(2,1)} %all-gather.8.cloned.1.call-done.p_ref.q_ref.x_ref, f32[1,4096]{1,0:T(1,128)} %bitcast.71, f32[1,2048]{1,0:T(1,128)} %bitcast.68), custom_call_target="tpu_custom_call" | custom-call | tf_op jit(solution)/shard_map/pallas_call | solution.py:42
  105.3 11.7 %all-gather.1 = f32[8,1,2048]{2,1,0:T(1,128)S(1)} all-gather(f32[1,1,2048]{2,1,0:T(1,128)} %bitcast.80), channel_id=1, replica_groups=mesh['row'=8,'col'=16] {'row'}, dimensions={0}, use_global_device_ids=true | all-gather | bytes 73728 | tf_op jit(solution)/shard_map/all_gather | solution.py:104
  117.7 13.6 %shard_map.61 = f32[1,4096]{1,0:T(1,128)} custom-call(bf16[4096,128]{1,0:T(8,128)(2,1)} %all-gather.8.cloned.1.call-done.p_ref.q_ref.x_ref, bf16[2048,128]{1,0:T(8,128)(2,1)} %bitcast.58, f32[1,2048]{1,0:T(1,128)} %bitcast.79, f32[1,4096]{1,0:T(1,128)} %bitcast.64), custom_call_target="tpu_custom_call" | custom-call | tf_op jit(solution)/shard_map/pallas_call | solution.py:42
  131.3 22.2 %all-gather.2 = f32[16,1,4096]{2,1,0:T(1,128)S(1)} all-gather(f32[1,1,4096]{2,1,0:T(1,128)} %bitcast.75), channel_id=1, replica_groups=mesh['row'=8,'col'=16] {'col'}, dimensions={0}, use_global_device_ids=true | all-gather | bytes 278528 | tf_op jit(solution)/shard_map/all_gather | solution.py:104
  153.8 0.6 subtract_multiply_fusion.1
  154.4 13.8 %shard_map.62 = f32[1,2048]{1,0:T(1,128)} custom-call(bf16[2048,128]{1,0:T(8,128)(2,1)} %bitcast.59, bf16[4096,128]{1,0:T(8,128)(2,1)} %all-gather.8.cloned.1.call-done.p_ref.q_ref.x_ref, f32[1,4096]{1,0:T(1,128)} %bitcast.72, f32[1,2048]{1,0:T(1,128)} %bitcast.69), custom_call_target="tpu_custom_call" | custom-call | tf_op jit(solution)/shard_map/pallas_call | solution.py:42
  168.2 12.9 %all-gather.3 = f32[8,1,2048]{2,1,0:T(1,128)S(1)} all-gather(f32[1,1,2048]{2,1,0:T(1,128)} %bitcast.81), channel_id=1, replica_groups=mesh['row'=8,'col'=16] {'row'}, dimensions={0}, use_global_device_ids=true | all-gather | bytes 73728 | tf_op jit(solution)/shard_map/all_gather | solution.py:104
  181.9 13.6 %shard_map.63 = f32[1,4096]{1,0:T(1,128)} custom-call(bf16[4096,128]{1,0:T(8,128)(2,1)} %all-gather.8.cloned.1.call-done.p_ref.q_ref.x_ref, bf16[2048,128]{1,0:T(8,128)(2,1)} %bitcast.60, f32[1,2048]{1,0:T(1,128)} %bitcast.78, f32[1,4096]{1,0:T(1,128)} %bitcast.65), custom_call_target="tpu_custom_call" | custom-call | tf_op jit(solution)/shard_map/pallas_call | solution.py:42
  195.4 22.6 %all-gather.4 = f32[16,1,4096]{2,1,0:T(1,128)S(1)} all-gather(f32[1,1,4096]{2,1,0:T(1,128)} %bitcast.73), channel_id=1, replica_groups=mesh['row'=8,'col'=16] {'col'}, dimensions={0}, use_global_device_ids=true | all-gather | bytes 278528 | tf_op jit(solution)/shard_map/all_gather | solution.py:104
  218.4 0.6 subtract_multiply_fusion
  219.1 13.8 %shard_map.64 = f32[1,2048]{1,0:T(1,128)} custom-call(bf16[2048,128]{1,0:T(8,128)(2,1)} %bitcast.61, bf16[4096,128]{1,0:T(8,128)(2,1)} %all-gather.8.cloned.1.call-done.p_ref.q_ref.x_ref, f32[1,4096]{1,0:T(1,128)} %bitcast.66, f32[1,2048]{1,0:T(1,128)} %bitcast.70), custom_call_target="tpu_custom_call" | custom-call | tf_op jit(solution)/shard_map/pallas_call | solution.py:42
  232.8 12.9 %all-gather.5 = f32[8,1,2048]{2,1,0:T(1,128)S(1)} all-gather(f32[1,1,2048]{2,1,0:T(1,128)} %bitcast.82), channel_id=1, replica_groups=mesh['row'=8,'col'=16] {'row'}, dimensions={0}, use_global_device_ids=true | all-gather | bytes 73728 | tf_op jit(solution)/shard_map/all_gather | solution.py:104
  246.5 20.4 %shard_map.65 = (f32[4096,128]{1,0:T(8,128)}, f32[2048,128]{1,0:T(8,128)}, f32[1,2048]{1,0:T(1,128)}) custom-call(bf16[4096,128]{1,0:T(8,128)(2,1)} %all-gather.8.cloned.1.call-done.p_ref.q_ref.x_ref, bf16[2048,128]{1,0:T(8,128)(2,1)} %bitcast.62, f32[1,4096]{1,0:T(1,128)} %bitcast.67, f32[1,2048]{1,0:T(1,128)} %bitcast.76), custom_call_target="tpu_custom_call" | custom-call | tf_op jit(solution)/shard_map/pallas_call | solution.py:76
  266.9 2.5 fusion.2
  269.5 0.7 reduce-scatter.3.cloned.1.call-update
  270.2 28.3 %reduce-scatter.5.cloned.1.call-done = f32[256,128]{1,0:T(8,128)} async-done(((f32[2048,128]{1,0:T(8,128)}), f32[256,128]{1,0:T(8,128)}) %reduce-scatter.5.cloned.1.call-update) | async-done | bytes 131088 | tf_op jit(solution)/shard_map/reduce_scatter | solution.py:134
  298.4 80.1 %reduce-scatter.3.cloned.1.call-done = f32[256,128]{1,0:T(8,128)} async-done(((f32[4096,128]{1,0:T(8,128)}), f32[256,128]{1,0:T(8,128)}) %reduce-scatter.3.cloned.1.call-update) | async-done | bytes 131088 | tf_op jit(solution)/shard_map/reduce_scatter | solution.py:133
  (30 shorter events, 4.9 us)
Async XLA Ops:
  7.2 44.9 %all-gather.8.cloned.1.call-start = ((), (), s32[]{:S(2)}) async-start(), calls=%async_computation.2 | async-start | bytes 1114112 | tf_op jit(solution)/shard_map/all_gather | solution.py:110
  7.9 290.6 %reduce-scatter.5.cloned.1.call-start = ((), (), s32[]{:S(2)}) async-start(), calls=%async_computation.4 | async-start | bytes 1179648 | tf_op jit(solution)/shard_map/reduce_scatter | solution.py:134
  20.1 34.4 %copy-start = (bf16[1,2048,128]{2,1,0:T(8,128)(2,1)}, bf16[1,2048,128]{2,1,0:T(8,128)(2,1)S(1)}, u32[]{:S(2)}) copy-start(bf16[1,2048,128]{2,1,0:T(8,128)(2,1)S(1)} %all_gather.25) | copy-start | bytes 1572868
  20.1 70.8 %copy-start.2 = (f32[4096]{0:T(1024)S(1)}, f32[4096]{0:T(1024)}, u32[]{:S(2)}) copy-start(f32[4096]{0:T(1024)} %param.6) | copy-start | bytes 49156
  54.5 62.6 %copy-start.3 = (f32[2048]{0:T(1024)S(1)}, f32[2048]{0:T(1024)}, u32[]{:S(2)}) copy-start(f32[2048]{0:T(1024)} %param.7) | copy-start | bytes 24580
  218.0 48.8 %copy-start.1 = (bf16[1,2048,128]{2,1,0:T(8,128)(2,1)S(1)}, bf16[1,2048,128]{2,1,0:T(8,128)(2,1)}, u32[]{:S(2)}) copy-start(bf16[1,2048,128]{2,1,0:T(8,128)(2,1)} %copy-done) | copy-start | bytes 1572868
  269.4 109.1 %reduce-scatter.3.cloned.1.call-start = ((), (), s32[]{:S(2)}) async-start(), calls=%async_computation.3 | async-start | bytes 2228224 | tf_op jit(solution)/shard_map/reduce_scatter | solution.py:133
Sparse Core Ops, SparseCore 0:
  10.1 41.8 all-gather.7
  269.5 28.8 reduce-scatter.4
  302.3 76.2 reduce-scatter.2

commit v4 on v3

--- a/solution.py
+++ b/solution.py
@@ -1,3 +1,5 @@
+import functools
+
 import jax
 import jax.numpy as jnp
 from jax import lax
@@ -100,10 +102,56 @@
     return jnp.sum(jnp.square(values.astype(jnp.float32)), axis=1)
 
 
+def _peer(axis, k):
+    if axis == "col":
+        return (lax.axis_index("row"), k)
+    return (k, lax.axis_index("col"))
+
+
+def _gather_lse_kernel(axis, n, x_ref, o_ref, buf, send, recv):
+    me = lax.axis_index(axis)
+    barrier = pltpu.get_barrier_semaphore()
+    for d in range(1, n):
+        pl.semaphore_signal(barrier, inc=1, device_id=_peer(axis, lax.rem(me + d, n)),
+                            device_id_type=pl.DeviceIdType.MESH)
+    pl.semaphore_wait(barrier, n - 1)
+    copies = []
+    for d in range(1, n):
+        copy = pltpu.make_async_remote_copy(
+            src_ref=x_ref, dst_ref=buf.at[me], send_sem=send.at[d], recv_sem=recv.at[me],
+            device_id=_peer(axis, lax.rem(me + d, n)), device_id_type=pl.DeviceIdType.MESH)
+        copy.start()
+        copies.append(copy)
+    for copy in copies:
+        copy.wait_send()
+    for d in range(1, n):
+        src = lax.rem(me + n - d, n)
+        pltpu.make_async_remote_copy(
+            src_ref=x_ref, dst_ref=buf.at[src], send_sem=send.at[d], recv_sem=recv.at[src],
+            device_id=_peer(axis, src), device_id_type=pl.DeviceIdType.MESH).wait_recv()
+    buf[me] = x_ref[...]
+    parts = buf[...]
+    top = jnp.max(parts, axis=0)
+    o_ref[...] = top + jnp.log(jnp.sum(jnp.exp(parts - top[None]), axis=0))
+
+
 def combine(part, axis):
-    parts = lax.all_gather(part, axis, axis=0)
-    top = jnp.max(parts, axis=0)
-    return top + jnp.log(jnp.sum(jnp.exp(parts - top[None, :]), axis=0))
+    n = lax.axis_size(axis)
+    block = part.reshape(8, part.shape[0] // 8)
+    out = pl.pallas_call(
+        functools.partial(_gather_lse_kernel, axis, n),
+        out_shape=jax.ShapeDtypeStruct(block.shape, jnp.float32),
+        in_specs=[pl.BlockSpec(memory_space=pltpu.VMEM)],
+        out_specs=pl.BlockSpec(memory_space=pltpu.VMEM),
+        scratch_shapes=[
+            pltpu.VMEM((n,) + block.shape, jnp.float32),
+            pltpu.SemaphoreType.DMA((n,)),
+            pltpu.SemaphoreType.DMA((n,)),
+        ],
+        compiler_params=pltpu.CompilerParams(
+            collective_id=0 if axis == "col" else 1, has_side_effects=True),
+    )(block)
+    return out.reshape(part.shape)
 
 
 def local(imu, camera, imu_mass, cam_mass):

time: 389 us -> 354 us (0.910)
  blocking collectives: 117 us -> 12.1 us
  Pallas kernels: 102 us -> 156 us
  other arithmetic: 11 us -> 22.5 us
  local copies, waits for them, and re-layouts: 0.01 us -> 4.29 us
    all_gather x6 -> x0, blocking collectives: 105 us -> none  [combine(): parts = lax.all_gather(part, axis, axis=0)]
    pallas_call x0 -> x6, Pallas kernels: none -> 53.3 us  [combine(): pl.pallas_call(functools.partial(_gather_lse_kernel, axis, n), out_shape=...]
    pallas_call x0 -> x6, other arithmetic: none -> 8.62 us  [lse(): pl.pallas_call(_lse_kernel, out_shape=jax.ShapeDtypeStruct((1, rows), jnp...]
    unnamed x0 -> x6, other arithmetic: none -> 4.26 us
where the time goes in v4:
time: 354 us; the launch traced here: 348 us
  Pallas kernels  156 us (44%)
  waiting for transfers between devices  140 us (40%)
  other arithmetic  22.5 us (6%)
  between operations  13.9 us (4%)
  blocking collectives  12.1 us (3%)
  local copies, waits for them, and re-layouts  4.29 us (1%)
    pallas_call x6, Pallas kernels, lse(): pl.pallas_call(_lse_kernel, out_shape=jax.ShapeDtypeStruct((1, rows), jnp...  82 us
    reduce_scatter x1, waiting for transfers between devices, local(): lax.psum_scatter(grad_rows, 'col', scatter_dimension=0, tiled=True)  80.3 us
    pallas_call x6, Pallas kernels, combine(): pl.pallas_call(functools.partial(_gather_lse_kernel, axis, n), out_shape=...  53.3 us
    all_gather x1, waiting for transfers between devices, local(): imu_rows = lax.all_gather(imu, 'col', axis=0, tiled=True)  31 us
    reduce_scatter x1, waiting for transfers between devices, local(): lax.psum_scatter(grad_cols, 'row', scatter_dimension=0, tiled=True)  27.3 us
    pallas_call x1, Pallas kernels, plan_grads(): pl.pallas_call(_plan_kernel, out_shape=(jax.ShapeDtypeStruct((rows, D), j...  20.4 us
    all_gather x1, blocking collectives, local(): cam_rows = lax.all_gather(camera, 'row', axis=1, tiled=True)[0]  12.1 us
    pallas_call x6, other arithmetic, lse(): pl.pallas_call(_lse_kernel, out_shape=jax.ShapeDtypeStruct((1, rows), jnp...  8.62 us
  transfers between devices with their start and end apart: 3, of which 3 were waited for; matrix products, arithmetic and copies ran while one was open for 0% of the time, Pallas kernels for 0%

profile of v4, /device:TPU:116, one launch (start us, length us, event | category | flops | bytes accessed | tf_op | source)
XLA Modules:
  0.0 348.5 jit_solution(8096386390930079257)
XLA Ops:
  8.0 12.1 %all_gather.7 = bf16[1,2048,128]{2,1,0:T(8,128)(2,1)S(1)} all-gather(bf16[1,256,128]{2,1,0:T(8,128)(2,1)} %param.5), channel_id=1, replica_groups=mesh['row'=8,'col'=16] {'row'}, dimensions={1}, use_global_device_ids=true | all-gather | bytes 589824 | tf_op jit(solution)/shard_map/all_gather | solution.py:159
  21.0 31.0 %all-gather.2.cloned.1.call-done.p_ref.q_ref.x_ref = bf16[4096,128]{1,0:T(8,128)(2,1)} async-done(((bf16[256,128]{1,0:T(8,128)(2,1)}), bf16[4096,128]{1,0:T(8,128)(2,1)}) %all-gather.2.cloned.1.call-update) | async-done | bytes 1048592 | tf_op jit(solution)/shard_map/all_gather | solution.py:158
  52.0 1.8 multiply_reduce_fusion
  54.5 13.6 %shard_map.59 = f32[1,4096]{1,0:T(1,128)} custom-call(bf16[4096,128]{1,0:T(8,128)(2,1)} %all-gather.2.cloned.1.call-done.p_ref.q_ref.x_ref, bf16[2048,128]{1,0:T(8,128)(2,1)} %bitcast.32, f32[1,2048]{1,0:T(1,128)} %bitcast.52, f32[1,4096]{1,0:T(1,128)} %bitcast.39), custom_call_target="tpu_custom_call" | custom-call | tf_op jit(solution)/shard_map/pallas_call | solution.py:44
  68.7 1.4 reduce.18
  70.7 10.7 %shard_map.60 = f32[8,512]{1,0:T(8,128)} custom-call(f32[8,512]{1,0:T(8,128)} %reshape_squeeze.18.x_ref), custom_call_target="tpu_custom_call" | custom-call | tf_op jit(solution)/shard_map/pallas_call | solution.py:141
  82.8 13.8 %shard_map.61 = f32[1,2048]{1,0:T(1,128)} custom-call(bf16[2048,128]{1,0:T(8,128)(2,1)} %bitcast.33, bf16[4096,128]{1,0:T(8,128)(2,1)} %all-gather.2.cloned.1.call-done.p_ref.q_ref.x_ref, f32[1,4096]{1,0:T(1,128)} %bitcast.47, f32[1,2048]{1,0:T(1,128)} %bitcast.44), custom_call_target="tpu_custom_call" | custom-call | tf_op jit(solution)/shard_map/pallas_call | solution.py:44
  96.5 1.4 reduce.19
  98.6 6.8 %shard_map.62 = f32[8,256]{1,0:T(8,128)} custom-call(f32[8,256]{1,0:T(8,128)} %reshape_squeeze.19.x_ref), custom_call_target="tpu_custom_call" | custom-call | tf_op jit(solution)/shard_map/pallas_call | solution.py:141
  106.7 13.6 %shard_map.63 = f32[1,4096]{1,0:T(1,128)} custom-call(bf16[4096,128]{1,0:T(8,128)(2,1)} %all-gather.2.cloned.1.call-done.p_ref.q_ref.x_ref, bf16[2048,128]{1,0:T(8,128)(2,1)} %bitcast.34, f32[1,2048]{1,0:T(1,128)} %bitcast.55, f32[1,4096]{1,0:T(1,128)} %bitcast.40), custom_call_target="tpu_custom_call" | custom-call | tf_op jit(solution)/shard_map/pallas_call | solution.py:44
  120.3 1.4 reduce.20
  122.3 11.1 %shard_map.64 = f32[8,512]{1,0:T(8,128)} custom-call(f32[8,512]{1,0:T(8,128)} %reshape_squeeze.20.x_ref), custom_call_target="tpu_custom_call" | custom-call | tf_op jit(solution)/shard_map/pallas_call | solution.py:141
  134.8 13.8 %shard_map.65 = f32[1,2048]{1,0:T(1,128)} custom-call(bf16[2048,128]{1,0:T(8,128)(2,1)} %bitcast.35, bf16[4096,128]{1,0:T(8,128)(2,1)} %all-gather.2.cloned.1.call-done.p_ref.q_ref.x_ref, f32[1,4096]{1,0:T(1,128)} %bitcast.48, f32[1,2048]{1,0:T(1,128)} %bitcast.45), custom_call_target="tpu_custom_call" | custom-call | tf_op jit(solution)/shard_map/pallas_call | solution.py:44
  148.6 1.4 reduce.21
  150.6 6.8 %shard_map.66 = f32[8,256]{1,0:T(8,128)} custom-call(f32[8,256]{1,0:T(8,128)} %reshape_squeeze.21.x_ref), custom_call_target="tpu_custom_call" | custom-call | tf_op jit(solution)/shard_map/pallas_call | solution.py:141
  158.7 13.6 %shard_map.67 = f32[1,4096]{1,0:T(1,128)} custom-call(bf16[4096,128]{1,0:T(8,128)(2,1)} %all-gather.2.cloned.1.call-done.p_ref.q_ref.x_ref, bf16[2048,128]{1,0:T(8,128)(2,1)} %bitcast.36, f32[1,2048]{1,0:T(1,128)} %bitcast.54, f32[1,4096]{1,0:T(1,128)} %bitcast.41), custom_call_target="tpu_custom_call" | custom-call | tf_op jit(solution)/shard_map/pallas_call | solution.py:44
  172.3 1.5 reduce.22
  174.4 11.1 %shard_map.68 = f32[8,512]{1,0:T(8,128)} custom-call(f32[8,512]{1,0:T(8,128)} %reshape_squeeze.22.x_ref), custom_call_target="tpu_custom_call" | custom-call | tf_op jit(solution)/shard_map/pallas_call | solution.py:141
  186.9 13.7 %shard_map.69 = f32[1,2048]{1,0:T(1,128)} custom-call(bf16[2048,128]{1,0:T(8,128)(2,1)} %bitcast.37, bf16[4096,128]{1,0:T(8,128)(2,1)} %all-gather.2.cloned.1.call-done.p_ref.q_ref.x_ref, f32[1,4096]{1,0:T(1,128)} %bitcast.42, f32[1,2048]{1,0:T(1,128)} %bitcast.46), custom_call_target="tpu_custom_call" | custom-call | tf_op jit(solution)/shard_map/pallas_call | solution.py:44
  202.6 6.8 %shard_map.70 = f32[8,256]{1,0:T(8,128)} custom-call(f32[8,256]{1,0:T(8,128)} %reshape_squeeze.23.x_ref), custom_call_target="tpu_custom_call" | custom-call | tf_op jit(solution)/shard_map/pallas_call | solution.py:141
  210.7 20.4 %shard_map.71 = (f32[4096,128]{1,0:T(8,128)}, f32[2048,128]{1,0:T(8,128)}, f32[1,2048]{1,0:T(1,128)}) custom-call(bf16[4096,128]{1,0:T(8,128)(2,1)} %all-gather.2.cloned.1.call-done.p_ref.q_ref.x_ref, bf16[2048,128]{1,0:T(8,128)(2,1)} %bitcast.38, f32[1,4096]{1,0:T(1,128)} %bitcast.43, f32[1,2048]{1,0:T(1,128)} %bitcast.53), custom_call_target="tpu_custom_call" | custom-call | tf_op jit(solution)/shard_map/pallas_call | solution.py:78
  231.1 2.5 fusion.2
  234.4 27.3 %reduce-scatter.5.cloned.1.call-done = f32[256,128]{1,0:T(8,128)} async-done(((f32[2048,128]{1,0:T(8,128)}), f32[256,128]{1,0:T(8,128)}) %reduce-scatter.5.cloned.1.call-update) | async-done | bytes 131088 | tf_op jit(solution)/shard_map/reduce_scatter | solution.py:182
  261.7 80.3 %reduce-scatter.3.cloned.1.call-done = f32[256,128]{1,0:T(8,128)} async-done(((f32[4096,128]{1,0:T(8,128)}), f32[256,128]{1,0:T(8,128)}) %reduce-scatter.3.cloned.1.call-update) | async-done | bytes 131088 | tf_op jit(solution)/shard_map/reduce_scatter | solution.py:181
  (43 shorter events, 16.7 us)
Async XLA Ops:
  7.2 75.0 %copy-start.2 = (f32[4096]{0:T(1024)S(1)}, f32[4096]{0:T(1024)}, u32[]{:S(2)}) copy-start(f32[4096]{0:T(1024)} %param.6) | copy-start | bytes 49156
  7.2 44.9 %all-gather.2.cloned.1.call-start = ((), (), s32[]{:S(2)}) async-start(), calls=%async_computation.2 | async-start | bytes 1114112 | tf_op jit(solution)/shard_map/all_gather | solution.py:158
  7.9 253.8 %reduce-scatter.5.cloned.1.call-start = ((), (), s32[]{:S(2)}) async-start(), calls=%async_computation.4 | async-start | bytes 1179648 | tf_op jit(solution)/shard_map/reduce_scatter | solution.py:182
  20.1 34.4 %copy-start = (bf16[1,2048,128]{2,1,0:T(8,128)(2,1)}, bf16[1,2048,128]{2,1,0:T(8,128)(2,1)S(1)}, u32[]{:S(2)}) copy-start(bf16[1,2048,128]{2,1,0:T(8,128)(2,1)S(1)} %all_gather.7) | copy-start | bytes 1572868
  21.0 85.1 %copy-start.3 = (f32[2048]{0:T(1024)S(1)}, f32[2048]{0:T(1024)}, u32[]{:S(2)}) copy-start(f32[2048]{0:T(1024)} %param.7) | copy-start | bytes 24580
  172.3 58.8 %copy-start.1 = (bf16[1,2048,128]{2,1,0:T(8,128)(2,1)S(1)}, bf16[1,2048,128]{2,1,0:T(8,128)(2,1)}, u32[]{:S(2)}) copy-start(bf16[1,2048,128]{2,1,0:T(8,128)(2,1)} %copy-done) | copy-start | bytes 1572868
  233.7 108.3 %reduce-scatter.3.cloned.1.call-start = ((), (), s32[]{:S(2)}) async-start(), calls=%async_computation.3 | async-start | bytes 2228224 | tf_op jit(solution)/shard_map/reduce_scatter | solution.py:181
Sparse Core Ops, SparseCore 0:
  10.1 41.8 all-gather.1
  233.8 27.8 reduce-scatter.4
  265.5 76.3 reduce-scatter.2

commit v5 on v4

--- a/solution.py
+++ b/solution.py
@@ -135,6 +135,65 @@
     o_ref[...] = top + jnp.log(jnp.sum(jnp.exp(parts - top[None]), axis=0))
 
 
+def _exchange_kernel(jobs, *refs):
+    count = len(jobs)
+    ins, outs = refs[:count], refs[count:2 * count]
+    bufs, sends, recvs = refs[2 * count::3], refs[2 * count + 1::3], refs[2 * count + 2::3]
+    barrier = pltpu.get_barrier_semaphore()
+    for axis, n, kind in jobs:
+        me = lax.axis_index(axis)
+        for d in range(1, n):
+            pl.semaphore_signal(barrier, inc=1, device_id=_peer(axis, lax.rem(me + d, n)),
+                                device_id_type=pl.DeviceIdType.MESH)
+    pl.semaphore_wait(barrier, sum(n - 1 for _, n, _ in jobs))
+
+    def copy(job, d, peer, slot):
+        axis, n, kind = jobs[job]
+        src = ins[job] if kind == "gather" else ins[job].at[peer]
+        return pltpu.make_async_remote_copy(
+            src_ref=src, dst_ref=bufs[job].at[slot], send_sem=sends[job].at[d],
+            recv_sem=recvs[job].at[slot], device_id=_peer(axis, peer),
+            device_id_type=pl.DeviceIdType.MESH)
+
+    started = []
+    for job, (axis, n, kind) in enumerate(jobs):
+        me = lax.axis_index(axis)
+        for d in range(1, n):
+            started.append(copy(job, d, lax.rem(me + d, n), me))
+            started[-1].start()
+    for c in started:
+        c.wait_send()
+    for job, (axis, n, kind) in enumerate(jobs):
+        me = lax.axis_index(axis)
+        for d in range(1, n):
+            src = lax.rem(me + n - d, n)
+            copy(job, d, src, src).wait_recv()
+        if kind == "gather":
+            bufs[job][me] = ins[job][...]
+            outs[job][...] = bufs[job][...]
+        else:
+            bufs[job][me] = ins[job][me]
+            outs[job][...] = jnp.sum(bufs[job][...], axis=0)
+
+
+def exchange(jobs, arrays, collective_id):
+    shapes, scratch = [], []
+    for (axis, n, kind), x in zip(jobs, arrays):
+        block = x.shape if kind == "gather" else x.shape[1:]
+        shapes.append(jax.ShapeDtypeStruct((n,) + block if kind == "gather" else block, x.dtype))
+        scratch += [pltpu.VMEM((n,) + block, x.dtype), pltpu.SemaphoreType.DMA((n,)),
+                    pltpu.SemaphoreType.DMA((n,))]
+    return pl.pallas_call(
+        functools.partial(_exchange_kernel, tuple(jobs)),
+        out_shape=tuple(shapes),
+        in_specs=[pl.BlockSpec(memory_space=pltpu.VMEM)] * len(jobs),
+        out_specs=tuple(pl.BlockSpec(memory_space=pltpu.VMEM) for _ in jobs),
+        scratch_shapes=scratch,
+        compiler_params=pltpu.CompilerParams(
+            collective_id=collective_id, has_side_effects=True, vmem_limit_bytes=VMEM_LIMIT),
+    )(*arrays)
+
+
 def combine(part, axis):
     n = lax.axis_size(axis)
     block = part.reshape(8, part.shape[0] // 8)
@@ -178,8 +237,10 @@
     u = ((f - rows_sq) * INV)[None, :]
     grad_rows, pulled_cam, col_total = plan_grads(imu_rows, cam_rows, u, a)
     grad_cols = 2.0 * (col_total[0][:, None] * cam_rows.astype(jnp.float32) - pulled_cam)
-    grad_imu = lax.psum_scatter(grad_rows, "col", scatter_dimension=0, tiled=True)
-    grad_cam = lax.psum_scatter(grad_cols, "row", scatter_dimension=0, tiled=True)
+    n_col, n_row = lax.axis_size("col"), lax.axis_size("row")
+    grad_imu, grad_cam = exchange(
+        [("col", n_col, "scatter"), ("row", n_row, "scatter")],
+        [grad_rows.reshape(n_col, -1, D), grad_cols.reshape(n_row, -1, D)], 2)
     return (grad_imu, grad_cam[None])
 
 

time: 354 us -> 295 us (0.83)
  waiting for transfers between devices: 140 us -> 31.7 us
  Pallas kernels: 156 us -> 203 us
    reduce_scatter x2 -> x0, waiting for transfers between devices: 108 us -> none  [the longest x1 80.3 us: local(): lax.psum_scatter(grad_rows, 'col', scatter_dimension=0, tiled=True)]
    pallas_call x0 -> x1, Pallas kernels: none -> 47.6 us  [exchange(): pl.pallas_call(functools.partial(_exchange_kernel, tuple(jobs)), out_shap...]
  transfers between devices with their start and end apart: 3 -> 1, of which waited for: 3 -> 1; matrix products, arithmetic and copies ran while one was open for 0% -> 0% of each run, Pallas kernels for 0% -> 0%
where the time goes in v5:
time: 295 us; the launch traced here: 291 us
  Pallas kernels  203 us (69%)
  waiting for transfers between devices  31.7 us (11%)
  other arithmetic  22.5 us (8%)
  between operations  14.1 us (5%)
  blocking collectives  12.1 us (4%)
  local copies, waits for them, and re-layouts  7.42 us (3%)
    pallas_call x6, Pallas kernels, lse(): pl.pallas_call(_lse_kernel, out_shape=jax.ShapeDtypeStruct((1, rows), jnp...  82 us
    pallas_call x6, Pallas kernels, combine(): pl.pallas_call(functools.partial(_gather_lse_kernel, axis, n), out_shape=...  53.3 us
    pallas_call x1, Pallas kernels, exchange(): pl.pallas_call(functools.partial(_exchange_kernel, tuple(jobs)), out_shap...  47.6 us
    all_gather x1, waiting for transfers between devices, local(): imu_rows = lax.all_gather(imu, 'col', axis=0, tiled=True)  31.1 us
    pallas_call x1, Pallas kernels, plan_grads(): pl.pallas_call(_plan_kernel, out_shape=(jax.ShapeDtypeStruct((rows, D), j...  20.4 us
    all_gather x1, blocking collectives, local(): cam_rows = lax.all_gather(camera, 'row', axis=1, tiled=True)[0]  12.1 us
    pallas_call x6, other arithmetic, lse(): pl.pallas_call(_lse_kernel, out_shape=jax.ShapeDtypeStruct((1, rows), jnp...  8.62 us
  transfers between devices with their start and end apart: 1, of which 1 were waited for; matrix products, arithmetic and copies ran while one was open for 0% of the time, Pallas kernels for 0%

profile of v5, /device:TPU:116, one launch (start us, length us, event | category | flops | bytes accessed | tf_op | source)
XLA Modules:
  0.0 291.2 jit_solution(16246411072319965348)
XLA Ops:
  7.9 12.1 %all_gather.7 = bf16[1,2048,128]{2,1,0:T(8,128)(2,1)S(1)} all-gather(bf16[1,256,128]{2,1,0:T(8,128)(2,1)} %param.5), channel_id=1, replica_groups=mesh['row'=8,'col'=16] {'row'}, dimensions={1}, use_global_device_ids=true | all-gather | bytes 589824 | tf_op jit(solution)/shard_map/all_gather | solution.py:218
  21.0 31.1 %all-gather.2.cloned.1.call-done.p_ref.q_ref.x_ref = bf16[4096,128]{1,0:T(8,128)(2,1)} async-done(((bf16[256,128]{1,0:T(8,128)(2,1)}), bf16[4096,128]{1,0:T(8,128)(2,1)}) %all-gather.2.cloned.1.call-update) | async-done | bytes 1048592 | tf_op jit(solution)/shard_map/all_gather | solution.py:217
  52.0 1.8 multiply_reduce_fusion
  54.5 13.6 %shard_map.59 = f32[1,4096]{1,0:T(1,128)} custom-call(bf16[4096,128]{1,0:T(8,128)(2,1)} %all-gather.2.cloned.1.call-done.p_ref.q_ref.x_ref, bf16[2048,128]{1,0:T(8,128)(2,1)} %bitcast.34, f32[1,2048]{1,0:T(1,128)} %bitcast.57, f32[1,4096]{1,0:T(1,128)} %bitcast.43), custom_call_target="tpu_custom_call" | custom-call | tf_op jit(solution)/shard_map/pallas_call | solution.py:44
  68.7 1.4 reduce.18
  70.7 10.7 %shard_map.60 = f32[8,512]{1,0:T(8,128)} custom-call(f32[8,512]{1,0:T(8,128)} %reshape_squeeze.18.x_ref), custom_call_target="tpu_custom_call" | custom-call | tf_op jit(solution)/shard_map/pallas_call | solution.py:200
  82.8 13.8 %shard_map.61 = f32[1,2048]{1,0:T(1,128)} custom-call(bf16[2048,128]{1,0:T(8,128)(2,1)} %bitcast.35, bf16[4096,128]{1,0:T(8,128)(2,1)} %all-gather.2.cloned.1.call-done.p_ref.q_ref.x_ref, f32[1,4096]{1,0:T(1,128)} %bitcast.52, f32[1,2048]{1,0:T(1,128)} %bitcast.48), custom_call_target="tpu_custom_call" | custom-call | tf_op jit(solution)/shard_map/pallas_call | solution.py:44
  96.5 1.4 reduce.19
  98.6 6.8 %shard_map.62 = f32[8,256]{1,0:T(8,128)} custom-call(f32[8,256]{1,0:T(8,128)} %reshape_squeeze.19.x_ref), custom_call_target="tpu_custom_call" | custom-call | tf_op jit(solution)/shard_map/pallas_call | solution.py:200
  106.7 13.6 %shard_map.63 = f32[1,4096]{1,0:T(1,128)} custom-call(bf16[4096,128]{1,0:T(8,128)(2,1)} %all-gather.2.cloned.1.call-done.p_ref.q_ref.x_ref, bf16[2048,128]{1,0:T(8,128)(2,1)} %bitcast.36, f32[1,2048]{1,0:T(1,128)} %bitcast.60, f32[1,4096]{1,0:T(1,128)} %bitcast.44), custom_call_target="tpu_custom_call" | custom-call | tf_op jit(solution)/shard_map/pallas_call | solution.py:44
  120.3 1.4 reduce.20
  122.3 11.1 %shard_map.64 = f32[8,512]{1,0:T(8,128)} custom-call(f32[8,512]{1,0:T(8,128)} %reshape_squeeze.20.x_ref), custom_call_target="tpu_custom_call" | custom-call | tf_op jit(solution)/shard_map/pallas_call | solution.py:200
  134.8 13.8 %shard_map.65 = f32[1,2048]{1,0:T(1,128)} custom-call(bf16[2048,128]{1,0:T(8,128)(2,1)} %bitcast.37, bf16[4096,128]{1,0:T(8,128)(2,1)} %all-gather.2.cloned.1.call-done.p_ref.q_ref.x_ref, f32[1,4096]{1,0:T(1,128)} %bitcast.53, f32[1,2048]{1,0:T(1,128)} %bitcast.49), custom_call_target="tpu_custom_call" | custom-call | tf_op jit(solution)/shard_map/pallas_call | solution.py:44
  150.6 6.8 %shard_map.66 = f32[8,256]{1,0:T(8,128)} custom-call(f32[8,256]{1,0:T(8,128)} %reshape_squeeze.21.x_ref), custom_call_target="tpu_custom_call" | custom-call | tf_op jit(solution)/shard_map/pallas_call | solution.py:200
  158.7 13.6 %shard_map.67 = f32[1,4096]{1,0:T(1,128)} custom-call(bf16[4096,128]{1,0:T(8,128)(2,1)} %all-gather.2.cloned.1.call-done.p_ref.q_ref.x_ref, bf16[2048,128]{1,0:T(8,128)(2,1)} %bitcast.38, f32[1,2048]{1,0:T(1,128)} %bitcast.59, f32[1,4096]{1,0:T(1,128)} %bitcast.45), custom_call_target="tpu_custom_call" | custom-call | tf_op jit(solution)/shard_map/pallas_call | solution.py:44
  172.3 1.5 reduce.22
  174.4 11.1 %shard_map.68 = f32[8,512]{1,0:T(8,128)} custom-call(f32[8,512]{1,0:T(8,128)} %reshape_squeeze.22.x_ref), custom_call_target="tpu_custom_call" | custom-call | tf_op jit(solution)/shard_map/pallas_call | solution.py:200
  186.9 13.7 %shard_map.69 = f32[1,2048]{1,0:T(1,128)} custom-call(bf16[2048,128]{1,0:T(8,128)(2,1)} %bitcast.39, bf16[4096,128]{1,0:T(8,128)(2,1)} %all-gather.2.cloned.1.call-done.p_ref.q_ref.x_ref, f32[1,4096]{1,0:T(1,128)} %bitcast.46, f32[1,2048]{1,0:T(1,128)} %bitcast.50), custom_call_target="tpu_custom_call" | custom-call | tf_op jit(solution)/shard_map/pallas_call | solution.py:44
  202.6 6.8 %shard_map.70 = f32[8,256]{1,0:T(8,128)} custom-call(f32[8,256]{1,0:T(8,128)} %reshape_squeeze.23.x_ref), custom_call_target="tpu_custom_call" | custom-call | tf_op jit(solution)/shard_map/pallas_call | solution.py:200
  210.7 20.4 %shard_map.71 = (f32[4096,128]{1,0:T(8,128)}, f32[2048,128]{1,0:T(8,128)}, f32[1,2048]{1,0:T(1,128)}) custom-call(bf16[4096,128]{1,0:T(8,128)(2,1)} %all-gather.2.cloned.1.call-done.p_ref.q_ref.x_ref, bf16[2048,128]{1,0:T(8,128)(2,1)} %bitcast.40, f32[1,4096]{1,0:T(1,128)} %bitcast.47, f32[1,2048]{1,0:T(1,128)} %bitcast.58), custom_call_target="tpu_custom_call" | custom-call | tf_op jit(solution)/shard_map/pallas_call | solution.py:78
  231.1 2.5 fusion.2
  233.7 47.6 %shard_map.72 = (f32[256,128]{1,0:T(8,128)}, f32[256,128]{1,0:T(8,128)}) custom-call(f32[16,256,128]{2,1,0:T(8,128)} %bitcast.42, f32[8,256,128]{2,1,0:T(8,128)} %bitcast.41), custom_call_target="tpu_custom_call" | custom-call | tf_op jit(solution)/shard_map/pallas_call | solution.py:186
  281.2 1.6 copy.14
  282.8 1.6 copy.15
  (40 shorter events, 17.3 us)
Async XLA Ops:
  7.2 75.0 %copy-start.2 = (f32[4096]{0:T(1024)S(1)}, f32[4096]{0:T(1024)}, u32[]{:S(2)}) copy-start(f32[4096]{0:T(1024)} %param.6) | copy-start | bytes 49156
  7.2 44.9 %all-gather.2.cloned.1.call-start = ((), (), s32[]{:S(2)}) async-start(), calls=%async_computation | async-start | bytes 1114112 | tf_op jit(solution)/shard_map/all_gather | solution.py:217
  20.0 34.5 %copy-start = (bf16[1,2048,128]{2,1,0:T(8,128)(2,1)}, bf16[1,2048,128]{2,1,0:T(8,128)(2,1)S(1)}, u32[]{:S(2)}) copy-start(bf16[1,2048,128]{2,1,0:T(8,128)(2,1)S(1)} %all_gather.7) | copy-start | bytes 1572868
  21.0 85.1 %copy-start.3 = (f32[2048]{0:T(1024)S(1)}, f32[2048]{0:T(1024)}, u32[]{:S(2)}) copy-start(f32[2048]{0:T(1024)} %param.7) | copy-start | bytes 24580
  172.3 58.8 %copy-start.1 = (bf16[1,2048,128]{2,1,0:T(8,128)(2,1)S(1)}, bf16[1,2048,128]{2,1,0:T(8,128)(2,1)}, u32[]{:S(2)}) copy-start(bf16[1,2048,128]{2,1,0:T(8,128)(2,1)} %copy-done) | copy-start | bytes 1572868
Sparse Core Ops, SparseCore 0:
  10.1 41.8 all-gather.1

commit v6 on v5

--- a/solution.py
+++ b/solution.py
@@ -214,8 +214,11 @@
 
 
 def local(imu, camera, imu_mass, cam_mass):
-    imu_rows = lax.all_gather(imu, "col", axis=0, tiled=True)
-    cam_rows = lax.all_gather(camera, "row", axis=1, tiled=True)[0]
+    n_col, n_row = lax.axis_size("col"), lax.axis_size("row")
+    imu_rows, cam_rows = exchange(
+        [("col", n_col, "gather"), ("row", n_row, "gather")], [imu, camera[0]], 3)
+    imu_rows = imu_rows.reshape(-1, D)
+    cam_rows = cam_rows.reshape(-1, D)
     rows_sq = squares(imu_rows)
     cols_sq = squares(cam_rows)
     log_a = jnp.log(imu_mass)
@@ -237,7 +240,6 @@
     u = ((f - rows_sq) * INV)[None, :]
     grad_rows, pulled_cam, col_total = plan_grads(imu_rows, cam_rows, u, a)
     grad_cols = 2.0 * (col_total[0][:, None] * cam_rows.astype(jnp.float32) - pulled_cam)
-    n_col, n_row = lax.axis_size("col"), lax.axis_size("row")
     grad_imu, grad_cam = exchange(
         [("col", n_col, "scatter"), ("row", n_row, "scatter")],
         [grad_rows.reshape(n_col, -1, D), grad_cols.reshape(n_row, -1, D)], 2)

time: 295 us -> 262 us (0.89)
  waiting for transfers between devices: 31.7 us -> 0 us
  Pallas kernels: 203 us -> 227 us
  between operations: 14.1 us -> 0.79 us
  blocking collectives: 12.1 us -> 0 us
    all_gather x1 -> x0, waiting for transfers between devices: 31.1 us -> none  [local(): imu_rows = lax.all_gather(imu, 'col', axis=0, tiled=True)]
    pallas_call x1 -> x2, Pallas kernels: 47.6 us -> 71.4 us  [exchange(): pl.pallas_call(functools.partial(_exchange_kernel, tuple(jobs)), out_shap...]
    all_gather x1 -> x0, blocking collectives: 12.1 us -> none  [local(): cam_rows = lax.all_gather(camera, 'row', axis=1, tiled=True)[0]]
  transfers between devices with their start and end apart: 1 -> 0, of which waited for: 1 -> 0; matrix products, arithmetic and copies ran while one was open for 0% -> 0% of each run, Pallas kernels for 0% -> 0%
where the time goes in v6:
time: 262 us; the launch traced here: 259 us
  Pallas kernels  227 us (87%)
  other arithmetic  22.4 us (9%)
  local copies, waits for them, and re-layouts  9.27 us (4%)
    pallas_call x6, Pallas kernels, lse(): pl.pallas_call(_lse_kernel, out_shape=jax.ShapeDtypeStruct((1, rows), jnp...  82 us
    pallas_call x2, Pallas kernels, exchange(): pl.pallas_call(functools.partial(_exchange_kernel, tuple(jobs)), out_shap...  71.4 us
    pallas_call x6, Pallas kernels, combine(): pl.pallas_call(functools.partial(_gather_lse_kernel, axis, n), out_shape=...  53.4 us
    pallas_call x1, Pallas kernels, plan_grads(): pl.pallas_call(_plan_kernel, out_shape=(jax.ShapeDtypeStruct((rows, D), j...  20.4 us
    pallas_call x6, other arithmetic, lse(): pl.pallas_call(_lse_kernel, out_shape=jax.ShapeDtypeStruct((1, rows), jnp...  8.62 us

profile of v6, /device:TPU:116, one launch (start us, length us, event | category | flops | bytes accessed | tf_op | source)
XLA Modules:
  0.0 259.5 jit_solution(18335296496604549280)
XLA Ops:
  0.6 22.3 %shard_map.59 = (bf16[16,256,128]{2,1,0:T(8,128)(2,1)}, bf16[8,256,128]{2,1,0:T(8,128)(2,1)}) custom-call(bf16[256,128]{1,0:T(8,128)(2,1)} %refs_0_.1, bf16[256,128]{1,0:T(8,128)(2,1)} %bitcast.83), custom_call_target="tpu_custom_call" | custom-call | tf_op jit(solution)/shard_map/pallas_call | solution.py:186
  24.3 1.8 multiply_reduce_fusion
  28.0 13.6 %shard_map.60 = f32[1,4096]{1,0:T(1,128)} custom-call(bf16[4096,128]{1,0:T(8,128)(2,1)} %bitcast.48, bf16[2048,128]{1,0:T(8,128)(2,1)} %bitcast.55, f32[1,2048]{1,0:T(1,128)} %bitcast.87, f32[1,4096]{1,0:T(1,128)} %bitcast.64), custom_call_target="tpu_custom_call" | custom-call | tf_op jit(solution)/shard_map/pallas_call | solution.py:44
  42.2 1.4 reduce.20
  44.3 10.5 %shard_map.61 = f32[8,512]{1,0:T(8,128)} custom-call(f32[8,512]{1,0:T(8,128)} %reshape_squeeze.18.x_ref), custom_call_target="tpu_custom_call" | custom-call | tf_op jit(solution)/shard_map/pallas_call | solution.py:200
  56.2 13.8 %shard_map.62 = f32[1,2048]{1,0:T(1,128)} custom-call(bf16[2048,128]{1,0:T(8,128)(2,1)} %bitcast.56, bf16[4096,128]{1,0:T(8,128)(2,1)} %bitcast.49, f32[1,4096]{1,0:T(1,128)} %bitcast.81, f32[1,2048]{1,0:T(1,128)} %bitcast.73), custom_call_target="tpu_custom_call" | custom-call | tf_op jit(solution)/shard_map/pallas_call | solution.py:44
  69.9 1.4 reduce.21
  71.9 6.8 %shard_map.63 = f32[8,256]{1,0:T(8,128)} custom-call(f32[8,256]{1,0:T(8,128)} %reshape_squeeze.19.x_ref), custom_call_target="tpu_custom_call" | custom-call | tf_op jit(solution)/shard_map/pallas_call | solution.py:200
  80.1 13.6 %shard_map.64 = f32[1,4096]{1,0:T(1,128)} custom-call(bf16[4096,128]{1,0:T(8,128)(2,1)} %bitcast.50, bf16[2048,128]{1,0:T(8,128)(2,1)} %bitcast.57, f32[1,2048]{1,0:T(1,128)} %bitcast.90, f32[1,4096]{1,0:T(1,128)} %bitcast.65), custom_call_target="tpu_custom_call" | custom-call | tf_op jit(solution)/shard_map/pallas_call | solution.py:44
  93.6 1.4 reduce.22
  95.7 11.2 %shard_map.65 = f32[8,512]{1,0:T(8,128)} custom-call(f32[8,512]{1,0:T(8,128)} %reshape_squeeze.20.x_ref), custom_call_target="tpu_custom_call" | custom-call | tf_op jit(solution)/shard_map/pallas_call | solution.py:200
  108.3 13.8 %shard_map.66 = f32[1,2048]{1,0:T(1,128)} custom-call(bf16[2048,128]{1,0:T(8,128)(2,1)} %bitcast.58, bf16[4096,128]{1,0:T(8,128)(2,1)} %bitcast.51, f32[1,4096]{1,0:T(1,128)} %bitcast.82, f32[1,2048]{1,0:T(1,128)} %bitcast.74), custom_call_target="tpu_custom_call" | custom-call | tf_op jit(solution)/shard_map/pallas_call | solution.py:44
  122.1 1.4 reduce.23
  124.1 6.8 %shard_map.67 = f32[8,256]{1,0:T(8,128)} custom-call(f32[8,256]{1,0:T(8,128)} %reshape_squeeze.21.x_ref), custom_call_target="tpu_custom_call" | custom-call | tf_op jit(solution)/shard_map/pallas_call | solution.py:200
  132.2 13.6 %shard_map.68 = f32[1,4096]{1,0:T(1,128)} custom-call(bf16[4096,128]{1,0:T(8,128)(2,1)} %bitcast.52, bf16[2048,128]{1,0:T(8,128)(2,1)} %bitcast.59, f32[1,2048]{1,0:T(1,128)} %bitcast.89, f32[1,4096]{1,0:T(1,128)} %bitcast.66), custom_call_target="tpu_custom_call" | custom-call | tf_op jit(solution)/shard_map/pallas_call | solution.py:44
  145.8 1.5 reduce.24
  147.9 11.2 %shard_map.69 = f32[8,512]{1,0:T(8,128)} custom-call(f32[8,512]{1,0:T(8,128)} %reshape_squeeze.22.x_ref), custom_call_target="tpu_custom_call" | custom-call | tf_op jit(solution)/shard_map/pallas_call | solution.py:200
  160.4 13.8 %shard_map.70 = f32[1,2048]{1,0:T(1,128)} custom-call(bf16[2048,128]{1,0:T(8,128)(2,1)} %bitcast.60, bf16[4096,128]{1,0:T(8,128)(2,1)} %bitcast.53, f32[1,4096]{1,0:T(1,128)} %bitcast.70, f32[1,2048]{1,0:T(1,128)} %bitcast.75), custom_call_target="tpu_custom_call" | custom-call | tf_op jit(solution)/shard_map/pallas_call | solution.py:44
  176.2 6.8 %shard_map.71 = f32[8,256]{1,0:T(8,128)} custom-call(f32[8,256]{1,0:T(8,128)} %reshape_squeeze.23.x_ref), custom_call_target="tpu_custom_call" | custom-call | tf_op jit(solution)/shard_map/pallas_call | solution.py:200
  184.3 20.4 %shard_map.72 = (f32[4096,128]{1,0:T(8,128)}, f32[2048,128]{1,0:T(8,128)}, f32[1,2048]{1,0:T(1,128)}) custom-call(bf16[4096,128]{1,0:T(8,128)(2,1)} %bitcast.54, bf16[2048,128]{1,0:T(8,128)(2,1)} %bitcast.61, f32[1,4096]{1,0:T(1,128)} %bitcast.71, f32[1,2048]{1,0:T(1,128)} %bitcast.88), custom_call_target="tpu_custom_call" | custom-call | tf_op jit(solution)/shard_map/pallas_call | solution.py:78
  204.7 2.6 subtract_multiply_fusion
  207.2 49.1 %shard_map.73 = (f32[256,128]{1,0:T(8,128)}, f32[256,128]{1,0:T(8,128)}) custom-call(f32[16,256,128]{2,1,0:T(8,128)} %bitcast.63, f32[8,256,128]{2,1,0:T(8,128)} %bitcast.62), custom_call_target="tpu_custom_call" | custom-call | tf_op jit(solution)/shard_map/pallas_call | solution.py:186
  256.4 1.6 copy.19
  257.9 1.6 copy.20
  (40 shorter events, 16.9 us)
Async XLA Ops:
  0.6 54.9 %copy-start.1 = (f32[4096]{0:T(1024)S(1)}, f32[4096]{0:T(1024)}, u32[]{:S(2)}) copy-start(f32[4096]{0:T(1024)} %param.6) | copy-start | bytes 49156
  26.2 53.3 %copy-start.2 = (f32[2048]{0:T(1024)S(1)}, f32[2048]{0:T(1024)}, u32[]{:S(2)}) copy-start(f32[2048]{0:T(1024)} %param.7) | copy-start | bytes 24580
  145.8 58.9 %copy-start = (bf16[8,256,128]{2,1,0:T(8,128)(2,1)S(1)}, bf16[8,256,128]{2,1,0:T(8,128)(2,1)}, u32[]{:S(2)}) copy-start(bf16[8,256,128]{2,1,0:T(8,128)(2,1)} %get-tuple-element.10) | copy-start | bytes 1572868

commit v7 on v6

--- a/solution.py
+++ b/solution.py
@@ -12,9 +12,10 @@
 EPS = D / 20.0
 INV = 1.0 / EPS
 TWO_INV = 2.0 / EPS
-ROW_TILE = 512
-COL_TILE = 256
 VMEM_LIMIT = 60 * 1024 * 1024
+LOG2E = 1.4426950408889634
+LN2 = 0.6931471805599453
+SCALE2 = TWO_INV * LOG2E
 NT = (((1,), (1,)), ((), ()))
 TN = (((0,), (0,)), ((), ()))
 
@@ -31,27 +32,33 @@
     return jnp.transpose(jnp.broadcast_to(row, (D, row.shape[1])))[:, 0:1]
 
 
+def _row_of(v):
+    return jnp.concatenate([v[k:k + 1, :] for k in range(v.shape[0])], axis=1)
+
+
 def _lse_kernel(p_ref, q_ref, a_ref, b_ref, o_ref):
+    i = pl.program_id(0)
     cross = lax.dot_general(p_ref[...], q_ref[...], NT, preferred_element_type=jnp.float32)
-    t = a_ref[...] + TWO_INV * cross
+    t = _row_of(a_ref[...]) * LOG2E + SCALE2 * cross
     top = jnp.max(t, axis=1, keepdims=True)
-    total = jnp.sum(jnp.exp(t - top), axis=1, keepdims=True)
-    o_ref[...] = _to_row(top + jnp.log(total)) - b_ref[...]
-
-
-def lse(p, q, a, b, tile):
+    total = jnp.sum(jnp.exp2(t - top), axis=1, keepdims=True)
+    o_ref[pl.ds(i, 1), :] = _to_row(top * LN2 + jnp.log(total)) - b_ref[pl.ds(i, 1), :]
+
+
+def lse(p, q, a, b):
     rows, cols = p.shape[0], q.shape[0]
+    tile = rows // 8
     return pl.pallas_call(
         _lse_kernel,
-        out_shape=jax.ShapeDtypeStruct((1, rows), jnp.float32),
-        grid=(rows // tile,),
+        out_shape=jax.ShapeDtypeStruct((8, tile), jnp.float32),
+        grid=(8,),
         in_specs=[
             pl.BlockSpec((tile, D), lambda i: (i, 0)),
             pl.BlockSpec((cols, D), lambda i: (0, 0)),
-            pl.BlockSpec((1, cols), lambda i: (0, 0)),
-            pl.BlockSpec((1, tile), lambda i: (0, i)),
+            pl.BlockSpec((8, cols // 8), lambda i: (0, 0)),
+            pl.BlockSpec((8, tile), lambda i: (0, 0)),
         ],
-        out_specs=pl.BlockSpec((1, tile), lambda i: (0, i)),
+        out_specs=pl.BlockSpec((8, tile), lambda i: (0, 0)),
         compiler_params=_params(("arbitrary",)),
     )(p, q, a, b)
 
@@ -62,9 +69,11 @@
         pc_ref[...] = jnp.zeros_like(pc_ref)
         c_ref[...] = jnp.zeros_like(c_ref)
 
+    i = pl.program_id(0)
     x = x_ref[...]
     cross = lax.dot_general(x, y_ref[...], NT, preferred_element_type=jnp.float32)
-    plan = jnp.exp(_to_col(u_ref[...]) + a_ref[...] + TWO_INV * cross).astype(jnp.bfloat16)
+    u = _to_col(u_ref[pl.ds(i, 1), :] * LOG2E)
+    plan = jnp.exp2(u + _row_of(a_ref[...]) * LOG2E + SCALE2 * cross).astype(jnp.bfloat16)
     wide = plan.astype(jnp.float32)
     r = jnp.sum(wide, axis=1, keepdims=True)
     c_ref[...] += jnp.sum(wide, axis=0, keepdims=True)
@@ -82,15 +91,15 @@
             jax.ShapeDtypeStruct((cols, D), jnp.float32),
             jax.ShapeDtypeStruct((1, cols), jnp.float32),
         ),
-        grid=(rows // ROW_TILE,),
+        grid=(8,),
         in_specs=[
-            pl.BlockSpec((ROW_TILE, D), lambda i: (i, 0)),
+            pl.BlockSpec((rows // 8, D), lambda i: (i, 0)),
             pl.BlockSpec((cols, D), lambda i: (0, 0)),
-            pl.BlockSpec((1, ROW_TILE), lambda i: (0, i)),
-            pl.BlockSpec((1, cols), lambda i: (0, 0)),
+            pl.BlockSpec((8, rows // 8), lambda i: (0, 0)),
+            pl.BlockSpec((8, cols // 8), lambda i: (0, 0)),
         ],
         out_specs=(
-            pl.BlockSpec((ROW_TILE, D), lambda i: (i, 0)),
+            pl.BlockSpec((rows // 8, D), lambda i: (i, 0)),
             pl.BlockSpec((cols, D), lambda i: (0, 0)),
             pl.BlockSpec((1, cols), lambda i: (0, 0)),
         ),
@@ -108,7 +117,7 @@
     return (k, lax.axis_index("col"))
 
 
-def _gather_lse_kernel(axis, n, x_ref, o_ref, buf, send, recv):
+def _gather_lse_kernel(axis, n, x_ref, m_ref, q_ref, o_ref, buf, send, recv):
     me = lax.axis_index(axis)
     barrier = pltpu.get_barrier_semaphore()
     for d in range(1, n):
@@ -132,7 +141,8 @@
     buf[me] = x_ref[...]
     parts = buf[...]
     top = jnp.max(parts, axis=0)
-    o_ref[...] = top + jnp.log(jnp.sum(jnp.exp(parts - top[None]), axis=0))
+    total = top + jnp.log(jnp.sum(jnp.exp(parts - top[None]), axis=0))
+    o_ref[...] = (EPS * (m_ref[...] - total) - q_ref[...]) * INV
 
 
 def _exchange_kernel(jobs, *refs):
@@ -194,13 +204,12 @@
     )(*arrays)
 
 
-def combine(part, axis):
+def combine(block, axis, log_mass, sq):
     n = lax.axis_size(axis)
-    block = part.reshape(8, part.shape[0] // 8)
-    out = pl.pallas_call(
+    return pl.pallas_call(
         functools.partial(_gather_lse_kernel, axis, n),
         out_shape=jax.ShapeDtypeStruct(block.shape, jnp.float32),
-        in_specs=[pl.BlockSpec(memory_space=pltpu.VMEM)],
+        in_specs=[pl.BlockSpec(memory_space=pltpu.VMEM)] * 3,
         out_specs=pl.BlockSpec(memory_space=pltpu.VMEM),
         scratch_shapes=[
             pltpu.VMEM((n,) + block.shape, jnp.float32),
@@ -209,8 +218,7 @@
         ],
         compiler_params=pltpu.CompilerParams(
             collective_id=0 if axis == "col" else 1, has_side_effects=True),
-    )(block)
-    return out.reshape(part.shape)
+    )(block, log_mass, sq)
 
 
 def local(imu, camera, imu_mass, cam_mass):
@@ -219,25 +227,18 @@
         [("col", n_col, "gather"), ("row", n_row, "gather")], [imu, camera[0]], 3)
     imu_rows = imu_rows.reshape(-1, D)
     cam_rows = cam_rows.reshape(-1, D)
-    rows_sq = squares(imu_rows)
-    cols_sq = squares(cam_rows)
-    log_a = jnp.log(imu_mass)
-    log_b = jnp.log(cam_mass)
-    row_b = (rows_sq * INV)[None, :]
-    col_b = (cols_sq * INV)[None, :]
-
-    g = jnp.zeros_like(cols_sq)
-    f = jnp.zeros_like(rows_sq)
+    rows_sq = squares(imu_rows).reshape(8, -1)
+    cols_sq = squares(cam_rows).reshape(8, -1)
+    log_a = jnp.log(imu_mass).reshape(8, -1)
+    log_b = jnp.log(cam_mass).reshape(8, -1)
+    row_b = rows_sq * INV
+    col_b = cols_sq * INV
+
+    a = -col_b
     for step in range(ITERS):
-        a = (g[None, :] - cols_sq[None, :]) * INV
-        lse_f = combine(lse(imu_rows, cam_rows, a, row_b, ROW_TILE)[0], "col")
-        f = EPS * log_a - EPS * lse_f
-        u = ((f - rows_sq) * INV)[None, :]
-        lse_g = combine(lse(cam_rows, imu_rows, u, col_b, COL_TILE)[0], "row")
-        g = EPS * log_b - EPS * lse_g
-
-    a = (g[None, :] - cols_sq[None, :]) * INV
-    u = ((f - rows_sq) * INV)[None, :]
+        u = combine(lse(imu_rows, cam_rows, a, row_b), "col", log_a, rows_sq)
+        a = combine(lse(cam_rows, imu_rows, u, col_b), "row", log_b, cols_sq)
+
     grad_rows, pulled_cam, col_total = plan_grads(imu_rows, cam_rows, u, a)
     grad_cols = 2.0 * (col_total[0][:, None] * cam_rows.astype(jnp.float32) - pulled_cam)
     grad_imu, grad_cam = exchange(

time: 262 us -> 243 us (0.927)
  other arithmetic: 22.4 us -> 7 us
  local copies, waits for them, and re-layouts: 9.27 us -> 5.78 us
    pallas_call x6 -> x0, other arithmetic: 8.62 us -> none  [lse(): pl.pallas_call(_lse_kernel, out_shape=jax.ShapeDtypeStruct((1, rows), jnp...]
    unnamed x8 -> x0, other arithmetic: 4.27 us -> none
    another operation x6 -> x0, local copies, waits for them, and re-layouts: 3.63 us -> none  [combine(): block = part.reshape(8, part.shape[0] // 8)]
where the time goes in v7:
time: 243 us; the launch traced here: 241 us
  Pallas kernels  227 us (93%)
  other arithmetic  7 us (3%)
  local copies, waits for them, and re-layouts  5.78 us (2%)
    pallas_call x6, Pallas kernels, lse(): pl.pallas_call(_lse_kernel, out_shape=jax.ShapeDtypeStruct((8, tile), jnp...  82.6 us
    pallas_call x2, Pallas kernels, exchange(): pl.pallas_call(functools.partial(_exchange_kernel, tuple(jobs)), out_shap...  71.1 us
    pallas_call x6, Pallas kernels, combine(): pl.pallas_call(functools.partial(_gather_lse_kernel, axis, n), out_shape=...  53.5 us
    pallas_call x1, Pallas kernels, plan_grads(): pl.pallas_call(_plan_kernel, out_shape=(jax.ShapeDtypeStruct((rows, D), j...  20 us

profile of v7, /device:TPU:116, one launch (start us, length us, event | category | flops | bytes accessed | tf_op | source)
XLA Modules:
  0.0 240.8 jit_solution(15491780996143852148)
XLA Ops:
  0.6 0.7 log.7
  1.9 0.7 log.6
  2.6 0.6 reshape.34.m_ref
  3.3 22.2 %shard_map.59 = (bf16[16,256,128]{2,1,0:T(8,128)(2,1)}, bf16[8,256,128]{2,1,0:T(8,128)(2,1)}) custom-call(bf16[256,128]{1,0:T(8,128)(2,1)} %refs_0_.1, bf16[256,128]{1,0:T(8,128)(2,1)} %bitcast.25), custom_call_target="tpu_custom_call" | custom-call | tf_op jit(solution)/shard_map/pallas_call | solution.py:196
  25.5 1.4 multiply_reduce_fusion.1.q_ref
  26.9 1.8 multiply_reduce_fusion
  28.7 0.6 broadcast_multiply_fusion.b_ref
  30.0 13.5 %shard_map.60.x_ref = f32[8,512]{1,0:T(8,128)} custom-call(bf16[4096,128]{1,0:T(8,128)(2,1)} %bitcast.8, bf16[2048,128]{1,0:T(8,128)(2,1)} %bitcast.15, f32[8,256]{1,0:T(8,128)} %get-tuple-element.17.a_ref, f32[8,512]{1,0:T(8,128)} %broadcast_multiply_fusion.b_ref), custom_call_target="tpu_custom_call" | custom-call | tf_op jit(solution)/shard_map/pallas_call | solution.py:51
  43.5 10.6 %shard_map.61.a_ref = f32[8,512]{1,0:T(8,128)} custom-call(f32[8,512]{1,0:T(8,128)} %shard_map.60.x_ref, f32[8,512]{1,0:T(8,128)} %reshape.34.m_ref, f32[8,512]{1,0:T(8,128)} %copy-done.1), custom_call_target="tpu_custom_call" | custom-call | tf_op jit(solution)/shard_map/pallas_call | solution.py:209
  54.1 14.0 %shard_map.62.x_ref = f32[8,256]{1,0:T(8,128)} custom-call(bf16[2048,128]{1,0:T(8,128)(2,1)} %bitcast.16, bf16[4096,128]{1,0:T(8,128)(2,1)} %bitcast.9, f32[8,512]{1,0:T(8,128)} %shard_map.61.a_ref, f32[8,256]{1,0:T(8,128)} %get-tuple-element.16.b_ref), custom_call_target="tpu_custom_call" | custom-call | tf_op jit(solution)/shard_map/pallas_call | solution.py:51
  68.1 6.8 %shard_map.63.a_ref = f32[8,256]{1,0:T(8,128)} custom-call(f32[8,256]{1,0:T(8,128)} %shard_map.62.x_ref, f32[8,256]{1,0:T(8,128)} %reshape.35.m_ref, f32[8,256]{1,0:T(8,128)} %copy-done.2), custom_call_target="tpu_custom_call" | custom-call | tf_op jit(solution)/shard_map/pallas_call | solution.py:209
  74.9 13.5 %shard_map.64.x_ref = f32[8,512]{1,0:T(8,128)} custom-call(bf16[4096,128]{1,0:T(8,128)(2,1)} %bitcast.10, bf16[2048,128]{1,0:T(8,128)(2,1)} %bitcast.17, f32[8,256]{1,0:T(8,128)} %shard_map.63.a_ref, f32[8,512]{1,0:T(8,128)} %broadcast_multiply_fusion.b_ref), custom_call_target="tpu_custom_call" | custom-call | tf_op jit(solution)/shard_map/pallas_call | solution.py:51
  88.5 11.2 %shard_map.65.a_ref = f32[8,512]{1,0:T(8,128)} custom-call(f32[8,512]{1,0:T(8,128)} %shard_map.64.x_ref, f32[8,512]{1,0:T(8,128)} %reshape.34.m_ref, f32[8,512]{1,0:T(8,128)} %copy-done.1), custom_call_target="tpu_custom_call" | custom-call | tf_op jit(solution)/shard_map/pallas_call | solution.py:209
  99.7 14.0 %shard_map.66.x_ref = f32[8,256]{1,0:T(8,128)} custom-call(bf16[2048,128]{1,0:T(8,128)(2,1)} %bitcast.18, bf16[4096,128]{1,0:T(8,128)(2,1)} %bitcast.11, f32[8,512]{1,0:T(8,128)} %shard_map.65.a_ref, f32[8,256]{1,0:T(8,128)} %get-tuple-element.16.b_ref), custom_call_target="tpu_custom_call" | custom-call | tf_op jit(solution)/shard_map/pallas_call | solution.py:51
  113.7 6.8 %shard_map.67.a_ref = f32[8,256]{1,0:T(8,128)} custom-call(f32[8,256]{1,0:T(8,128)} %shard_map.66.x_ref, f32[8,256]{1,0:T(8,128)} %reshape.35.m_ref, f32[8,256]{1,0:T(8,128)} %copy-done.2), custom_call_target="tpu_custom_call" | custom-call | tf_op jit(solution)/shard_map/pallas_call | solution.py:209
  120.6 13.6 %shard_map.68.x_ref = f32[8,512]{1,0:T(8,128)} custom-call(bf16[4096,128]{1,0:T(8,128)(2,1)} %bitcast.12, bf16[2048,128]{1,0:T(8,128)(2,1)} %bitcast.19, f32[8,256]{1,0:T(8,128)} %shard_map.67.a_ref, f32[8,512]{1,0:T(8,128)} %broadcast_multiply_fusion.b_ref), custom_call_target="tpu_custom_call" | custom-call | tf_op jit(solution)/shard_map/pallas_call | solution.py:51
  134.1 11.2 %shard_map.69.a_ref.u_ref = f32[8,512]{1,0:T(8,128)} custom-call(f32[8,512]{1,0:T(8,128)} %shard_map.68.x_ref, f32[8,512]{1,0:T(8,128)} %reshape.34.m_ref, f32[8,512]{1,0:T(8,128)} %copy-done.1), custom_call_target="tpu_custom_call" | custom-call | tf_op jit(solution)/shard_map/pallas_call | solution.py:209
  145.4 14.0 %shard_map.70.x_ref = f32[8,256]{1,0:T(8,128)} custom-call(bf16[2048,128]{1,0:T(8,128)(2,1)} %bitcast.20, bf16[4096,128]{1,0:T(8,128)(2,1)} %bitcast.13, f32[8,512]{1,0:T(8,128)} %shard_map.69.a_ref.u_ref, f32[8,256]{1,0:T(8,128)} %get-tuple-element.16.b_ref), custom_call_target="tpu_custom_call" | custom-call | tf_op jit(solution)/shard_map/pallas_call | solution.py:51
  159.4 6.8 %shard_map.71.a_ref = f32[8,256]{1,0:T(8,128)} custom-call(f32[8,256]{1,0:T(8,128)} %shard_map.70.x_ref, f32[8,256]{1,0:T(8,128)} %reshape.35.m_ref, f32[8,256]{1,0:T(8,128)} %copy-done.2), custom_call_target="tpu_custom_call" | custom-call | tf_op jit(solution)/shard_map/pallas_call | solution.py:209
  166.2 20.0 %shard_map.72 = (f32[4096,128]{1,0:T(8,128)}, f32[2048,128]{1,0:T(8,128)}, f32[1,2048]{1,0:T(1,128)}) custom-call(bf16[4096,128]{1,0:T(8,128)(2,1)} %bitcast.14, bf16[2048,128]{1,0:T(8,128)(2,1)} %bitcast.21, f32[8,512]{1,0:T(8,128)} %shard_map.69.a_ref.u_ref, f32[8,256]{1,0:T(8,128)} %shard_map.71.a_ref), custom_call_target="tpu_custom_call" | custom-call | tf_op jit(solution)/shard_map/pallas_call | solution.py:87
  186.2 2.6 %subtract_multiply_fusion = f32[2048,128]{1,0:T(8,128)} fusion(f32[2048,128]{1,0:T(8,128)} %get-tuple-element.13, f32[2048]{0:T(1024)} %bitcast.26, bf16[8,256,128]{2,1,0:T(8,128)(2,1)S(1)} %copy-done), kind=kLoop, calls=%fused_computation.1 | loop fusion | flops 1048576 | bytes 2629632 | tf_op jit(solution)/shard_map/mul | solution.py:243
  188.8 48.9 %shard_map.73 = (f32[256,128]{1,0:T(8,128)}, f32[256,128]{1,0:T(8,128)}) custom-call(f32[16,256,128]{2,1,0:T(8,128)} %bitcast.23, f32[8,256,128]{2,1,0:T(8,128)} %bitcast.22), custom_call_target="tpu_custom_call" | custom-call | tf_op jit(solution)/shard_map/pallas_call | solution.py:196
  237.6 1.6 copy.8
  239.2 1.6 copy.9
  (9 shorter events, 1.2 us)
Async XLA Ops:
  26.9 41.2 %copy-start.2 = (f32[8,256]{1,0:T(8,128)}, f32[8,256]{1,0:T(8,128)S(1)}, u32[]{:S(2)}) copy-start(f32[8,256]{1,0:T(8,128)S(1)} %multiply_reduce_fusion.1.q_ref) | copy-start | bytes 24580
  28.7 14.7 %copy-start.1 = (f32[8,512]{1,0:T(8,128)}, f32[8,512]{1,0:T(8,128)S(1)}, u32[]{:S(2)}) copy-start(f32[8,512]{1,0:T(8,128)S(1)} %reshape.33.q_ref) | copy-start | bytes 49156
  120.6 65.6 %copy-start = (bf16[8,256,128]{2,1,0:T(8,128)(2,1)S(1)}, bf16[8,256,128]{2,1,0:T(8,128)(2,1)}, u32[]{:S(2)}) copy-start(bf16[8,256,128]{2,1,0:T(8,128)(2,1)} %get-tuple-element.10) | copy-start | bytes 1572868

commit v8 on v7

--- a/solution.py
+++ b/solution.py
@@ -104,6 +104,98 @@
             pl.BlockSpec((1, cols), lambda i: (0, 0)),
         ),
         compiler_params=_params(("arbitrary",)),
+    )(x, y, u, a)
+
+
+def _plan_scatter_kernel(n_col, n_row, x_ref, y_ref, u_ref, a_ref, gi_out, gc_out,
+                         gi, pc, csum, gcs, bufi, bufc, sendi, recvi, sendc, recvc):
+    me_c, me_r = lax.axis_index("col"), lax.axis_index("row")
+    barrier = pltpu.get_barrier_semaphore()
+    for d in range(1, n_col):
+        pl.semaphore_signal(barrier, inc=1, device_id=_peer("col", lax.rem(me_c + d, n_col)),
+                            device_id_type=pl.DeviceIdType.MESH)
+    for d in range(1, n_row):
+        pl.semaphore_signal(barrier, inc=1, device_id=_peer("row", lax.rem(me_r + d, n_row)),
+                            device_id_type=pl.DeviceIdType.MESH)
+    pl.semaphore_wait(barrier, n_col + n_row - 2)
+
+    def to_col_dev(k, slot):
+        return pltpu.make_async_remote_copy(
+            src_ref=gi.at[k], dst_ref=bufi.at[slot], send_sem=sendi.at[k], recv_sem=recvi.at[slot],
+            device_id=_peer("col", k), device_id_type=pl.DeviceIdType.MESH)
+
+    def to_row_dev(k, slot):
+        return pltpu.make_async_remote_copy(
+            src_ref=gcs.at[k], dst_ref=bufc.at[slot], send_sem=sendc.at[k], recv_sem=recvc.at[slot],
+            device_id=_peer("row", k), device_id_type=pl.DeviceIdType.MESH)
+
+    def each(n, me, body):
+        for k in range(n):
+            pl.when(me != k)(functools.partial(body, k))
+
+    rows, cols = x_ref.shape[0], y_ref.shape[0]
+    tiles = u_ref.shape[0]
+    tile, m, mc = rows // tiles, rows // n_col, cols // n_row
+    per = tile // m
+    y = y_ref[...]
+    a2 = _row_of(a_ref[...]) * LOG2E
+    pc[...] = jnp.zeros_like(pc)
+    csum[...] = jnp.zeros_like(csum)
+    for i in range(tiles):
+        x = x_ref[i * tile:(i + 1) * tile, :]
+        cross = lax.dot_general(x, y, NT, preferred_element_type=jnp.float32)
+        u = _to_col(u_ref[i:i + 1, :] * LOG2E)
+        plan = jnp.exp2(u + a2 + SCALE2 * cross).astype(jnp.bfloat16)
+        wide = plan.astype(jnp.float32)
+        r = jnp.sum(wide, axis=1, keepdims=True)
+        csum[...] += jnp.sum(wide, axis=0, keepdims=True)
+        pulled = jnp.dot(plan, y, preferred_element_type=jnp.float32)
+        g = 2.0 * (r * x.astype(jnp.float32) - pulled)
+        for s in range(per):
+            gi[i * per + s] = g[s * m:(s + 1) * m]
+        pc[...] += lax.dot_general(plan, x, TN, preferred_element_type=jnp.float32)
+        if i >= 1:
+            for s in range((i - 1) * per, i * per):
+                pl.when(me_c != s)(functools.partial(lambda k: to_col_dev(k, me_c).start(), s))
+    for s in range((tiles - 1) * per, tiles * per):
+        pl.when(me_c != s)(functools.partial(lambda k: to_col_dev(k, me_c).start(), s))
+    gcv = 2.0 * (_to_col(csum[...]) * y.astype(jnp.float32) - pc[...])
+    for k in range(n_row):
+        gcs[k] = gcv[k * mc:(k + 1) * mc]
+    each(n_row, me_r, lambda k: to_row_dev(k, me_r).start())
+    each(n_col, me_c, lambda k: to_col_dev(k, me_c).wait_send())
+    each(n_row, me_r, lambda k: to_row_dev(k, me_r).wait_send())
+    each(n_col, me_c, lambda k: to_col_dev(k, k).wait_recv())
+    each(n_row, me_r, lambda k: to_row_dev(k, k).wait_recv())
+    bufi[me_c] = gi[me_c]
+    bufc[me_r] = gcs[me_r]
+    gi_out[...] = jnp.sum(bufi[...], axis=0)
+    gc_out[...] = jnp.sum(bufc[...], axis=0)
+
+
+def plan_scatter(x, y, u, a, n_col, n_row):
+    rows, cols = x.shape[0], y.shape[0]
+    m, mc = rows // n_col, cols // n_row
+    return pl.pallas_call(
+        functools.partial(_plan_scatter_kernel, n_col, n_row),
+        out_shape=(jax.ShapeDtypeStruct((m, D), jnp.float32),
+                   jax.ShapeDtypeStruct((mc, D), jnp.float32)),
+        in_specs=[pl.BlockSpec(memory_space=pltpu.VMEM)] * 4,
+        out_specs=(pl.BlockSpec(memory_space=pltpu.VMEM),) * 2,
+        scratch_shapes=[
+            pltpu.VMEM((n_col, m, D), jnp.float32),
+            pltpu.VMEM((cols, D), jnp.float32),
+            pltpu.VMEM((1, cols), jnp.float32),
+            pltpu.VMEM((n_row, mc, D), jnp.float32),
+            pltpu.VMEM((n_col, m, D), jnp.float32),
+            pltpu.VMEM((n_row, mc, D), jnp.float32),
+            pltpu.SemaphoreType.DMA((n_col,)),
+            pltpu.SemaphoreType.DMA((n_col,)),
+            pltpu.SemaphoreType.DMA((n_row,)),
+            pltpu.SemaphoreType.DMA((n_row,)),
+        ],
+        compiler_params=pltpu.CompilerParams(
+            collective_id=4, has_side_effects=True, vmem_limit_bytes=VMEM_LIMIT),
     )(x, y, u, a)
 
 
@@ -239,11 +331,7 @@
         u = combine(lse(imu_rows, cam_rows, a, row_b), "col", log_a, rows_sq)
         a = combine(lse(cam_rows, imu_rows, u, col_b), "row", log_b, cols_sq)
 
-    grad_rows, pulled_cam, col_total = plan_grads(imu_rows, cam_rows, u, a)
-    grad_cols = 2.0 * (col_total[0][:, None] * cam_rows.astype(jnp.float32) - pulled_cam)
-    grad_imu, grad_cam = exchange(
-        [("col", n_col, "scatter"), ("row", n_row, "scatter")],
-        [grad_rows.reshape(n_col, -1, D), grad_cols.reshape(n_row, -1, D)], 2)
+    grad_imu, grad_cam = plan_scatter(imu_rows, cam_rows, u, a, n_col, n_row)
     return (grad_imu, grad_cam[None])
 
 

time: 243 us -> 229 us (0.942)
  Pallas kernels: 227 us -> 215 us
  other arithmetic: 7 us -> 4.44 us
    pallas_call x2 -> x1, Pallas kernels: 71.1 us -> 22.2 us  [exchange(): pl.pallas_call(functools.partial(_exchange_kernel, tuple(jobs)), out_shap...]
    pallas_call x1, Pallas kernels: 20 us -> 56.6 us  [plan_scatter(): pl.pallas_call(functools.partial(_plan_scatter_kernel, n_col, n_row), out...]
    mul x1 -> x0, other arithmetic: 2.56 us -> none  [local(): 2.0 * (col_total[0][:, None] * cam_rows.astype(jnp.float32) - pulled_cam)]
where the time goes in v8:
time: 229 us; the launch traced here: 226 us
  Pallas kernels  215 us (94%)
  local copies, waits for them, and re-layouts  5.78 us (3%)
  other arithmetic  4.44 us (2%)
    pallas_call x6, Pallas kernels, lse(): pl.pallas_call(_lse_kernel, out_shape=jax.ShapeDtypeStruct((8, tile), jnp...  82.6 us
    pallas_call x1, Pallas kernels, plan_scatter(): pl.pallas_call(functools.partial(_plan_scatter_kernel, n_col, n_row), out...  56.6 us
    pallas_call x6, Pallas kernels, combine(): pl.pallas_call(functools.partial(_gather_lse_kernel, axis, n), out_shape=...  53.6 us
    pallas_call x1, Pallas kernels, exchange(): pl.pallas_call(functools.partial(_exchange_kernel, tuple(jobs)), out_shap...  22.2 us

profile of v8, /device:TPU:116, one launch (start us, length us, event | category | flops | bytes accessed | tf_op | source)
XLA Modules:
  0.0 225.9 jit_solution(97665130765070951)
XLA Ops:
  0.6 0.7 log.7
  1.3 0.6 reshape.28.m_ref
  1.9 0.7 log.6
  2.7 0.6 reshape.27.m_ref
  3.3 22.2 %shard_map.59 = (bf16[16,256,128]{2,1,0:T(8,128)(2,1)}, bf16[8,256,128]{2,1,0:T(8,128)(2,1)}) custom-call(bf16[256,128]{1,0:T(8,128)(2,1)} %refs_0_.1, bf16[256,128]{1,0:T(8,128)(2,1)} %bitcast.19), custom_call_target="tpu_custom_call" | custom-call | tf_op jit(solution)/shard_map/pallas_call | solution.py:288
  25.5 1.4 multiply_reduce_fusion.1.q_ref
  26.9 1.8 multiply_reduce_fusion
  28.7 0.6 broadcast_multiply_fusion.b_ref
  29.3 0.6 broadcast_multiply_fusion.1
  29.9 13.5 %shard_map.60.x_ref = f32[8,512]{1,0:T(8,128)} custom-call(bf16[4096,128]{1,0:T(8,128)(2,1)} %bitcast.4, bf16[2048,128]{1,0:T(8,128)(2,1)} %bitcast.11, f32[8,256]{1,0:T(8,128)} %get-tuple-element.11.a_ref, f32[8,512]{1,0:T(8,128)} %broadcast_multiply_fusion.b_ref), custom_call_target="tpu_custom_call" | custom-call | tf_op jit(solution)/shard_map/pallas_call | solution.py:51
  43.4 10.6 %shard_map.61.a_ref = f32[8,512]{1,0:T(8,128)} custom-call(f32[8,512]{1,0:T(8,128)} %shard_map.60.x_ref, f32[8,512]{1,0:T(8,128)} %reshape.27.m_ref, f32[8,512]{1,0:T(8,128)} %copy-done), custom_call_target="tpu_custom_call" | custom-call | tf_op jit(solution)/shard_map/pallas_call | solution.py:301
  54.0 14.0 %shard_map.62.x_ref = f32[8,256]{1,0:T(8,128)} custom-call(bf16[2048,128]{1,0:T(8,128)(2,1)} %bitcast.12, bf16[4096,128]{1,0:T(8,128)(2,1)} %bitcast.5, f32[8,512]{1,0:T(8,128)} %shard_map.61.a_ref, f32[8,256]{1,0:T(8,128)} %get-tuple-element.10.b_ref), custom_call_target="tpu_custom_call" | custom-call | tf_op jit(solution)/shard_map/pallas_call | solution.py:51
  68.1 6.8 %shard_map.63.a_ref = f32[8,256]{1,0:T(8,128)} custom-call(f32[8,256]{1,0:T(8,128)} %shard_map.62.x_ref, f32[8,256]{1,0:T(8,128)} %reshape.28.m_ref, f32[8,256]{1,0:T(8,128)} %copy-done.1), custom_call_target="tpu_custom_call" | custom-call | tf_op jit(solution)/shard_map/pallas_call | solution.py:301
  74.9 13.5 %shard_map.64.x_ref = f32[8,512]{1,0:T(8,128)} custom-call(bf16[4096,128]{1,0:T(8,128)(2,1)} %bitcast.6, bf16[2048,128]{1,0:T(8,128)(2,1)} %bitcast.13, f32[8,256]{1,0:T(8,128)} %shard_map.63.a_ref, f32[8,512]{1,0:T(8,128)} %broadcast_multiply_fusion.b_ref), custom_call_target="tpu_custom_call" | custom-call | tf_op jit(solution)/shard_map/pallas_call | solution.py:51
  88.4 11.2 %shard_map.65.a_ref = f32[8,512]{1,0:T(8,128)} custom-call(f32[8,512]{1,0:T(8,128)} %shard_map.64.x_ref, f32[8,512]{1,0:T(8,128)} %reshape.27.m_ref, f32[8,512]{1,0:T(8,128)} %copy-done), custom_call_target="tpu_custom_call" | custom-call | tf_op jit(solution)/shard_map/pallas_call | solution.py:301
  99.7 14.0 %shard_map.66.x_ref = f32[8,256]{1,0:T(8,128)} custom-call(bf16[2048,128]{1,0:T(8,128)(2,1)} %bitcast.14, bf16[4096,128]{1,0:T(8,128)(2,1)} %bitcast.7, f32[8,512]{1,0:T(8,128)} %shard_map.65.a_ref, f32[8,256]{1,0:T(8,128)} %get-tuple-element.10.b_ref), custom_call_target="tpu_custom_call" | custom-call | tf_op jit(solution)/shard_map/pallas_call | solution.py:51
  113.7 6.8 %shard_map.67.a_ref = f32[8,256]{1,0:T(8,128)} custom-call(f32[8,256]{1,0:T(8,128)} %shard_map.66.x_ref, f32[8,256]{1,0:T(8,128)} %reshape.28.m_ref, f32[8,256]{1,0:T(8,128)} %copy-done.1), custom_call_target="tpu_custom_call" | custom-call | tf_op jit(solution)/shard_map/pallas_call | solution.py:301
  120.6 13.5 %shard_map.68.x_ref = f32[8,512]{1,0:T(8,128)} custom-call(bf16[4096,128]{1,0:T(8,128)(2,1)} %bitcast.8, bf16[2048,128]{1,0:T(8,128)(2,1)} %bitcast.15, f32[8,256]{1,0:T(8,128)} %shard_map.67.a_ref, f32[8,512]{1,0:T(8,128)} %broadcast_multiply_fusion.b_ref), custom_call_target="tpu_custom_call" | custom-call | tf_op jit(solution)/shard_map/pallas_call | solution.py:51
  134.1 11.2 %shard_map.69.a_ref.u_ref = f32[8,512]{1,0:T(8,128)} custom-call(f32[8,512]{1,0:T(8,128)} %shard_map.68.x_ref, f32[8,512]{1,0:T(8,128)} %reshape.27.m_ref, f32[8,512]{1,0:T(8,128)} %copy-done), custom_call_target="tpu_custom_call" | custom-call | tf_op jit(solution)/shard_map/pallas_call | solution.py:301
  145.3 14.0 %shard_map.70.x_ref = f32[8,256]{1,0:T(8,128)} custom-call(bf16[2048,128]{1,0:T(8,128)(2,1)} %bitcast.16, bf16[4096,128]{1,0:T(8,128)(2,1)} %bitcast.9, f32[8,512]{1,0:T(8,128)} %shard_map.69.a_ref.u_ref, f32[8,256]{1,0:T(8,128)} %get-tuple-element.10.b_ref), custom_call_target="tpu_custom_call" | custom-call | tf_op jit(solution)/shard_map/pallas_call | solution.py:51
  159.3 6.8 %shard_map.71.a_ref = f32[8,256]{1,0:T(8,128)} custom-call(f32[8,256]{1,0:T(8,128)} %shard_map.70.x_ref, f32[8,256]{1,0:T(8,128)} %reshape.28.m_ref, f32[8,256]{1,0:T(8,128)} %copy-done.1), custom_call_target="tpu_custom_call" | custom-call | tf_op jit(solution)/shard_map/pallas_call | solution.py:301
  166.2 56.6 %shard_map.72 = (f32[256,128]{1,0:T(8,128)}, f32[256,128]{1,0:T(8,128)}) custom-call(bf16[4096,128]{1,0:T(8,128)(2,1)} %bitcast.10, bf16[2048,128]{1,0:T(8,128)(2,1)} %bitcast.17, f32[8,512]{1,0:T(8,128)} %shard_map.69.a_ref.u_ref, f32[8,256]{1,0:T(8,128)} %shard_map.71.a_ref), custom_call_target="tpu_custom_call" | custom-call | tf_op jit(solution)/shard_map/pallas_call | solution.py:179
  222.8 1.6 copy.8
  224.3 1.6 copy.9
  (5 shorter events, 0.0 us)
Async XLA Ops:
  26.8 16.6 %copy-start.1 = (f32[8,256]{1,0:T(8,128)}, f32[8,256]{1,0:T(8,128)S(1)}, u32[]{:S(2)}) copy-start(f32[8,256]{1,0:T(8,128)S(1)} %multiply_reduce_fusion.1.q_ref) | copy-start | bytes 24580
  28.7 14.7 %copy-start = (f32[8,512]{1,0:T(8,128)}, f32[8,512]{1,0:T(8,128)S(1)}, u32[]{:S(2)}) copy-start(f32[8,512]{1,0:T(8,128)S(1)} %reshape.26.q_ref) | copy-start | bytes 49156

commit v9 on v8

--- a/solution.py
+++ b/solution.py
@@ -199,6 +199,92 @@
     )(x, y, u, a)
 
 
+def _lse_combine_kernel(axis, n, p_ref, q_ref, a_ref, b_ref, m_ref, s_ref, o_ref,
+                        part, buf, send, recv):
+    me = lax.axis_index(axis)
+    barrier = pltpu.get_barrier_semaphore()
+    for d in range(1, n):
+        pl.semaphore_signal(barrier, inc=1, device_id=_peer(axis, lax.rem(me + d, n)),
+                            device_id_type=pl.DeviceIdType.MESH)
+    pl.semaphore_wait(barrier, n - 1)
+
+    def out_copy(c, d):
+        return pltpu.make_async_remote_copy(
+            src_ref=part.at[c], dst_ref=buf.at[me, c], send_sem=send.at[c, d],
+            recv_sem=recv.at[c, me], device_id=_peer(axis, lax.rem(me + d, n)),
+            device_id_type=pl.DeviceIdType.MESH)
+
+    def in_copy(c, d):
+        src = lax.rem(me + n - d, n)
+        return pltpu.make_async_remote_copy(
+            src_ref=part.at[c], dst_ref=buf.at[src, c], send_sem=send.at[c, d],
+            recv_sem=recv.at[c, src], device_id=_peer(axis, src),
+            device_id_type=pl.DeviceIdType.MESH)
+
+    def send_half(c):
+        for d in range(1, n):
+            out_copy(c, d).start()
+
+    half = part.shape[1]
+    tile = p_ref.shape[0] // (2 * half)
+    q = q_ref[...]
+    a2 = _row_of(a_ref[...]) * LOG2E
+
+    def body(i, carry):
+        start = pl.multiple_of(i * tile, tile)
+        cross = lax.dot_general(p_ref[pl.ds(start, tile), :], q, NT,
+                                preferred_element_type=jnp.float32)
+        t = a2 + SCALE2 * cross
+        top = jnp.max(t, axis=1, keepdims=True)
+        total = jnp.sum(jnp.exp2(t - top), axis=1, keepdims=True)
+        row = _to_row(top * LN2 + jnp.log(total)) - b_ref[pl.ds(i, 1), :]
+        part.at[i // half][pl.ds(i % half, 1), :] = row
+
+        @pl.when(i == half)
+        def _():
+            send_half(0)
+
+        return carry
+
+    lax.fori_loop(0, 2 * half, body, 0)
+
+    def finish(c):
+        for d in range(1, n):
+            out_copy(c, d).wait_send()
+        for d in range(1, n):
+            in_copy(c, d).wait_recv()
+        buf[me, c] = part[c]
+        parts = buf[:, c]
+        top = jnp.max(parts, axis=0)
+        total = top + jnp.log(jnp.sum(jnp.exp(parts - top[None]), axis=0))
+        rows = slice(c * half, (c + 1) * half)
+        o_ref[rows, :] = (EPS * (m_ref[rows, :] - total) - s_ref[rows, :]) * INV
+
+    finish(0)
+    send_half(1)
+    finish(1)
+
+
+def lse_combine(p, q, a, b, log_mass, sq, axis):
+    n = lax.axis_size(axis)
+    m = p.shape[0] // 8
+    return pl.pallas_call(
+        functools.partial(_lse_combine_kernel, axis, n),
+        out_shape=jax.ShapeDtypeStruct((8, m), jnp.float32),
+        in_specs=[pl.BlockSpec(memory_space=pltpu.VMEM)] * 6,
+        out_specs=pl.BlockSpec(memory_space=pltpu.VMEM),
+        scratch_shapes=[
+            pltpu.VMEM((2, 4, m), jnp.float32),
+            pltpu.VMEM((n, 2, 4, m), jnp.float32),
+            pltpu.SemaphoreType.DMA((2, n)),
+            pltpu.SemaphoreType.DMA((2, n)),
+        ],
+        compiler_params=pltpu.CompilerParams(
+            collective_id=5 if axis == "col" else 6, has_side_effects=True,
+            vmem_limit_bytes=VMEM_LIMIT),
+    )(p, q, a, b, log_mass, sq)
+
+
 def squares(values):
     return jnp.sum(jnp.square(values.astype(jnp.float32)), axis=1)
 
@@ -328,8 +414,8 @@
 
     a = -col_b
     for step in range(ITERS):
-        u = combine(lse(imu_rows, cam_rows, a, row_b), "col", log_a, rows_sq)
-        a = combine(lse(cam_rows, imu_rows, u, col_b), "row", log_b, cols_sq)
+        u = lse_combine(imu_rows, cam_rows, a, row_b, log_a, rows_sq, "col")
+        a = lse_combine(cam_rows, imu_rows, u, col_b, log_b, cols_sq, "row")
 
     grad_imu, grad_cam = plan_scatter(imu_rows, cam_rows, u, a, n_col, n_row)
     return (grad_imu, grad_cam[None])

time: 229 us -> 222 us (0.969)
  Pallas kernels: 215 us -> 209 us
    pallas_call x12 -> x6, Pallas kernels: 136 us -> 131 us  [lse_combine(): pl.pallas_call(functools.partial(_lse_combine_kernel, axis, n), out_shape...]
where the time goes in v9:
time: 222 us; the launch traced here: 220 us
  Pallas kernels  209 us (94%)
  local copies, waits for them, and re-layouts  5.79 us (3%)
  other arithmetic  4.43 us (2%)
    pallas_call x6, Pallas kernels, lse_combine(): pl.pallas_call(functools.partial(_lse_combine_kernel, axis, n), out_shape...  131 us
    pallas_call x1, Pallas kernels, plan_scatter(): pl.pallas_call(functools.partial(_plan_scatter_kernel, n_col, n_row), out...  55.6 us
    pallas_call x1, Pallas kernels, exchange(): pl.pallas_call(functools.partial(_exchange_kernel, tuple(jobs)), out_shap...  22.2 us

profile of v9, /device:TPU:116, one launch (start us, length us, event | category | flops | bytes accessed | tf_op | source)
XLA Modules:
  0.0 219.7 jit_solution(13726397997074493549)
XLA Ops:
  0.6 0.7 log.7
  1.3 0.6 reshape.28.m_ref
  1.9 0.7 log.6
  2.7 0.6 reshape.27.m_ref
  3.3 22.2 %shard_map.59 = (bf16[16,256,128]{2,1,0:T(8,128)(2,1)}, bf16[8,256,128]{2,1,0:T(8,128)(2,1)}) custom-call(bf16[256,128]{1,0:T(8,128)(2,1)} %refs_0_.1, bf16[256,128]{1,0:T(8,128)(2,1)} %bitcast.19), custom_call_target="tpu_custom_call" | custom-call | tf_op jit(solution)/shard_map/pallas_call | solution.py:374
  25.5 1.4 multiply_reduce_fusion.1.s_ref
  26.9 0.0 copy-start.1
  26.9 1.8 multiply_reduce_fusion
  28.7 0.0 copy-start
  28.7 0.6 broadcast_multiply_fusion.b_ref
  29.3 0.6 broadcast_multiply_fusion.1
  29.9 0.0 copy-done
  29.9 22.9 %shard_map.60.a_ref = f32[8,512]{1,0:T(8,128)} custom-call(bf16[4096,128]{1,0:T(8,128)(2,1)} %bitcast.4, bf16[2048,128]{1,0:T(8,128)(2,1)} %bitcast.11, f32[8,256]{1,0:T(8,128)} %get-tuple-element.11.a_ref, f32[8,512]{1,0:T(8,128)} %broadcast_multiply_fusion.b_ref, f32[8,512]{1,0:T(8,128)} %reshape.27.m_ref, f32[8,512]{1,0:T(8,128)} %copy-done), custom_call_target="tpu_custom_call" | custom-call | tf_op jit(solution)/shard_map/pallas_call | solution.py:271
  52.9 0.0 copy-done.1
  52.9 20.5 %shard_map.61.a_ref = f32[8,256]{1,0:T(8,128)} custom-call(bf16[2048,128]{1,0:T(8,128)(2,1)} %bitcast.12, bf16[4096,128]{1,0:T(8,128)(2,1)} %bitcast.5, f32[8,512]{1,0:T(8,128)} %shard_map.60.a_ref, f32[8,256]{1,0:T(8,128)} %get-tuple-element.10.b_ref, f32[8,256]{1,0:T(8,128)} %reshape.28.m_ref, f32[8,256]{1,0:T(8,128)} %copy-done.1), custom_call_target="tpu_custom_call" | custom-call | tf_op jit(solution)/shard_map/pallas_call | solution.py:271
  73.4 23.8 %shard_map.62.a_ref = f32[8,512]{1,0:T(8,128)} custom-call(bf16[4096,128]{1,0:T(8,128)(2,1)} %bitcast.6, bf16[2048,128]{1,0:T(8,128)(2,1)} %bitcast.13, f32[8,256]{1,0:T(8,128)} %shard_map.61.a_ref, f32[8,512]{1,0:T(8,128)} %broadcast_multiply_fusion.b_ref, f32[8,512]{1,0:T(8,128)} %reshape.27.m_ref, f32[8,512]{1,0:T(8,128)} %copy-done), custom_call_target="tpu_custom_call" | custom-call | tf_op jit(solution)/shard_map/pallas_call | solution.py:271
  97.1 20.2 %shard_map.63.a_ref = f32[8,256]{1,0:T(8,128)} custom-call(bf16[2048,128]{1,0:T(8,128)(2,1)} %bitcast.14, bf16[4096,128]{1,0:T(8,128)(2,1)} %bitcast.7, f32[8,512]{1,0:T(8,128)} %shard_map.62.a_ref, f32[8,256]{1,0:T(8,128)} %get-tuple-element.10.b_ref, f32[8,256]{1,0:T(8,128)} %reshape.28.m_ref, f32[8,256]{1,0:T(8,128)} %copy-done.1), custom_call_target="tpu_custom_call" | custom-call | tf_op jit(solution)/shard_map/pallas_call | solution.py:271
  117.3 23.3 %shard_map.64.a_ref.u_ref = f32[8,512]{1,0:T(8,128)} custom-call(bf16[4096,128]{1,0:T(8,128)(2,1)} %bitcast.8, bf16[2048,128]{1,0:T(8,128)(2,1)} %bitcast.15, f32[8,256]{1,0:T(8,128)} %shard_map.63.a_ref, f32[8,512]{1,0:T(8,128)} %broadcast_multiply_fusion.b_ref, f32[8,512]{1,0:T(8,128)} %reshape.27.m_ref, f32[8,512]{1,0:T(8,128)} %copy-done), custom_call_target="tpu_custom_call" | custom-call | tf_op jit(solution)/shard_map/pallas_call | solution.py:271
  140.6 20.3 %shard_map.65.a_ref = f32[8,256]{1,0:T(8,128)} custom-call(bf16[2048,128]{1,0:T(8,128)(2,1)} %bitcast.16, bf16[4096,128]{1,0:T(8,128)(2,1)} %bitcast.9, f32[8,512]{1,0:T(8,128)} %shard_map.64.a_ref.u_ref, f32[8,256]{1,0:T(8,128)} %get-tuple-element.10.b_ref, f32[8,256]{1,0:T(8,128)} %reshape.28.m_ref, f32[8,256]{1,0:T(8,128)} %copy-done.1), custom_call_target="tpu_custom_call" | custom-call | tf_op jit(solution)/shard_map/pallas_call | solution.py:271
  160.9 55.6 %shard_map.66 = (f32[256,128]{1,0:T(8,128)}, f32[256,128]{1,0:T(8,128)}) custom-call(bf16[4096,128]{1,0:T(8,128)(2,1)} %bitcast.10, bf16[2048,128]{1,0:T(8,128)(2,1)} %bitcast.17, f32[8,512]{1,0:T(8,128)} %shard_map.64.a_ref.u_ref, f32[8,256]{1,0:T(8,128)} %shard_map.65.a_ref), custom_call_target="tpu_custom_call" | custom-call | tf_op jit(solution)/shard_map/pallas_call | solution.py:179
  216.6 1.6 copy.8
  218.1 1.6 copy.9
  (1 shorter events, 0.0 us)
Async XLA Ops:
  26.9 26.0 %copy-start.1 = (f32[8,256]{1,0:T(8,128)}, f32[8,256]{1,0:T(8,128)S(1)}, u32[]{:S(2)}) copy-start(f32[8,256]{1,0:T(8,128)S(1)} %multiply_reduce_fusion.1.s_ref) | copy-start | bytes 24580
  28.7 1.2 copy-start

commit v10 on v9

--- a/solution.py
+++ b/solution.py
@@ -117,7 +117,6 @@
     for d in range(1, n_row):
         pl.semaphore_signal(barrier, inc=1, device_id=_peer("row", lax.rem(me_r + d, n_row)),
                             device_id_type=pl.DeviceIdType.MESH)
-    pl.semaphore_wait(barrier, n_col + n_row - 2)
 
     def to_col_dev(k, slot):
         return pltpu.make_async_remote_copy(
@@ -154,6 +153,8 @@
         for s in range(per):
             gi[i * per + s] = g[s * m:(s + 1) * m]
         pc[...] += lax.dot_general(plan, x, TN, preferred_element_type=jnp.float32)
+        if i == 1:
+            pl.semaphore_wait(barrier, n_col + n_row - 2)
         if i >= 1:
             for s in range((i - 1) * per, i * per):
                 pl.when(me_c != s)(functools.partial(lambda k: to_col_dev(k, me_c).start(), s))
@@ -206,7 +207,6 @@
     for d in range(1, n):
         pl.semaphore_signal(barrier, inc=1, device_id=_peer(axis, lax.rem(me + d, n)),
                             device_id_type=pl.DeviceIdType.MESH)
-    pl.semaphore_wait(barrier, n - 1)
 
     def out_copy(c, d):
         return pltpu.make_async_remote_copy(
@@ -242,6 +242,7 @@
 
         @pl.when(i == half)
         def _():
+            pl.semaphore_wait(barrier, n - 1)
             send_half(0)
 
         return carry

time: 222 us -> 204 us (0.919)
  Pallas kernels: 209 us -> 193 us
    pallas_call x6, Pallas kernels: 131 us -> 117 us  [lse_combine(): pl.pallas_call(functools.partial(_lse_combine_kernel, axis, n), out_shape...]
    pallas_call x1, Pallas kernels: 55.6 us -> 53.3 us  [plan_scatter(): pl.pallas_call(functools.partial(_plan_scatter_kernel, n_col, n_row), out...]
where the time goes in v10:
time: 204 us
  Pallas kernels  193 us (95%)
  local copies, waits for them, and re-layouts  5.79 us (3%)
  other arithmetic  4.43 us (2%)
    pallas_call x6, Pallas kernels, lse_combine(): pl.pallas_call(functools.partial(_lse_combine_kernel, axis, n), out_shape...  117 us
    pallas_call x1, Pallas kernels, plan_scatter(): pl.pallas_call(functools.partial(_plan_scatter_kernel, n_col, n_row), out...  53.3 us
    pallas_call x1, Pallas kernels, exchange(): pl.pallas_call(functools.partial(_exchange_kernel, tuple(jobs)), out_shap...  22.2 us

profile of v10, /device:TPU:116, one launch (start us, length us, event | category | flops | bytes accessed | tf_op | source)
XLA Modules:
  0.0 203.7 jit_solution(17005473943337389528)
XLA Ops:
  0.6 0.7 log.7
  1.3 0.6 reshape.28.m_ref
  1.9 0.7 log.6
  2.7 0.6 reshape.27.m_ref
  3.3 22.2 %shard_map.59 = (bf16[16,256,128]{2,1,0:T(8,128)(2,1)}, bf16[8,256,128]{2,1,0:T(8,128)(2,1)}) custom-call(bf16[256,128]{1,0:T(8,128)(2,1)} %refs_0_.1, bf16[256,128]{1,0:T(8,128)(2,1)} %bitcast.19), custom_call_target="tpu_custom_call" | custom-call | tf_op jit(solution)/shard_map/pallas_call | solution.py:375
  25.5 1.4 multiply_reduce_fusion.1.s_ref
  26.9 0.0 copy-start.1
  26.9 1.8 multiply_reduce_fusion
  28.7 0.0 copy-start
  28.7 0.6 broadcast_multiply_fusion.b_ref
  29.3 0.6 broadcast_multiply_fusion.1
  29.9 0.0 copy-done
  29.9 20.5 %shard_map.60.a_ref = f32[8,512]{1,0:T(8,128)} custom-call(bf16[4096,128]{1,0:T(8,128)(2,1)} %bitcast.4, bf16[2048,128]{1,0:T(8,128)(2,1)} %bitcast.11, f32[8,256]{1,0:T(8,128)} %get-tuple-element.11.a_ref, f32[8,512]{1,0:T(8,128)} %broadcast_multiply_fusion.b_ref, f32[8,512]{1,0:T(8,128)} %reshape.27.m_ref, f32[8,512]{1,0:T(8,128)} %copy-done), custom_call_target="tpu_custom_call" | custom-call | tf_op jit(solution)/shard_map/pallas_call | solution.py:272
  50.4 0.0 copy-done.1
  50.4 18.5 %shard_map.61.a_ref = f32[8,256]{1,0:T(8,128)} custom-call(bf16[2048,128]{1,0:T(8,128)(2,1)} %bitcast.12, bf16[4096,128]{1,0:T(8,128)(2,1)} %bitcast.5, f32[8,512]{1,0:T(8,128)} %shard_map.60.a_ref, f32[8,256]{1,0:T(8,128)} %get-tuple-element.10.b_ref, f32[8,256]{1,0:T(8,128)} %reshape.28.m_ref, f32[8,256]{1,0:T(8,128)} %copy-done.1), custom_call_target="tpu_custom_call" | custom-call | tf_op jit(solution)/shard_map/pallas_call | solution.py:272
  68.9 20.7 %shard_map.62.a_ref = f32[8,512]{1,0:T(8,128)} custom-call(bf16[4096,128]{1,0:T(8,128)(2,1)} %bitcast.6, bf16[2048,128]{1,0:T(8,128)(2,1)} %bitcast.13, f32[8,256]{1,0:T(8,128)} %shard_map.61.a_ref, f32[8,512]{1,0:T(8,128)} %broadcast_multiply_fusion.b_ref, f32[8,512]{1,0:T(8,128)} %reshape.27.m_ref, f32[8,512]{1,0:T(8,128)} %copy-done), custom_call_target="tpu_custom_call" | custom-call | tf_op jit(solution)/shard_map/pallas_call | solution.py:272
  89.7 18.3 %shard_map.63.a_ref = f32[8,256]{1,0:T(8,128)} custom-call(bf16[2048,128]{1,0:T(8,128)(2,1)} %bitcast.14, bf16[4096,128]{1,0:T(8,128)(2,1)} %bitcast.7, f32[8,512]{1,0:T(8,128)} %shard_map.62.a_ref, f32[8,256]{1,0:T(8,128)} %get-tuple-element.10.b_ref, f32[8,256]{1,0:T(8,128)} %reshape.28.m_ref, f32[8,256]{1,0:T(8,128)} %copy-done.1), custom_call_target="tpu_custom_call" | custom-call | tf_op jit(solution)/shard_map/pallas_call | solution.py:272
  107.9 20.7 %shard_map.64.a_ref.u_ref = f32[8,512]{1,0:T(8,128)} custom-call(bf16[4096,128]{1,0:T(8,128)(2,1)} %bitcast.8, bf16[2048,128]{1,0:T(8,128)(2,1)} %bitcast.15, f32[8,256]{1,0:T(8,128)} %shard_map.63.a_ref, f32[8,512]{1,0:T(8,128)} %broadcast_multiply_fusion.b_ref, f32[8,512]{1,0:T(8,128)} %reshape.27.m_ref, f32[8,512]{1,0:T(8,128)} %copy-done), custom_call_target="tpu_custom_call" | custom-call | tf_op jit(solution)/shard_map/pallas_call | solution.py:272
  128.6 18.7 %shard_map.65.a_ref = f32[8,256]{1,0:T(8,128)} custom-call(bf16[2048,128]{1,0:T(8,128)(2,1)} %bitcast.16, bf16[4096,128]{1,0:T(8,128)(2,1)} %bitcast.9, f32[8,512]{1,0:T(8,128)} %shard_map.64.a_ref.u_ref, f32[8,256]{1,0:T(8,128)} %get-tuple-element.10.b_ref, f32[8,256]{1,0:T(8,128)} %reshape.28.m_ref, f32[8,256]{1,0:T(8,128)} %copy-done.1), custom_call_target="tpu_custom_call" | custom-call | tf_op jit(solution)/shard_map/pallas_call | solution.py:272
  147.3 53.3 %shard_map.66 = (f32[256,128]{1,0:T(8,128)}, f32[256,128]{1,0:T(8,128)}) custom-call(bf16[4096,128]{1,0:T(8,128)(2,1)} %bitcast.10, bf16[2048,128]{1,0:T(8,128)(2,1)} %bitcast.17, f32[8,512]{1,0:T(8,128)} %shard_map.64.a_ref.u_ref, f32[8,256]{1,0:T(8,128)} %shard_map.65.a_ref), custom_call_target="tpu_custom_call" | custom-call | tf_op jit(solution)/shard_map/pallas_call | solution.py:180
  200.6 1.6 copy.8
  202.2 1.6 copy.9
  (1 shorter events, 0.0 us)
Async XLA Ops:
  26.9 23.6 %copy-start.1 = (f32[8,256]{1,0:T(8,128)}, f32[8,256]{1,0:T(8,128)S(1)}, u32[]{:S(2)}) copy-start(f32[8,256]{1,0:T(8,128)S(1)} %multiply_reduce_fusion.1.s_ref) | copy-start | bytes 24580
  28.7 1.2 copy-start

commit v11 on v10

--- a/solution.py
+++ b/solution.py
@@ -200,7 +200,7 @@
     )(x, y, u, a)
 
 
-def _lse_combine_kernel(axis, n, p_ref, q_ref, a_ref, b_ref, m_ref, s_ref, o_ref,
+def _lse_combine_kernel(axis, n, p_ref, q_ref, a_ref, m_ref, s_ref, o_ref,
                         part, buf, send, recv):
     me = lax.axis_index(axis)
     barrier = pltpu.get_barrier_semaphore()
@@ -237,7 +237,7 @@
         t = a2 + SCALE2 * cross
         top = jnp.max(t, axis=1, keepdims=True)
         total = jnp.sum(jnp.exp2(t - top), axis=1, keepdims=True)
-        row = _to_row(top * LN2 + jnp.log(total)) - b_ref[pl.ds(i, 1), :]
+        row = _to_row(top * LN2 + jnp.log(total)) - s_ref[pl.ds(i, 1), :] * INV
         part.at[i // half][pl.ds(i % half, 1), :] = row
 
         @pl.when(i == half)
@@ -266,13 +266,13 @@
     finish(1)
 
 
-def lse_combine(p, q, a, b, log_mass, sq, axis):
+def lse_combine(p, q, a, log_mass, sq, axis):
     n = lax.axis_size(axis)
     m = p.shape[0] // 8
     return pl.pallas_call(
         functools.partial(_lse_combine_kernel, axis, n),
         out_shape=jax.ShapeDtypeStruct((8, m), jnp.float32),
-        in_specs=[pl.BlockSpec(memory_space=pltpu.VMEM)] * 6,
+        in_specs=[pl.BlockSpec(memory_space=pltpu.VMEM)] * 5,
         out_specs=pl.BlockSpec(memory_space=pltpu.VMEM),
         scratch_shapes=[
             pltpu.VMEM((2, 4, m), jnp.float32),
@@ -283,7 +283,7 @@
         compiler_params=pltpu.CompilerParams(
             collective_id=5 if axis == "col" else 6, has_side_effects=True,
             vmem_limit_bytes=VMEM_LIMIT),
-    )(p, q, a, b, log_mass, sq)
+    )(p, q, a, log_mass, sq)
 
 
 def squares(values):
@@ -327,7 +327,10 @@
 def _exchange_kernel(jobs, *refs):
     count = len(jobs)
     ins, outs = refs[:count], refs[count:2 * count]
-    bufs, sends, recvs = refs[2 * count::3], refs[2 * count + 1::3], refs[2 * count + 2::3]
+    gathers = sum(kind == "gather" for _, _, kind in jobs)
+    sqs = refs[2 * count:2 * count + gathers]
+    rest = refs[2 * count + gathers:]
+    bufs, sends, recvs = rest[0::3], rest[1::3], rest[2::3]
     barrier = pltpu.get_barrier_semaphore()
     for axis, n, kind in jobs:
         me = lax.axis_index(axis)
@@ -360,6 +363,13 @@
         if kind == "gather":
             bufs[job][me] = ins[job][...]
             outs[job][...] = bufs[job][...]
+            sq = sqs[job]
+            m = bufs[job].shape[1]
+            per = sq.shape[1] // m
+            for j in range(n):
+                v = bufs[job][j].astype(jnp.float32)
+                row = _to_row(jnp.sum(v * v, axis=1, keepdims=True))
+                sq[j // per:j // per + 1, (j % per) * m:(j % per + 1) * m] = row
         else:
             bufs[job][me] = ins[job][me]
             outs[job][...] = jnp.sum(bufs[job][...], axis=0)
@@ -372,11 +382,14 @@
         shapes.append(jax.ShapeDtypeStruct((n,) + block if kind == "gather" else block, x.dtype))
         scratch += [pltpu.VMEM((n,) + block, x.dtype), pltpu.SemaphoreType.DMA((n,)),
                     pltpu.SemaphoreType.DMA((n,))]
+    for (axis, n, kind), x in zip(jobs, arrays):
+        if kind == "gather":
+            shapes.append(jax.ShapeDtypeStruct((8, n * x.shape[0] // 8), jnp.float32))
     return pl.pallas_call(
         functools.partial(_exchange_kernel, tuple(jobs)),
         out_shape=tuple(shapes),
         in_specs=[pl.BlockSpec(memory_space=pltpu.VMEM)] * len(jobs),
-        out_specs=tuple(pl.BlockSpec(memory_space=pltpu.VMEM) for _ in jobs),
+        out_specs=tuple(pl.BlockSpec(memory_space=pltpu.VMEM) for _ in shapes),
         scratch_shapes=scratch,
         compiler_params=pltpu.CompilerParams(
             collective_id=collective_id, has_side_effects=True, vmem_limit_bytes=VMEM_LIMIT),
@@ -402,21 +415,17 @@
 
 def local(imu, camera, imu_mass, cam_mass):
     n_col, n_row = lax.axis_size("col"), lax.axis_size("row")
-    imu_rows, cam_rows = exchange(
+    imu_rows, cam_rows, rows_sq, cols_sq = exchange(
         [("col", n_col, "gather"), ("row", n_row, "gather")], [imu, camera[0]], 3)
     imu_rows = imu_rows.reshape(-1, D)
     cam_rows = cam_rows.reshape(-1, D)
-    rows_sq = squares(imu_rows).reshape(8, -1)
-    cols_sq = squares(cam_rows).reshape(8, -1)
     log_a = jnp.log(imu_mass).reshape(8, -1)
     log_b = jnp.log(cam_mass).reshape(8, -1)
-    row_b = rows_sq * INV
-    col_b = cols_sq * INV
-
-    a = -col_b
+
+    a = -cols_sq * INV
     for step in range(ITERS):
-        u = lse_combine(imu_rows, cam_rows, a, row_b, log_a, rows_sq, "col")
-        a = lse_combine(cam_rows, imu_rows, u, col_b, log_b, cols_sq, "row")
+        u = lse_combine(imu_rows, cam_rows, a, log_a, rows_sq, "col")
+        a = lse_combine(cam_rows, imu_rows, u, log_b, cols_sq, "row")
 
     grad_imu, grad_cam = plan_scatter(imu_rows, cam_rows, u, a, n_col, n_row)
     return (grad_imu, grad_cam[None])

time: 204 us -> 201 us (0.985)
  other arithmetic: 4.43 us -> 0.6 us
    reduce_sum x2 -> x0, other arithmetic: 3.22 us -> none  [squares(): return jnp.sum(jnp.square(values.astype(jnp.float32)), axis=1)]
where the time goes in v11:
time: 201 us; the launch traced here: 200 us
  Pallas kernels  194 us (97%)
  local copies, waits for them, and re-layouts  4.88 us (2%)
    pallas_call x6, Pallas kernels, lse_combine(): pl.pallas_call(functools.partial(_lse_combine_kernel, axis, n), out_shape...  117 us
    pallas_call x1, Pallas kernels, plan_scatter(): pl.pallas_call(functools.partial(_plan_scatter_kernel, n_col, n_row), out...  53.3 us
    pallas_call x1, Pallas kernels, exchange(): pl.pallas_call(functools.partial(_exchange_kernel, tuple(jobs)), out_shap...  23.5 us

profile of v11, /device:TPU:116, one launch (start us, length us, event | category | flops | bytes accessed | tf_op | source)
XLA Modules:
  0.0 200.1 jit_solution(5292973410627792659)
XLA Ops:
  0.6 0.0 copy-start.2
  0.6 0.7 log.7
  1.3 0.6 reshape.19.m_ref
  1.9 0.0 copy-done.2
  2.0 0.6 reshape.18.m_ref
  2.6 23.5 %shard_map.59 = (bf16[16,256,128]{2,1,0:T(8,128)(2,1)}, bf16[8,256,128]{2,1,0:T(8,128)(2,1)}, f32[8,512]{1,0:T(8,128)}, f32[8,256]{1,0:T(8,128)}) custom-call(bf16[256,128]{1,0:T(8,128)(2,1)} %refs_0_.1, bf16[256,128]{1,0:T(8,128)(2,1)} %bitcast.19), custom_call_target="tpu_custom_call" | custom-call | tf_op jit(solution)/shard_map/pallas_call | solution.py:388
  26.1 0.0 copy-start
  26.1 0.7 copy-done
  26.8 0.6 negate_multiply_fusion.a_ref
  27.4 20.4 %shard_map.60.a_ref = f32[8,512]{1,0:T(8,128)} custom-call(bf16[4096,128]{1,0:T(8,128)(2,1)} %bitcast.4, bf16[2048,128]{1,0:T(8,128)(2,1)} %bitcast.11, f32[8,256]{1,0:T(8,128)} %negate_multiply_fusion.a_ref, f32[8,512]{1,0:T(8,128)} %reshape.18.m_ref, f32[8,512]{1,0:T(8,128)} %get-tuple-element.11.s_ref), custom_call_target="tpu_custom_call" | custom-call | tf_op jit(solution)/shard_map/pallas_call | solution.py:272
  47.9 18.5 %shard_map.61.a_ref = f32[8,256]{1,0:T(8,128)} custom-call(bf16[2048,128]{1,0:T(8,128)(2,1)} %bitcast.12, bf16[4096,128]{1,0:T(8,128)(2,1)} %bitcast.5, f32[8,512]{1,0:T(8,128)} %shard_map.60.a_ref, f32[8,256]{1,0:T(8,128)} %reshape.19.m_ref, f32[8,256]{1,0:T(8,128)} %get-tuple-element.10.s_ref), custom_call_target="tpu_custom_call" | custom-call | tf_op jit(solution)/shard_map/pallas_call | solution.py:272
  66.3 20.7 %shard_map.62.a_ref = f32[8,512]{1,0:T(8,128)} custom-call(bf16[4096,128]{1,0:T(8,128)(2,1)} %bitcast.6, bf16[2048,128]{1,0:T(8,128)(2,1)} %bitcast.13, f32[8,256]{1,0:T(8,128)} %shard_map.61.a_ref, f32[8,512]{1,0:T(8,128)} %reshape.18.m_ref, f32[8,512]{1,0:T(8,128)} %get-tuple-element.11.s_ref), custom_call_target="tpu_custom_call" | custom-call | tf_op jit(solution)/shard_map/pallas_call | solution.py:272
  87.0 18.2 %shard_map.63.a_ref = f32[8,256]{1,0:T(8,128)} custom-call(bf16[2048,128]{1,0:T(8,128)(2,1)} %bitcast.14, bf16[4096,128]{1,0:T(8,128)(2,1)} %bitcast.7, f32[8,512]{1,0:T(8,128)} %shard_map.62.a_ref, f32[8,256]{1,0:T(8,128)} %reshape.19.m_ref, f32[8,256]{1,0:T(8,128)} %get-tuple-element.10.s_ref), custom_call_target="tpu_custom_call" | custom-call | tf_op jit(solution)/shard_map/pallas_call | solution.py:272
  105.3 20.6 %shard_map.64.a_ref.u_ref = f32[8,512]{1,0:T(8,128)} custom-call(bf16[4096,128]{1,0:T(8,128)(2,1)} %bitcast.8, bf16[2048,128]{1,0:T(8,128)(2,1)} %bitcast.15, f32[8,256]{1,0:T(8,128)} %shard_map.63.a_ref, f32[8,512]{1,0:T(8,128)} %reshape.18.m_ref, f32[8,512]{1,0:T(8,128)} %get-tuple-element.11.s_ref), custom_call_target="tpu_custom_call" | custom-call | tf_op jit(solution)/shard_map/pallas_call | solution.py:272
  125.9 18.7 %shard_map.65.a_ref = f32[8,256]{1,0:T(8,128)} custom-call(bf16[2048,128]{1,0:T(8,128)(2,1)} %bitcast.16, bf16[4096,128]{1,0:T(8,128)(2,1)} %bitcast.9, f32[8,512]{1,0:T(8,128)} %shard_map.64.a_ref.u_ref, f32[8,256]{1,0:T(8,128)} %reshape.19.m_ref, f32[8,256]{1,0:T(8,128)} %get-tuple-element.10.s_ref), custom_call_target="tpu_custom_call" | custom-call | tf_op jit(solution)/shard_map/pallas_call | solution.py:272
  144.6 53.3 %shard_map.66 = (f32[256,128]{1,0:T(8,128)}, f32[256,128]{1,0:T(8,128)}) custom-call(bf16[4096,128]{1,0:T(8,128)(2,1)} %bitcast.10, bf16[2048,128]{1,0:T(8,128)(2,1)} %bitcast.17, f32[8,512]{1,0:T(8,128)} %shard_map.64.a_ref.u_ref, f32[8,256]{1,0:T(8,128)} %shard_map.65.a_ref), custom_call_target="tpu_custom_call" | custom-call | tf_op jit(solution)/shard_map/pallas_call | solution.py:180
  197.9 0.0 copy-start.1
  197.9 1.6 copy.8
  199.5 0.0 copy-done.1
  199.5 0.7 copy.9
  (1 shorter events, 0.0 us)
Async XLA Ops:
  0.6 1.3 copy-start.2
  26.1 0.7 copy-start
  197.9 1.6 copy-start.1

commit v12 on v11

--- a/solution.py
+++ b/solution.py
@@ -286,6 +286,127 @@
     )(p, q, a, log_mass, sq)
 
 
+def _first_kernel(n, x_ref, q_ref, a_ref, m_ref, o_ref, rows_out, sq_out,
+                  gbuf, sqs, part, buf, send, recv, gsend, grecv):
+    axis = "col"
+    me = lax.axis_index(axis)
+    barrier = pltpu.get_barrier_semaphore()
+    for d in range(1, n):
+        pl.semaphore_signal(barrier, inc=1, device_id=_peer(axis, lax.rem(me + d, n)),
+                            device_id_type=pl.DeviceIdType.MESH)
+    pl.semaphore_wait(barrier, n - 1)
+
+    def gather_copy(d, slot):
+        return pltpu.make_async_remote_copy(
+            src_ref=x_ref, dst_ref=gbuf.at[slot], send_sem=gsend.at[d], recv_sem=grecv.at[slot],
+            device_id=_peer(axis, lax.rem(me + d, n)), device_id_type=pl.DeviceIdType.MESH)
+
+    for d in range(1, n):
+        gather_copy(d, me).start()
+    gbuf[me] = x_ref[...]
+
+    def out_copy(c, d):
+        return pltpu.make_async_remote_copy(
+            src_ref=part.at[c], dst_ref=buf.at[me, c], send_sem=send.at[c, d],
+            recv_sem=recv.at[c, me], device_id=_peer(axis, lax.rem(me + d, n)),
+            device_id_type=pl.DeviceIdType.MESH)
+
+    def in_copy(c, d):
+        src = lax.rem(me + n - d, n)
+        return pltpu.make_async_remote_copy(
+            src_ref=part.at[c], dst_ref=buf.at[src, c], send_sem=send.at[c, d],
+            recv_sem=recv.at[c, src], device_id=_peer(axis, src),
+            device_id_type=pl.DeviceIdType.MESH)
+
+    def send_half(c):
+        for d in range(1, n):
+            out_copy(c, d).start()
+
+    half = part.shape[1]
+    m = x_ref.shape[0]
+    tile = sqs.shape[1]
+    per = tile // m
+    q = q_ref[...]
+    a2 = _row_of(a_ref[...]) * LOG2E
+
+    def body(i, carry):
+        for s in range(per):
+            slot = i * per + s
+
+            @pl.when(slot != me)
+            def _():
+                d = lax.rem(me + n - slot, n)
+                pltpu.make_async_remote_copy(
+                    src_ref=x_ref, dst_ref=gbuf.at[slot], send_sem=gsend.at[d],
+                    recv_sem=grecv.at[slot], device_id=_peer(axis, slot),
+                    device_id_type=pl.DeviceIdType.MESH).wait_recv()
+
+        p = jnp.concatenate([gbuf[i * per + s] for s in range(per)], axis=0)
+        v = p.astype(jnp.float32)
+        sq = _to_row(jnp.sum(v * v, axis=1, keepdims=True))
+        sqs[pl.ds(i, 1), :] = sq
+        cross = lax.dot_general(p, q, NT, preferred_element_type=jnp.float32)
+        t = a2 + SCALE2 * cross
+        top = jnp.max(t, axis=1, keepdims=True)
+        total = jnp.sum(jnp.exp2(t - top), axis=1, keepdims=True)
+        row = _to_row(top * LN2 + jnp.log(total)) - sq * INV
+        part.at[i // half][pl.ds(i % half, 1), :] = row
+
+        @pl.when(i == half)
+        def _():
+            send_half(0)
+
+        return carry
+
+    lax.fori_loop(0, 2 * half, body, 0)
+
+    def finish(c):
+        for d in range(1, n):
+            out_copy(c, d).wait_send()
+        for d in range(1, n):
+            in_copy(c, d).wait_recv()
+        buf[me, c] = part[c]
+        parts = buf[:, c]
+        top = jnp.max(parts, axis=0)
+        total = top + jnp.log(jnp.sum(jnp.exp(parts - top[None]), axis=0))
+        rows = slice(c * half, (c + 1) * half)
+        o_ref[rows, :] = (EPS * (m_ref[rows, :] - total) - sqs[rows, :]) * INV
+
+    finish(0)
+    send_half(1)
+    finish(1)
+    for d in range(1, n):
+        gather_copy(d, me).wait_send()
+    rows_out[...] = gbuf[...]
+    sq_out[...] = sqs[...]
+
+
+def first_lse(x, q, a, log_mass):
+    n = lax.axis_size("col")
+    m = x.shape[0]
+    tile = n * m // 8
+    return pl.pallas_call(
+        functools.partial(_first_kernel, n),
+        out_shape=(jax.ShapeDtypeStruct((8, tile), jnp.float32),
+                   jax.ShapeDtypeStruct((n, m, D), x.dtype),
+                   jax.ShapeDtypeStruct((8, tile), jnp.float32)),
+        in_specs=[pl.BlockSpec(memory_space=pltpu.VMEM)] * 4,
+        out_specs=(pl.BlockSpec(memory_space=pltpu.VMEM),) * 3,
+        scratch_shapes=[
+            pltpu.VMEM((n, m, D), x.dtype),
+            pltpu.VMEM((8, tile), jnp.float32),
+            pltpu.VMEM((2, 4, tile), jnp.float32),
+            pltpu.VMEM((n, 2, 4, tile), jnp.float32),
+            pltpu.SemaphoreType.DMA((2, n)),
+            pltpu.SemaphoreType.DMA((2, n)),
+            pltpu.SemaphoreType.DMA((n,)),
+            pltpu.SemaphoreType.DMA((n,)),
+        ],
+        compiler_params=pltpu.CompilerParams(
+            collective_id=7, has_side_effects=True, vmem_limit_bytes=VMEM_LIMIT),
+    )(x, q, a, log_mass)
+
+
 def squares(values):
     return jnp.sum(jnp.square(values.astype(jnp.float32)), axis=1)
 
@@ -415,15 +536,16 @@
 
 def local(imu, camera, imu_mass, cam_mass):
     n_col, n_row = lax.axis_size("col"), lax.axis_size("row")
-    imu_rows, cam_rows, rows_sq, cols_sq = exchange(
-        [("col", n_col, "gather"), ("row", n_row, "gather")], [imu, camera[0]], 3)
-    imu_rows = imu_rows.reshape(-1, D)
+    cam_rows, cols_sq = exchange([("row", n_row, "gather")], [camera[0]], 3)
     cam_rows = cam_rows.reshape(-1, D)
     log_a = jnp.log(imu_mass).reshape(8, -1)
     log_b = jnp.log(cam_mass).reshape(8, -1)
 
     a = -cols_sq * INV
-    for step in range(ITERS):
+    u, imu_rows, rows_sq = first_lse(imu, cam_rows, a, log_a)
+    imu_rows = imu_rows.reshape(-1, D)
+    a = lse_combine(cam_rows, imu_rows, u, log_b, cols_sq, "row")
+    for step in range(1, ITERS):
         u = lse_combine(imu_rows, cam_rows, a, log_a, rows_sq, "col")
         a = lse_combine(cam_rows, imu_rows, u, log_b, cols_sq, "row")
 

time: 201 us -> 217 us (1.080); the launches traced: 200 us -> 214 us
  Pallas kernels: 194 us -> 208 us
    pallas_call x0 -> x1, Pallas kernels: none -> 42.8 us  [first_lse(): pl.pallas_call(functools.partial(_first_kernel, n), out_shape=(jax.ShapeD...]
    pallas_call x6 -> x5, Pallas kernels: 117 us -> 96.4 us  [lse_combine(): pl.pallas_call(functools.partial(_lse_combine_kernel, axis, n), out_shape...]
    pallas_call x1, Pallas kernels: 23.5 us -> 11.6 us  [exchange(): pl.pallas_call(functools.partial(_exchange_kernel, tuple(jobs)), out_shap...]
    pallas_call x1, Pallas kernels: 53.3 us -> 57 us  [plan_scatter(): pl.pallas_call(functools.partial(_plan_scatter_kernel, n_col, n_row), out...]
where the time goes in v12:
time: 217 us; the launch traced here: 214 us
  Pallas kernels  208 us (96%)
  local copies, waits for them, and re-layouts  4.2 us (2%)
    pallas_call x5, Pallas kernels, lse_combine(): pl.pallas_call(functools.partial(_lse_combine_kernel, axis, n), out_shape...  96.4 us
    pallas_call x1, Pallas kernels, plan_scatter(): pl.pallas_call(functools.partial(_plan_scatter_kernel, n_col, n_row), out...  57 us
    pallas_call x1, Pallas kernels, first_lse(): pl.pallas_call(functools.partial(_first_kernel, n), out_shape=(jax.ShapeD...  42.8 us
    pallas_call x1, Pallas kernels, exchange(): pl.pallas_call(functools.partial(_exchange_kernel, tuple(jobs)), out_shap...  11.6 us

profile of v12, /device:TPU:116, one launch (start us, length us, event | category | flops | bytes accessed | tf_op | source)
XLA Modules:
  0.0 213.9 jit_solution(10849877039160288307)
XLA Ops:
  0.6 0.0 copy-start.1
  0.6 0.7 log.7
  1.3 0.6 reshape.19.m_ref
  2.0 0.0 copy-done.1
  2.0 0.6 reshape.17.m_ref
  2.6 11.6 %shard_map.59 = (bf16[8,256,128]{2,1,0:T(8,128)(2,1)}, f32[8,256]{1,0:T(8,128)}) custom-call(bf16[256,128]{1,0:T(8,128)(2,1)} %bitcast.18), custom_call_target="tpu_custom_call" | custom-call | tf_op jit(solution)/shard_map/pallas_call | solution.py:509
  14.2 1.3 negate_multiply_fusion.a_ref
  15.5 42.8 %shard_map.60 = (f32[8,512]{1,0:T(8,128)}, bf16[16,256,128]{2,1,0:T(8,128)(2,1)}, f32[8,512]{1,0:T(8,128)}) custom-call(bf16[256,128]{1,0:T(8,128)(2,1)} %x_ref.1, bf16[2048,128]{1,0:T(8,128)(2,1)} %bitcast.10, f32[8,256]{1,0:T(8,128)} %negate_multiply_fusion.a_ref, f32[8,512]{1,0:T(8,128)} %reshape.17.m_ref), custom_call_target="tpu_custom_call" | custom-call | tf_op jit(solution)/shard_map/pallas_call | solution.py:388
  58.2 18.2 %shard_map.61.a_ref = f32[8,256]{1,0:T(8,128)} custom-call(bf16[2048,128]{1,0:T(8,128)(2,1)} %bitcast.11, bf16[4096,128]{1,0:T(8,128)(2,1)} %bitcast.4, f32[8,512]{1,0:T(8,128)} %get-tuple-element.12.a_ref, f32[8,256]{1,0:T(8,128)} %reshape.19.m_ref, f32[8,256]{1,0:T(8,128)} %get-tuple-element.10.s_ref), custom_call_target="tpu_custom_call" | custom-call | tf_op jit(solution)/shard_map/pallas_call | solution.py:272
  76.5 20.6 %shard_map.62.a_ref = f32[8,512]{1,0:T(8,128)} custom-call(bf16[4096,128]{1,0:T(8,128)(2,1)} %bitcast.5, bf16[2048,128]{1,0:T(8,128)(2,1)} %bitcast.12, f32[8,256]{1,0:T(8,128)} %shard_map.61.a_ref, f32[8,512]{1,0:T(8,128)} %reshape.17.m_ref, f32[8,512]{1,0:T(8,128)} %get-tuple-element.13.s_ref), custom_call_target="tpu_custom_call" | custom-call | tf_op jit(solution)/shard_map/pallas_call | solution.py:272
  97.1 18.6 %shard_map.63.a_ref = f32[8,256]{1,0:T(8,128)} custom-call(bf16[2048,128]{1,0:T(8,128)(2,1)} %bitcast.13, bf16[4096,128]{1,0:T(8,128)(2,1)} %bitcast.6, f32[8,512]{1,0:T(8,128)} %shard_map.62.a_ref, f32[8,256]{1,0:T(8,128)} %reshape.19.m_ref, f32[8,256]{1,0:T(8,128)} %get-tuple-element.10.s_ref), custom_call_target="tpu_custom_call" | custom-call | tf_op jit(solution)/shard_map/pallas_call | solution.py:272
  115.7 20.6 %shard_map.64.a_ref.u_ref = f32[8,512]{1,0:T(8,128)} custom-call(bf16[4096,128]{1,0:T(8,128)(2,1)} %bitcast.7, bf16[2048,128]{1,0:T(8,128)(2,1)} %bitcast.14, f32[8,256]{1,0:T(8,128)} %shard_map.63.a_ref, f32[8,512]{1,0:T(8,128)} %reshape.17.m_ref, f32[8,512]{1,0:T(8,128)} %get-tuple-element.13.s_ref), custom_call_target="tpu_custom_call" | custom-call | tf_op jit(solution)/shard_map/pallas_call | solution.py:272
  136.4 18.3 %shard_map.65.a_ref = f32[8,256]{1,0:T(8,128)} custom-call(bf16[2048,128]{1,0:T(8,128)(2,1)} %bitcast.15, bf16[4096,128]{1,0:T(8,128)(2,1)} %bitcast.8, f32[8,512]{1,0:T(8,128)} %shard_map.64.a_ref.u_ref, f32[8,256]{1,0:T(8,128)} %reshape.19.m_ref, f32[8,256]{1,0:T(8,128)} %get-tuple-element.10.s_ref), custom_call_target="tpu_custom_call" | custom-call | tf_op jit(solution)/shard_map/pallas_call | solution.py:272
  154.7 57.0 %shard_map.66 = (f32[256,128]{1,0:T(8,128)}, f32[256,128]{1,0:T(8,128)}) custom-call(bf16[4096,128]{1,0:T(8,128)(2,1)} %bitcast.9, bf16[2048,128]{1,0:T(8,128)(2,1)} %bitcast.16, f32[8,512]{1,0:T(8,128)} %shard_map.64.a_ref.u_ref, f32[8,256]{1,0:T(8,128)} %shard_map.65.a_ref), custom_call_target="tpu_custom_call" | custom-call | tf_op jit(solution)/shard_map/pallas_call | solution.py:180
  211.7 0.0 copy-start
  211.7 1.6 copy.8
  213.3 0.0 copy-done
  213.3 0.7 copy.9
  (1 shorter events, 0.0 us)
Async XLA Ops:
  0.6 1.3 copy-start.1
  211.7 1.6 copy-start

commit v13 on v11

--- a/solution.py
+++ b/solution.py
@@ -259,14 +259,14 @@
         top = jnp.max(parts, axis=0)
         total = top + jnp.log(jnp.sum(jnp.exp(parts - top[None]), axis=0))
         rows = slice(c * half, (c + 1) * half)
-        o_ref[rows, :] = (EPS * (m_ref[rows, :] - total) - s_ref[rows, :]) * INV
+        o_ref[rows, :] = (EPS * (jnp.log(m_ref[rows, :]) - total) - s_ref[rows, :]) * INV
 
     finish(0)
     send_half(1)
     finish(1)
 
 
-def lse_combine(p, q, a, log_mass, sq, axis):
+def lse_combine(p, q, a, mass, sq, axis):
     n = lax.axis_size(axis)
     m = p.shape[0] // 8
     return pl.pallas_call(
@@ -283,7 +283,7 @@
         compiler_params=pltpu.CompilerParams(
             collective_id=5 if axis == "col" else 6, has_side_effects=True,
             vmem_limit_bytes=VMEM_LIMIT),
-    )(p, q, a, log_mass, sq)
+    )(p, q, a, mass, sq)
 
 
 def squares(values):
@@ -419,8 +419,8 @@
         [("col", n_col, "gather"), ("row", n_row, "gather")], [imu, camera[0]], 3)
     imu_rows = imu_rows.reshape(-1, D)
     cam_rows = cam_rows.reshape(-1, D)
-    log_a = jnp.log(imu_mass).reshape(8, -1)
-    log_b = jnp.log(cam_mass).reshape(8, -1)
+    log_a = imu_mass.reshape(8, -1)
+    log_b = cam_mass.reshape(8, -1)
 
     a = -cols_sq * INV
     for step in range(ITERS):

time: 201 us -> 201 us (level)
  no operation moved by 1% of the time
where the time goes in v13:
time: 201 us; the launch traced here: 200 us
  Pallas kernels  194 us (97%)
  local copies, waits for them, and re-layouts  4.86 us (2%)
    pallas_call x6, Pallas kernels, lse_combine(): pl.pallas_call(functools.partial(_lse_combine_kernel, axis, n), out_shape...  117 us
    pallas_call x1, Pallas kernels, plan_scatter(): pl.pallas_call(functools.partial(_plan_scatter_kernel, n_col, n_row), out...  53.3 us
    pallas_call x1, Pallas kernels, exchange(): pl.pallas_call(functools.partial(_exchange_kernel, tuple(jobs)), out_shap...  23.5 us

profile of v13, /device:TPU:116, one launch (start us, length us, event | category | flops | bytes accessed | tf_op | source)
XLA Modules:
  0.0 200.1 jit_solution(16082531443494496269)
XLA Ops:
  0.6 0.0 copy-start.2
  0.6 1.3 reshape.19.m_ref
  1.9 0.0 copy-done.2
  1.9 0.6 reshape.18.m_ref
  2.5 23.5 %shard_map.59 = (bf16[16,256,128]{2,1,0:T(8,128)(2,1)}, bf16[8,256,128]{2,1,0:T(8,128)(2,1)}, f32[8,512]{1,0:T(8,128)}, f32[8,256]{1,0:T(8,128)}) custom-call(bf16[256,128]{1,0:T(8,128)(2,1)} %refs_0_.1, bf16[256,128]{1,0:T(8,128)(2,1)} %bitcast.19), custom_call_target="tpu_custom_call" | custom-call | tf_op jit(solution)/shard_map/pallas_call | solution.py:388
  26.1 0.0 copy-start
  26.1 0.7 copy-done
  26.8 0.6 negate_multiply_fusion.a_ref
  27.4 20.4 %shard_map.60.a_ref = f32[8,512]{1,0:T(8,128)} custom-call(bf16[4096,128]{1,0:T(8,128)(2,1)} %bitcast.4, bf16[2048,128]{1,0:T(8,128)(2,1)} %bitcast.11, f32[8,256]{1,0:T(8,128)} %negate_multiply_fusion.a_ref, f32[8,512]{1,0:T(8,128)} %reshape.18.m_ref, f32[8,512]{1,0:T(8,128)} %get-tuple-element.11.s_ref), custom_call_target="tpu_custom_call" | custom-call | tf_op jit(solution)/shard_map/pallas_call | solution.py:272
  47.8 18.5 %shard_map.61.a_ref = f32[8,256]{1,0:T(8,128)} custom-call(bf16[2048,128]{1,0:T(8,128)(2,1)} %bitcast.12, bf16[4096,128]{1,0:T(8,128)(2,1)} %bitcast.5, f32[8,512]{1,0:T(8,128)} %shard_map.60.a_ref, f32[8,256]{1,0:T(8,128)} %reshape.19.m_ref, f32[8,256]{1,0:T(8,128)} %get-tuple-element.10.s_ref), custom_call_target="tpu_custom_call" | custom-call | tf_op jit(solution)/shard_map/pallas_call | solution.py:272
  66.3 20.7 %shard_map.62.a_ref = f32[8,512]{1,0:T(8,128)} custom-call(bf16[4096,128]{1,0:T(8,128)(2,1)} %bitcast.6, bf16[2048,128]{1,0:T(8,128)(2,1)} %bitcast.13, f32[8,256]{1,0:T(8,128)} %shard_map.61.a_ref, f32[8,512]{1,0:T(8,128)} %reshape.18.m_ref, f32[8,512]{1,0:T(8,128)} %get-tuple-element.11.s_ref), custom_call_target="tpu_custom_call" | custom-call | tf_op jit(solution)/shard_map/pallas_call | solution.py:272
  87.0 18.2 %shard_map.63.a_ref = f32[8,256]{1,0:T(8,128)} custom-call(bf16[2048,128]{1,0:T(8,128)(2,1)} %bitcast.14, bf16[4096,128]{1,0:T(8,128)(2,1)} %bitcast.7, f32[8,512]{1,0:T(8,128)} %shard_map.62.a_ref, f32[8,256]{1,0:T(8,128)} %reshape.19.m_ref, f32[8,256]{1,0:T(8,128)} %get-tuple-element.10.s_ref), custom_call_target="tpu_custom_call" | custom-call | tf_op jit(solution)/shard_map/pallas_call | solution.py:272
  105.3 20.6 %shard_map.64.a_ref.u_ref = f32[8,512]{1,0:T(8,128)} custom-call(bf16[4096,128]{1,0:T(8,128)(2,1)} %bitcast.8, bf16[2048,128]{1,0:T(8,128)(2,1)} %bitcast.15, f32[8,256]{1,0:T(8,128)} %shard_map.63.a_ref, f32[8,512]{1,0:T(8,128)} %reshape.18.m_ref, f32[8,512]{1,0:T(8,128)} %get-tuple-element.11.s_ref), custom_call_target="tpu_custom_call" | custom-call | tf_op jit(solution)/shard_map/pallas_call | solution.py:272
  125.9 18.7 %shard_map.65.a_ref = f32[8,256]{1,0:T(8,128)} custom-call(bf16[2048,128]{1,0:T(8,128)(2,1)} %bitcast.16, bf16[4096,128]{1,0:T(8,128)(2,1)} %bitcast.9, f32[8,512]{1,0:T(8,128)} %shard_map.64.a_ref.u_ref, f32[8,256]{1,0:T(8,128)} %reshape.19.m_ref, f32[8,256]{1,0:T(8,128)} %get-tuple-element.10.s_ref), custom_call_target="tpu_custom_call" | custom-call | tf_op jit(solution)/shard_map/pallas_call | solution.py:272
  144.6 53.3 %shard_map.66 = (f32[256,128]{1,0:T(8,128)}, f32[256,128]{1,0:T(8,128)}) custom-call(bf16[4096,128]{1,0:T(8,128)(2,1)} %bitcast.10, bf16[2048,128]{1,0:T(8,128)(2,1)} %bitcast.17, f32[8,512]{1,0:T(8,128)} %shard_map.64.a_ref.u_ref, f32[8,256]{1,0:T(8,128)} %shard_map.65.a_ref), custom_call_target="tpu_custom_call" | custom-call | tf_op jit(solution)/shard_map/pallas_call | solution.py:180
  197.8 0.0 copy-start.1
  197.8 1.6 copy.8
  199.4 0.0 copy-done.1
  199.4 0.7 copy.9
Async XLA Ops:
  0.6 1.3 copy-start.2
  26.1 0.7 copy-start
  197.8 1.6 copy-start.1

commit v14 on v13

--- a/solution.py
+++ b/solution.py
@@ -227,17 +227,25 @@
 
     half = part.shape[1]
     tile = p_ref.shape[0] // (2 * half)
-    q = q_ref[...]
-    a2 = _row_of(a_ref[...]) * LOG2E
+    cq = q_ref.shape[0]
+    wide = jnp.transpose(jnp.broadcast_to(_row_of(a_ref[...]) * (EPS / 2.0), (D, cq)))
+    hi = wide.astype(jnp.bfloat16)
+    rest = wide - hi.astype(jnp.float32)
+    mid = rest.astype(jnp.bfloat16)
+    low = (rest - mid.astype(jnp.float32)).astype(jnp.bfloat16)
+    lane = lax.broadcasted_iota(jnp.int32, (cq, D), 1)
+    zero = jnp.zeros_like(hi)
+    extra = jnp.where(lane == 0, hi, jnp.where(lane == 1, mid, jnp.where(lane == 2, low, zero)))
+    q = jnp.concatenate([q_ref[...], extra], axis=1)
+    ones = jnp.where(lax.broadcasted_iota(jnp.int32, (tile, D), 1) < 3, 1.0, 0.0).astype(jnp.bfloat16)
 
     def body(i, carry):
         start = pl.multiple_of(i * tile, tile)
-        cross = lax.dot_general(p_ref[pl.ds(start, tile), :], q, NT,
-                                preferred_element_type=jnp.float32)
-        t = a2 + SCALE2 * cross
-        top = jnp.max(t, axis=1, keepdims=True)
-        total = jnp.sum(jnp.exp2(t - top), axis=1, keepdims=True)
-        row = _to_row(top * LN2 + jnp.log(total)) - s_ref[pl.ds(i, 1), :] * INV
+        p = jnp.concatenate([p_ref[pl.ds(start, tile), :], ones], axis=1)
+        shifted = lax.dot_general(p, q, NT, preferred_element_type=jnp.float32)
+        top = jnp.max(shifted, axis=1, keepdims=True)
+        total = jnp.sum(jnp.exp2((shifted - top) * SCALE2), axis=1, keepdims=True)
+        row = _to_row(top * TWO_INV + jnp.log(total)) - s_ref[pl.ds(i, 1), :] * INV
         part.at[i // half][pl.ds(i % half, 1), :] = row
 
         @pl.when(i == half)

time: 201 us -> 200 us (level)
  no operation moved by 1% of the time
where the time goes in v14:
time: 200 us; the launch traced here: 199 us
  Pallas kernels  193 us (96%)
  local copies, waits for them, and re-layouts  4.86 us (2%)
    pallas_call x6, Pallas kernels, lse_combine(): pl.pallas_call(functools.partial(_lse_combine_kernel, axis, n), out_shape...  116 us
    pallas_call x1, Pallas kernels, plan_scatter(): pl.pallas_call(functools.partial(_plan_scatter_kernel, n_col, n_row), out...  53.1 us
    pallas_call x1, Pallas kernels, exchange(): pl.pallas_call(functools.partial(_exchange_kernel, tuple(jobs)), out_shap...  23.5 us

profile of v14, /device:TPU:116, one launch (start us, length us, event | category | flops | bytes accessed | tf_op | source)
XLA Modules:
  0.0 199.1 jit_solution(1848469454563417417)
XLA Ops:
  0.6 0.0 copy-start.2
  0.6 1.3 reshape.19.m_ref
  1.9 0.0 copy-done.2
  1.9 0.6 reshape.18.m_ref
  2.5 23.5 %shard_map.59 = (bf16[16,256,128]{2,1,0:T(8,128)(2,1)}, bf16[8,256,128]{2,1,0:T(8,128)(2,1)}, f32[8,512]{1,0:T(8,128)}, f32[8,256]{1,0:T(8,128)}) custom-call(bf16[256,128]{1,0:T(8,128)(2,1)} %refs_0_.1, bf16[256,128]{1,0:T(8,128)(2,1)} %bitcast.19), custom_call_target="tpu_custom_call" | custom-call | tf_op jit(solution)/shard_map/pallas_call | solution.py:396
  26.1 0.0 copy-start
  26.1 0.7 copy-done
  26.8 0.6 negate_multiply_fusion.a_ref
  27.4 20.6 %shard_map.60.a_ref = f32[8,512]{1,0:T(8,128)} custom-call(bf16[4096,128]{1,0:T(8,128)(2,1)} %bitcast.4, bf16[2048,128]{1,0:T(8,128)(2,1)} %bitcast.11, f32[8,256]{1,0:T(8,128)} %negate_multiply_fusion.a_ref, f32[8,512]{1,0:T(8,128)} %reshape.18.m_ref, f32[8,512]{1,0:T(8,128)} %get-tuple-element.11.s_ref), custom_call_target="tpu_custom_call" | custom-call | tf_op jit(solution)/shard_map/pallas_call | solution.py:280
  48.0 18.2 %shard_map.61.a_ref = f32[8,256]{1,0:T(8,128)} custom-call(bf16[2048,128]{1,0:T(8,128)(2,1)} %bitcast.12, bf16[4096,128]{1,0:T(8,128)(2,1)} %bitcast.5, f32[8,512]{1,0:T(8,128)} %shard_map.60.a_ref, f32[8,256]{1,0:T(8,128)} %reshape.19.m_ref, f32[8,256]{1,0:T(8,128)} %get-tuple-element.10.s_ref), custom_call_target="tpu_custom_call" | custom-call | tf_op jit(solution)/shard_map/pallas_call | solution.py:280
  66.2 20.7 %shard_map.62.a_ref = f32[8,512]{1,0:T(8,128)} custom-call(bf16[4096,128]{1,0:T(8,128)(2,1)} %bitcast.6, bf16[2048,128]{1,0:T(8,128)(2,1)} %bitcast.13, f32[8,256]{1,0:T(8,128)} %shard_map.61.a_ref, f32[8,512]{1,0:T(8,128)} %reshape.18.m_ref, f32[8,512]{1,0:T(8,128)} %get-tuple-element.11.s_ref), custom_call_target="tpu_custom_call" | custom-call | tf_op jit(solution)/shard_map/pallas_call | solution.py:280
  86.9 17.9 %shard_map.63.a_ref = f32[8,256]{1,0:T(8,128)} custom-call(bf16[2048,128]{1,0:T(8,128)(2,1)} %bitcast.14, bf16[4096,128]{1,0:T(8,128)(2,1)} %bitcast.7, f32[8,512]{1,0:T(8,128)} %shard_map.62.a_ref, f32[8,256]{1,0:T(8,128)} %reshape.19.m_ref, f32[8,256]{1,0:T(8,128)} %get-tuple-element.10.s_ref), custom_call_target="tpu_custom_call" | custom-call | tf_op jit(solution)/shard_map/pallas_call | solution.py:280
  104.9 20.6 %shard_map.64.a_ref.u_ref = f32[8,512]{1,0:T(8,128)} custom-call(bf16[4096,128]{1,0:T(8,128)(2,1)} %bitcast.8, bf16[2048,128]{1,0:T(8,128)(2,1)} %bitcast.15, f32[8,256]{1,0:T(8,128)} %shard_map.63.a_ref, f32[8,512]{1,0:T(8,128)} %reshape.18.m_ref, f32[8,512]{1,0:T(8,128)} %get-tuple-element.11.s_ref), custom_call_target="tpu_custom_call" | custom-call | tf_op jit(solution)/shard_map/pallas_call | solution.py:280
  125.5 18.3 %shard_map.65.a_ref = f32[8,256]{1,0:T(8,128)} custom-call(bf16[2048,128]{1,0:T(8,128)(2,1)} %bitcast.16, bf16[4096,128]{1,0:T(8,128)(2,1)} %bitcast.9, f32[8,512]{1,0:T(8,128)} %shard_map.64.a_ref.u_ref, f32[8,256]{1,0:T(8,128)} %reshape.19.m_ref, f32[8,256]{1,0:T(8,128)} %get-tuple-element.10.s_ref), custom_call_target="tpu_custom_call" | custom-call | tf_op jit(solution)/shard_map/pallas_call | solution.py:280
  143.8 53.1 %shard_map.66 = (f32[256,128]{1,0:T(8,128)}, f32[256,128]{1,0:T(8,128)}) custom-call(bf16[4096,128]{1,0:T(8,128)(2,1)} %bitcast.10, bf16[2048,128]{1,0:T(8,128)(2,1)} %bitcast.17, f32[8,512]{1,0:T(8,128)} %shard_map.64.a_ref.u_ref, f32[8,256]{1,0:T(8,128)} %shard_map.65.a_ref), custom_call_target="tpu_custom_call" | custom-call | tf_op jit(solution)/shard_map/pallas_call | solution.py:180
  196.9 0.0 copy-start.1
  196.9 1.6 copy.8
  198.5 0.0 copy-done.1
  198.5 0.7 copy.9
Async XLA Ops:
  0.6 1.3 copy-start.2
  26.1 0.7 copy-start
  196.9 1.6 copy-start.1

commit v15 on v14

--- a/solution.py
+++ b/solution.py
@@ -200,7 +200,7 @@
     )(x, y, u, a)
 
 
-def _lse_combine_kernel(axis, n, p_ref, q_ref, a_ref, m_ref, s_ref, o_ref,
+def _lse_combine_kernel(axis, n, scale, p_ref, q_ref, a_ref, m_ref, s_ref, o_ref,
                         part, buf, send, recv):
     me = lax.axis_index(axis)
     barrier = pltpu.get_barrier_semaphore()
@@ -228,7 +228,7 @@
     half = part.shape[1]
     tile = p_ref.shape[0] // (2 * half)
     cq = q_ref.shape[0]
-    wide = jnp.transpose(jnp.broadcast_to(_row_of(a_ref[...]) * (EPS / 2.0), (D, cq)))
+    wide = jnp.transpose(jnp.broadcast_to(_row_of(a_ref[...]) * scale, (D, cq)))
     hi = wide.astype(jnp.bfloat16)
     rest = wide - hi.astype(jnp.float32)
     mid = rest.astype(jnp.bfloat16)
@@ -267,18 +267,19 @@
         top = jnp.max(parts, axis=0)
         total = top + jnp.log(jnp.sum(jnp.exp(parts - top[None]), axis=0))
         rows = slice(c * half, (c + 1) * half)
-        o_ref[rows, :] = (EPS * (jnp.log(m_ref[rows, :]) - total) - s_ref[rows, :]) * INV
+        mass = m_ref[...].reshape(2 * half, -1)[rows, :]
+        o_ref[rows, :] = (EPS * (jnp.log(mass) - total) - s_ref[rows, :]) * INV
 
     finish(0)
     send_half(1)
     finish(1)
 
 
-def lse_combine(p, q, a, mass, sq, axis):
+def lse_combine(p, q, a, mass, sq, axis, scale=EPS / 2.0):
     n = lax.axis_size(axis)
     m = p.shape[0] // 8
     return pl.pallas_call(
-        functools.partial(_lse_combine_kernel, axis, n),
+        functools.partial(_lse_combine_kernel, axis, n, scale),
         out_shape=jax.ShapeDtypeStruct((8, m), jnp.float32),
         in_specs=[pl.BlockSpec(memory_space=pltpu.VMEM)] * 5,
         out_specs=pl.BlockSpec(memory_space=pltpu.VMEM),
@@ -289,7 +290,8 @@
             pltpu.SemaphoreType.DMA((2, n)),
         ],
         compiler_params=pltpu.CompilerParams(
-            collective_id=5 if axis == "col" else 6, has_side_effects=True,
+            collective_id=(5 if axis == "col" else 6) + (0 if scale == EPS / 2.0 else 3),
+            has_side_effects=True,
             vmem_limit_bytes=VMEM_LIMIT),
     )(p, q, a, mass, sq)
 
@@ -427,13 +429,11 @@
         [("col", n_col, "gather"), ("row", n_row, "gather")], [imu, camera[0]], 3)
     imu_rows = imu_rows.reshape(-1, D)
     cam_rows = cam_rows.reshape(-1, D)
-    log_a = imu_mass.reshape(8, -1)
-    log_b = cam_mass.reshape(8, -1)
-
-    a = -cols_sq * INV
+    a, scale = cols_sq, -INV * EPS / 2.0
     for step in range(ITERS):
-        u = lse_combine(imu_rows, cam_rows, a, log_a, rows_sq, "col")
-        a = lse_combine(cam_rows, imu_rows, u, log_b, cols_sq, "row")
+        u = lse_combine(imu_rows, cam_rows, a, imu_mass, rows_sq, "col", scale)
+        a = lse_combine(cam_rows, imu_rows, u, cam_mass, cols_sq, "row")
+        scale = EPS / 2.0
 
     grad_imu, grad_cam = plan_scatter(imu_rows, cam_rows, u, a, n_col, n_row)
     return (grad_imu, grad_cam[None])

time: 200 us -> 196 us (0.980)
  local copies, waits for them, and re-layouts: 4.86 us -> 2.26 us
where the time goes in v15:
time: 196 us
  Pallas kernels  193 us (98%)
  local copies, waits for them, and re-layouts  2.26 us (1%)
    pallas_call x6, Pallas kernels, lse_combine(): pl.pallas_call(functools.partial(_lse_combine_kernel, axis, n, scale), ou...  116 us
    pallas_call x1, Pallas kernels, plan_scatter(): pl.pallas_call(functools.partial(_plan_scatter_kernel, n_col, n_row), out...  52.9 us
    pallas_call x1, Pallas kernels, exchange(): pl.pallas_call(functools.partial(_exchange_kernel, tuple(jobs)), out_shap...  23.6 us

profile of v15, /device:TPU:116, one launch (start us, length us, event | category | flops | bytes accessed | tf_op | source)
XLA Modules:
  0.0 195.9 jit_solution(3678253512935890391)
XLA Ops:
  0.6 23.6 %shard_map.59 = (bf16[16,256,128]{2,1,0:T(8,128)(2,1)}, bf16[8,256,128]{2,1,0:T(8,128)(2,1)}, f32[8,512]{1,0:T(8,128)}, f32[8,256]{1,0:T(8,128)}) custom-call(bf16[256,128]{1,0:T(8,128)(2,1)} %refs_0_.1, bf16[256,128]{1,0:T(8,128)(2,1)} %bitcast.19), custom_call_target="tpu_custom_call" | custom-call | tf_op jit(solution)/shard_map/pallas_call | solution.py:398
  24.2 20.7 %shard_map.60.a_ref = f32[8,512]{1,0:T(8,128)} custom-call(bf16[4096,128]{1,0:T(8,128)(2,1)} %bitcast.4, bf16[2048,128]{1,0:T(8,128)(2,1)} %bitcast.11, f32[8,256]{1,0:T(8,128)} %get-tuple-element.10.a_ref.s_ref, f32[4096]{0:T(1024)} %m_ref.10, f32[8,512]{1,0:T(8,128)} %get-tuple-element.11.s_ref), custom_call_target="tpu_custom_call" | custom-call | tf_op jit(solution)/shard_map/pallas_call | solution.py:281
  44.9 18.2 %shard_map.61.a_ref = f32[8,256]{1,0:T(8,128)} custom-call(bf16[2048,128]{1,0:T(8,128)(2,1)} %bitcast.12, bf16[4096,128]{1,0:T(8,128)(2,1)} %bitcast.5, f32[8,512]{1,0:T(8,128)} %shard_map.60.a_ref, f32[2048]{0:T(1024)} %m_ref.11, f32[8,256]{1,0:T(8,128)} %get-tuple-element.10.a_ref.s_ref), custom_call_target="tpu_custom_call" | custom-call | tf_op jit(solution)/shard_map/pallas_call | solution.py:281
  63.1 20.7 %shard_map.62.a_ref = f32[8,512]{1,0:T(8,128)} custom-call(bf16[4096,128]{1,0:T(8,128)(2,1)} %bitcast.6, bf16[2048,128]{1,0:T(8,128)(2,1)} %bitcast.13, f32[8,256]{1,0:T(8,128)} %shard_map.61.a_ref, f32[4096]{0:T(1024)} %m_ref.10, f32[8,512]{1,0:T(8,128)} %get-tuple-element.11.s_ref), custom_call_target="tpu_custom_call" | custom-call | tf_op jit(solution)/shard_map/pallas_call | solution.py:281
  83.9 17.9 %shard_map.63.a_ref = f32[8,256]{1,0:T(8,128)} custom-call(bf16[2048,128]{1,0:T(8,128)(2,1)} %bitcast.14, bf16[4096,128]{1,0:T(8,128)(2,1)} %bitcast.7, f32[8,512]{1,0:T(8,128)} %shard_map.62.a_ref, f32[2048]{0:T(1024)} %m_ref.11, f32[8,256]{1,0:T(8,128)} %get-tuple-element.10.a_ref.s_ref), custom_call_target="tpu_custom_call" | custom-call | tf_op jit(solution)/shard_map/pallas_call | solution.py:281
  101.8 20.6 %shard_map.64.a_ref.u_ref = f32[8,512]{1,0:T(8,128)} custom-call(bf16[4096,128]{1,0:T(8,128)(2,1)} %bitcast.8, bf16[2048,128]{1,0:T(8,128)(2,1)} %bitcast.15, f32[8,256]{1,0:T(8,128)} %shard_map.63.a_ref, f32[4096]{0:T(1024)} %m_ref.10, f32[8,512]{1,0:T(8,128)} %get-tuple-element.11.s_ref), custom_call_target="tpu_custom_call" | custom-call | tf_op jit(solution)/shard_map/pallas_call | solution.py:281
  122.5 18.3 %shard_map.65.a_ref = f32[8,256]{1,0:T(8,128)} custom-call(bf16[2048,128]{1,0:T(8,128)(2,1)} %bitcast.16, bf16[4096,128]{1,0:T(8,128)(2,1)} %bitcast.9, f32[8,512]{1,0:T(8,128)} %shard_map.64.a_ref.u_ref, f32[2048]{0:T(1024)} %m_ref.11, f32[8,256]{1,0:T(8,128)} %get-tuple-element.10.a_ref.s_ref), custom_call_target="tpu_custom_call" | custom-call | tf_op jit(solution)/shard_map/pallas_call | solution.py:281
  140.8 52.9 %shard_map.66 = (f32[256,128]{1,0:T(8,128)}, f32[256,128]{1,0:T(8,128)}) custom-call(bf16[4096,128]{1,0:T(8,128)(2,1)} %bitcast.10, bf16[2048,128]{1,0:T(8,128)(2,1)} %bitcast.17, f32[8,512]{1,0:T(8,128)} %shard_map.64.a_ref.u_ref, f32[8,256]{1,0:T(8,128)} %shard_map.65.a_ref), custom_call_target="tpu_custom_call" | custom-call | tf_op jit(solution)/shard_map/pallas_call | solution.py:180
  193.7 0.0 copy-start
  193.7 1.6 copy.8
  195.3 0.0 copy-done
  195.3 0.7 copy.9
Async XLA Ops:
  193.7 1.6 copy-start

commit v16 on v15

--- a/solution.py
+++ b/solution.py
@@ -128,6 +128,11 @@
             src_ref=gcs.at[k], dst_ref=bufc.at[slot], send_sem=sendc.at[k], recv_sem=recvc.at[slot],
             device_id=_peer("row", k), device_id_type=pl.DeviceIdType.MESH)
 
+    def send_tile(t):
+        for s in range(per):
+            k = t * per + s
+            pl.when(me_c != k)(functools.partial(lambda k: to_col_dev(k, me_c).start(), k))
+
     def each(n, me, body):
         for k in range(n):
             pl.when(me != k)(functools.partial(body, k))
@@ -140,10 +145,12 @@
     a2 = _row_of(a_ref[...]) * LOG2E
     pc[...] = jnp.zeros_like(pc)
     csum[...] = jnp.zeros_like(csum)
+    order = [lax.rem(me_c // per + 1 + i, tiles) for i in range(tiles)]
     for i in range(tiles):
-        x = x_ref[i * tile:(i + 1) * tile, :]
+        t = order[i]
+        x = x_ref[pl.ds(pl.multiple_of(t * tile, tile), tile), :]
         cross = lax.dot_general(x, y, NT, preferred_element_type=jnp.float32)
-        u = _to_col(u_ref[i:i + 1, :] * LOG2E)
+        u = _to_col(u_ref[pl.ds(t, 1), :] * LOG2E)
         plan = jnp.exp2(u + a2 + SCALE2 * cross).astype(jnp.bfloat16)
         wide = plan.astype(jnp.float32)
         r = jnp.sum(wide, axis=1, keepdims=True)
@@ -151,15 +158,13 @@
         pulled = jnp.dot(plan, y, preferred_element_type=jnp.float32)
         g = 2.0 * (r * x.astype(jnp.float32) - pulled)
         for s in range(per):
-            gi[i * per + s] = g[s * m:(s + 1) * m]
+            gi[t * per + s] = g[s * m:(s + 1) * m]
         pc[...] += lax.dot_general(plan, x, TN, preferred_element_type=jnp.float32)
         if i == 1:
             pl.semaphore_wait(barrier, n_col + n_row - 2)
         if i >= 1:
-            for s in range((i - 1) * per, i * per):
-                pl.when(me_c != s)(functools.partial(lambda k: to_col_dev(k, me_c).start(), s))
-    for s in range((tiles - 1) * per, tiles * per):
-        pl.when(me_c != s)(functools.partial(lambda k: to_col_dev(k, me_c).start(), s))
+            send_tile(order[i - 1])
+    send_tile(order[tiles - 1])
     gcv = 2.0 * (_to_col(csum[...]) * y.astype(jnp.float32) - pc[...])
     for k in range(n_row):
         gcs[k] = gcv[k * mc:(k + 1) * mc]

time: 196 us -> 190 us (0.969); the launches traced: 196 us -> 188 us
  Pallas kernels: 193 us -> 185 us
    pallas_call x1, Pallas kernels: 52.9 us -> 44.5 us  [plan_scatter(): pl.pallas_call(functools.partial(_plan_scatter_kernel, n_col, n_row), out...]
where the time goes in v16:
time: 190 us; the launch traced here: 188 us
  Pallas kernels  185 us (97%)
  local copies, waits for them, and re-layouts  2.26 us (1%)
    pallas_call x6, Pallas kernels, lse_combine(): pl.pallas_call(functools.partial(_lse_combine_kernel, axis, n, scale), ou...  116 us
    pallas_call x1, Pallas kernels, plan_scatter(): pl.pallas_call(functools.partial(_plan_scatter_kernel, n_col, n_row), out...  44.5 us
    pallas_call x1, Pallas kernels, exchange(): pl.pallas_call(functools.partial(_exchange_kernel, tuple(jobs)), out_shap...  23.6 us

profile of v16, /device:TPU:116, one launch (start us, length us, event | category | flops | bytes accessed | tf_op | source)
XLA Modules:
  0.0 187.5 jit_solution(12624390218525448187)
XLA Ops:
  0.6 23.6 %shard_map.59 = (bf16[16,256,128]{2,1,0:T(8,128)(2,1)}, bf16[8,256,128]{2,1,0:T(8,128)(2,1)}, f32[8,512]{1,0:T(8,128)}, f32[8,256]{1,0:T(8,128)}) custom-call(bf16[256,128]{1,0:T(8,128)(2,1)} %refs_0_.1, bf16[256,128]{1,0:T(8,128)(2,1)} %bitcast.19), custom_call_target="tpu_custom_call" | custom-call | tf_op jit(solution)/shard_map/pallas_call | solution.py:403
  24.2 20.7 %shard_map.60.a_ref = f32[8,512]{1,0:T(8,128)} custom-call(bf16[4096,128]{1,0:T(8,128)(2,1)} %bitcast.4, bf16[2048,128]{1,0:T(8,128)(2,1)} %bitcast.11, f32[8,256]{1,0:T(8,128)} %get-tuple-element.10.a_ref.s_ref, f32[4096]{0:T(1024)} %m_ref.10, f32[8,512]{1,0:T(8,128)} %get-tuple-element.11.s_ref), custom_call_target="tpu_custom_call" | custom-call | tf_op jit(solution)/shard_map/pallas_call | solution.py:286
  44.9 18.2 %shard_map.61.a_ref = f32[8,256]{1,0:T(8,128)} custom-call(bf16[2048,128]{1,0:T(8,128)(2,1)} %bitcast.12, bf16[4096,128]{1,0:T(8,128)(2,1)} %bitcast.5, f32[8,512]{1,0:T(8,128)} %shard_map.60.a_ref, f32[2048]{0:T(1024)} %m_ref.11, f32[8,256]{1,0:T(8,128)} %get-tuple-element.10.a_ref.s_ref), custom_call_target="tpu_custom_call" | custom-call | tf_op jit(solution)/shard_map/pallas_call | solution.py:286
  63.1 20.7 %shard_map.62.a_ref = f32[8,512]{1,0:T(8,128)} custom-call(bf16[4096,128]{1,0:T(8,128)(2,1)} %bitcast.6, bf16[2048,128]{1,0:T(8,128)(2,1)} %bitcast.13, f32[8,256]{1,0:T(8,128)} %shard_map.61.a_ref, f32[4096]{0:T(1024)} %m_ref.10, f32[8,512]{1,0:T(8,128)} %get-tuple-element.11.s_ref), custom_call_target="tpu_custom_call" | custom-call | tf_op jit(solution)/shard_map/pallas_call | solution.py:286
  83.9 17.9 %shard_map.63.a_ref = f32[8,256]{1,0:T(8,128)} custom-call(bf16[2048,128]{1,0:T(8,128)(2,1)} %bitcast.14, bf16[4096,128]{1,0:T(8,128)(2,1)} %bitcast.7, f32[8,512]{1,0:T(8,128)} %shard_map.62.a_ref, f32[2048]{0:T(1024)} %m_ref.11, f32[8,256]{1,0:T(8,128)} %get-tuple-element.10.a_ref.s_ref), custom_call_target="tpu_custom_call" | custom-call | tf_op jit(solution)/shard_map/pallas_call | solution.py:286
  101.8 20.6 %shard_map.64.a_ref.u_ref = f32[8,512]{1,0:T(8,128)} custom-call(bf16[4096,128]{1,0:T(8,128)(2,1)} %bitcast.8, bf16[2048,128]{1,0:T(8,128)(2,1)} %bitcast.15, f32[8,256]{1,0:T(8,128)} %shard_map.63.a_ref, f32[4096]{0:T(1024)} %m_ref.10, f32[8,512]{1,0:T(8,128)} %get-tuple-element.11.s_ref), custom_call_target="tpu_custom_call" | custom-call | tf_op jit(solution)/shard_map/pallas_call | solution.py:286
  122.5 18.3 %shard_map.65.a_ref = f32[8,256]{1,0:T(8,128)} custom-call(bf16[2048,128]{1,0:T(8,128)(2,1)} %bitcast.16, bf16[4096,128]{1,0:T(8,128)(2,1)} %bitcast.9, f32[8,512]{1,0:T(8,128)} %shard_map.64.a_ref.u_ref, f32[2048]{0:T(1024)} %m_ref.11, f32[8,256]{1,0:T(8,128)} %get-tuple-element.10.a_ref.s_ref), custom_call_target="tpu_custom_call" | custom-call | tf_op jit(solution)/shard_map/pallas_call | solution.py:286
  140.8 44.5 %shard_map.66 = (f32[256,128]{1,0:T(8,128)}, f32[256,128]{1,0:T(8,128)}) custom-call(bf16[4096,128]{1,0:T(8,128)(2,1)} %bitcast.10, bf16[2048,128]{1,0:T(8,128)(2,1)} %bitcast.17, f32[8,512]{1,0:T(8,128)} %shard_map.64.a_ref.u_ref, f32[8,256]{1,0:T(8,128)} %shard_map.65.a_ref), custom_call_target="tpu_custom_call" | custom-call | tf_op jit(solution)/shard_map/pallas_call | solution.py:185
  185.3 0.0 copy-start
  185.3 1.6 copy.8
  186.9 0.0 copy-done
  186.9 0.7 copy.9
Async XLA Ops:
  185.3 1.6 copy-start

commit v17 on v16

--- a/solution.py
+++ b/solution.py
@@ -168,7 +168,8 @@
     gcv = 2.0 * (_to_col(csum[...]) * y.astype(jnp.float32) - pc[...])
     for k in range(n_row):
         gcs[k] = gcv[k * mc:(k + 1) * mc]
-    each(n_row, me_r, lambda k: to_row_dev(k, me_r).start())
+    for d in range(1, n_row):
+        to_row_dev(lax.rem(me_r + d, n_row), me_r).start()
     each(n_col, me_c, lambda k: to_col_dev(k, me_c).wait_send())
     each(n_row, me_r, lambda k: to_row_dev(k, me_r).wait_send())
     each(n_col, me_c, lambda k: to_col_dev(k, k).wait_recv())

time: 190 us -> 190 us (level)
  no operation moved by 1% of the time
where the time goes in v17:
time: 190 us; the launch traced here: 188 us
  Pallas kernels  185 us (97%)
  local copies, waits for them, and re-layouts  2.26 us (1%)
    pallas_call x6, Pallas kernels, lse_combine(): pl.pallas_call(functools.partial(_lse_combine_kernel, axis, n, scale), ou...  116 us
    pallas_call x1, Pallas kernels, plan_scatter(): pl.pallas_call(functools.partial(_plan_scatter_kernel, n_col, n_row), out...  44.5 us
    pallas_call x1, Pallas kernels, exchange(): pl.pallas_call(functools.partial(_exchange_kernel, tuple(jobs)), out_shap...  23.6 us

profile of v17, /device:TPU:116, one launch (start us, length us, event | category | flops | bytes accessed | tf_op | source)
XLA Modules:
  0.0 187.6 jit_solution(16099584543803041428)
XLA Ops:
  0.6 23.6 %shard_map.59 = (bf16[16,256,128]{2,1,0:T(8,128)(2,1)}, bf16[8,256,128]{2,1,0:T(8,128)(2,1)}, f32[8,512]{1,0:T(8,128)}, f32[8,256]{1,0:T(8,128)}) custom-call(bf16[256,128]{1,0:T(8,128)(2,1)} %refs_0_.1, bf16[256,128]{1,0:T(8,128)(2,1)} %bitcast.19), custom_call_target="tpu_custom_call" | custom-call | tf_op jit(solution)/shard_map/pallas_call | solution.py:404
  24.2 20.7 %shard_map.60.a_ref = f32[8,512]{1,0:T(8,128)} custom-call(bf16[4096,128]{1,0:T(8,128)(2,1)} %bitcast.4, bf16[2048,128]{1,0:T(8,128)(2,1)} %bitcast.11, f32[8,256]{1,0:T(8,128)} %get-tuple-element.10.a_ref.s_ref, f32[4096]{0:T(1024)} %m_ref.10, f32[8,512]{1,0:T(8,128)} %get-tuple-element.11.s_ref), custom_call_target="tpu_custom_call" | custom-call | tf_op jit(solution)/shard_map/pallas_call | solution.py:287
  44.9 18.2 %shard_map.61.a_ref = f32[8,256]{1,0:T(8,128)} custom-call(bf16[2048,128]{1,0:T(8,128)(2,1)} %bitcast.12, bf16[4096,128]{1,0:T(8,128)(2,1)} %bitcast.5, f32[8,512]{1,0:T(8,128)} %shard_map.60.a_ref, f32[2048]{0:T(1024)} %m_ref.11, f32[8,256]{1,0:T(8,128)} %get-tuple-element.10.a_ref.s_ref), custom_call_target="tpu_custom_call" | custom-call | tf_op jit(solution)/shard_map/pallas_call | solution.py:287
  63.1 20.7 %shard_map.62.a_ref = f32[8,512]{1,0:T(8,128)} custom-call(bf16[4096,128]{1,0:T(8,128)(2,1)} %bitcast.6, bf16[2048,128]{1,0:T(8,128)(2,1)} %bitcast.13, f32[8,256]{1,0:T(8,128)} %shard_map.61.a_ref, f32[4096]{0:T(1024)} %m_ref.10, f32[8,512]{1,0:T(8,128)} %get-tuple-element.11.s_ref), custom_call_target="tpu_custom_call" | custom-call | tf_op jit(solution)/shard_map/pallas_call | solution.py:287
  83.9 17.9 %shard_map.63.a_ref = f32[8,256]{1,0:T(8,128)} custom-call(bf16[2048,128]{1,0:T(8,128)(2,1)} %bitcast.14, bf16[4096,128]{1,0:T(8,128)(2,1)} %bitcast.7, f32[8,512]{1,0:T(8,128)} %shard_map.62.a_ref, f32[2048]{0:T(1024)} %m_ref.11, f32[8,256]{1,0:T(8,128)} %get-tuple-element.10.a_ref.s_ref), custom_call_target="tpu_custom_call" | custom-call | tf_op jit(solution)/shard_map/pallas_call | solution.py:287
  101.8 20.6 %shard_map.64.a_ref.u_ref = f32[8,512]{1,0:T(8,128)} custom-call(bf16[4096,128]{1,0:T(8,128)(2,1)} %bitcast.8, bf16[2048,128]{1,0:T(8,128)(2,1)} %bitcast.15, f32[8,256]{1,0:T(8,128)} %shard_map.63.a_ref, f32[4096]{0:T(1024)} %m_ref.10, f32[8,512]{1,0:T(8,128)} %get-tuple-element.11.s_ref), custom_call_target="tpu_custom_call" | custom-call | tf_op jit(solution)/shard_map/pallas_call | solution.py:287
  122.5 18.3 %shard_map.65.a_ref = f32[8,256]{1,0:T(8,128)} custom-call(bf16[2048,128]{1,0:T(8,128)(2,1)} %bitcast.16, bf16[4096,128]{1,0:T(8,128)(2,1)} %bitcast.9, f32[8,512]{1,0:T(8,128)} %shard_map.64.a_ref.u_ref, f32[2048]{0:T(1024)} %m_ref.11, f32[8,256]{1,0:T(8,128)} %get-tuple-element.10.a_ref.s_ref), custom_call_target="tpu_custom_call" | custom-call | tf_op jit(solution)/shard_map/pallas_call | solution.py:287
  140.8 44.5 %shard_map.66 = (f32[256,128]{1,0:T(8,128)}, f32[256,128]{1,0:T(8,128)}) custom-call(bf16[4096,128]{1,0:T(8,128)(2,1)} %bitcast.10, bf16[2048,128]{1,0:T(8,128)(2,1)} %bitcast.17, f32[8,512]{1,0:T(8,128)} %shard_map.64.a_ref.u_ref, f32[8,256]{1,0:T(8,128)} %shard_map.65.a_ref), custom_call_target="tpu_custom_call" | custom-call | tf_op jit(solution)/shard_map/pallas_call | solution.py:186
  185.3 0.0 copy-start
  185.3 1.6 copy.8
  186.9 0.0 copy-done
  186.9 0.7 copy.9
Async XLA Ops:
  185.3 1.6 copy-start
